TPU v7x, 32 devices: a whole 2x2x4 slice. The times are simulated.
32 devices in a mesh: batch: 8 (over z, y), ffn: 4 (over x, core).
Axes of the slice: x: 2, y: 2, z: 4, core: 2. Of those that a mesh axis runs over, the one named last changes fastest.
Arguments:
- tokens: bfloat16 [50112, 768], P(('batch', 'ffn')), may hold values from -6 to 6
- text_lengths: int32 [192], P(('batch', 'ffn')), may hold values from 8 to 64
- routes: int32 [50112, 1], P(('batch', 'ffn')), may hold values from 0 to 7; in each aligned block of 1566 rows (0 to 1565, 1566 to 3131, ...) at most 261 rows name the same one
- group_map: int32 [8], replicated, may hold values from 0 to 2, as said below
- gain_one: float32 [768], replicated, may hold values from 0.1 to 1.9
- w_qkv: bfloat16 [768, 2304], replicated, may hold values from -0.3125 to 0.3125
- w_proj: bfloat16 [768, 768], replicated, may hold values from -0.875 to 0.875
- gain_two: float32 [768], replicated, may hold values from 0.1 to 1.9
- w_in: bfloat16 [8, 768, 3072], P('batch', None, 'ffn'), as said below
- w_back: bfloat16 [8, 3072, 768], P('batch', 'ffn'), as said below
- cotangent: bfloat16 [50112, 768], P(('batch', 'ffn')), may hold values from -6 to 6
Outputs:
- block_out: float32 [50112, 768], P(('batch', 'ffn'))
- input_grad: float32 [50112, 768], P(('batch', 'ffn'))
- grad_gain_one: float32 [768], replicated
- grad_w_qkv: float32 [768, 2304], replicated
- grad_w_proj: float32 [768, 768], replicated
- grad_gain_two: float32 [768], replicated
- grad_w_in: float32 [8, 768, 3072], P('batch', None, 'ffn')
- grad_w_back: float32 [8, 3072, 768], P('batch', 'ffn')
Inputs may be any that keep to these rules, and one draw needn't show every extreme that they name: `routes`: among the rows of one device each index of batch is named by at most 261 rows, and by exactly 261 rows in some devices' rows. `group_map`: every expert is hosted by at least one index of batch; the numbers of indices hosting each expert differ by at most one. w_in[i] equals w_in[j] whenever group_map[i] equals group_map[j]. w_back[i] equals w_back[j] whenever group_map[i] equals group_map[j].
All inputs are finite; a program needn't handle non-finite values.
Results may differ from a plain program's by a relative error of at most 0.015.
The roundings to bfloat16 on the way count: a program that leaves them out, or rounds other values in their place, can miss the bound.
Values may be sent and summed in bfloat16 or wider, within the bound.
A program may use at most 256 MiB of HBM per device.

v0:
```python
import math

import jax
import jax.numpy as jnp
from jax import lax
from jax.sharding import PartitionSpec as P

D = 768
HEADS = 12
HEAD_DIM = 64
EXPERTS = 3
PATCHES = 197
SEQ_DEV = 6
SEQ_LEN = 261
TOK_DEV = 1566


epsilon = 1e-05


def norm_forward(values, gain):
    average = jnp.mean(values, axis=-1, keepdims=True)
    centred = values - average
    variance = jnp.mean(centred * centred, axis=-1, keepdims=True)
    inverse = lax.rsqrt(variance + epsilon)
    normal = centred * inverse
    return (normal * gain, normal, inverse)


def norm_backward(grad_normed, gain, normal, inverse):
    scaled = grad_normed * gain
    mean_grad = jnp.mean(scaled, axis=-1, keepdims=True)
    mean_proj = jnp.mean(scaled * normal, axis=-1, keepdims=True)
    return (
        inverse * (scaled - mean_grad - normal * mean_proj),
        jnp.sum(grad_normed * normal, axis=0),
    )


def gelu_slope(inner_act):
    cumulative = 0.5 * (1.0 + lax.erf(inner_act * (1.0 / math.sqrt(2.0))))
    density = jnp.exp(-0.5 * inner_act * inner_act) * (1.0 / math.sqrt(2.0 * math.pi))
    return cumulative + inner_act * density


def masked_scores(seq_pair, visible):
    queries = seq_pair[:, :, 0]
    key_rows = seq_pair[:, :, 1]
    scores = jnp.einsum(
        "sqhd,skhd->shqk", queries, key_rows, preferred_element_type=jnp.float32
    ) * HEAD_DIM ** (-0.5)
    return jnp.where(visible[:, None, None, :], scores, -1e30)


def attend_forward(operands):
    seq_pair, visible = operands
    scores = masked_scores(seq_pair, visible)
    row_peak = jnp.max(scores, axis=-1, keepdims=True)
    exponent = jnp.exp(scores - row_peak)
    row_total = jnp.sum(exponent, axis=-1, keepdims=True)
    log_total = row_peak + jnp.log(row_total)
    attn_probs = jnp.exp(scores - log_total).astype(jnp.bfloat16)
    context = jnp.einsum(
        "shqk,skhd->sqhd", attn_probs, seq_pair[:, :, 2], preferred_element_type=jnp.float32
    )
    return (context.astype(jnp.bfloat16), log_total)


def attend_backward(operands):
    seq_pair, visible, log_total, grad_context = operands
    queries = seq_pair[:, :, 0]
    key_rows = seq_pair[:, :, 1]
    value_rows = seq_pair[:, :, 2]
    probs_full = jnp.exp(masked_scores(seq_pair, visible) - log_total)
    attn_probs = probs_full.astype(jnp.bfloat16)
    grad_probs = jnp.einsum(
        "sqhd,skhd->shqk", grad_context, value_rows, preferred_element_type=jnp.float32
    )
    grad_values = jnp.einsum(
        "shqk,sqhd->skhd", attn_probs, grad_context, preferred_element_type=jnp.float32
    )
    row_delta = jnp.sum(grad_probs * probs_full, axis=-1, keepdims=True)
    grad_scores = (probs_full * (grad_probs - row_delta)).astype(jnp.bfloat16)
    grad_queries = jnp.einsum(
        "shqk,skhd->sqhd", grad_scores, key_rows, preferred_element_type=jnp.float32
    ) * HEAD_DIM ** (-0.5)
    grad_keys = jnp.einsum(
        "shqk,sqhd->skhd", grad_scores, queries, preferred_element_type=jnp.float32
    ) * HEAD_DIM ** (-0.5)
    return jnp.stack([grad_queries, grad_keys, grad_values], axis=2).astype(jnp.bfloat16)


def body(
    tokens,
    text_lengths,
    routes,
    group_map,
    gain_one,
    w_qkv,
    w_proj,
    gain_two,
    w_in,
    w_back,
    cotangent,
):
    token_rows = tokens.astype(jnp.float32)
    normed_one, normal_one, inverse_one = norm_forward(token_rows, gain_one)
    normed_low = normed_one.astype(jnp.bfloat16)
    qkv_rows = jnp.dot(normed_low, w_qkv, preferred_element_type=jnp.float32).astype(jnp.bfloat16)
    seq_pairs = qkv_rows.reshape(SEQ_DEV // 2, 2, SEQ_LEN, 3, HEADS, HEAD_DIM)
    position = jnp.arange(SEQ_LEN, dtype=jnp.int32)
    visible = (position[None, :] < PATCHES + text_lengths[:, None]).reshape(
        SEQ_DEV // 2, 2, SEQ_LEN
    )
    context, log_total = lax.map(attend_forward, (seq_pairs, visible))
    context = context.reshape(TOK_DEV, D)
    middle = token_rows + jnp.dot(context, w_proj, preferred_element_type=jnp.float32)
    normed_two, normal_two, inverse_two = norm_forward(middle, gain_two)
    sending = normed_two.astype(jnp.bfloat16)
    n_batch = lax.axis_size("batch")
    capacity = (4 * TOK_DEV + 3 * n_batch - 1) // (3 * n_batch)
    slot_count = n_batch * capacity
    target = routes[:, 0]
    onehot = (target[:, None] == jnp.arange(n_batch, dtype=jnp.int32)[None, :]).astype(jnp.int32)
    slot_rank = jnp.sum((jnp.cumsum(onehot, axis=0) - 1) * onehot, axis=1)
    slot_index = target * capacity + slot_rank
    outgoing = jnp.zeros((slot_count, D), jnp.bfloat16).at[slot_index].set(sending)
    arrived = lax.all_to_all(
        outgoing.reshape(n_batch, capacity, D), "batch", split_axis=0, concat_axis=0, tiled=True
    ).reshape(slot_count, D)
    own_expert = group_map[lax.axis_index("batch")]
    w_in_own = w_in[0]
    w_back_own = w_back[0]
    gathered = lax.all_gather(arrived, "ffn", axis=0, tiled=True)
    inner_act = jnp.dot(gathered, w_in_own, preferred_element_type=jnp.float32)
    hidden = jax.nn.gelu(inner_act, approximate=False).astype(jnp.bfloat16)
    produced = lax.psum_scatter(
        jnp.dot(hidden, w_back_own, preferred_element_type=jnp.float32).astype(jnp.bfloat16),
        "ffn",
        scatter_dimension=0,
        tiled=True,
    )
    returning = produced.reshape(n_batch, capacity, D)
    returned = lax.all_to_all(returning, "batch", split_axis=0, concat_axis=0, tiled=True).reshape(
        slot_count, D
    )
    block_out = middle + returned[slot_index].astype(jnp.float32)
    grad_slots = jnp.zeros((slot_count, D), jnp.bfloat16).at[slot_index].set(cotangent)
    grad_arrived = lax.all_to_all(
        grad_slots.reshape(n_batch, capacity, D), "batch", split_axis=0, concat_axis=0, tiled=True
    ).reshape(slot_count, D)
    grad_gathered = lax.all_gather(grad_arrived, "ffn", axis=0, tiled=True)
    grad_hidden = jnp.dot(grad_gathered, w_back_own.T, preferred_element_type=jnp.float32).astype(
        jnp.bfloat16
    )
    grad_inner = (grad_hidden.astype(jnp.float32) * gelu_slope(inner_act)).astype(jnp.bfloat16)
    grad_back_own = jnp.dot(hidden.T, grad_gathered, preferred_element_type=jnp.float32)
    grad_in_own = jnp.dot(gathered.T, grad_inner, preferred_element_type=jnp.float32)
    grad_sent = lax.psum_scatter(
        jnp.dot(grad_inner, w_in_own.T, preferred_element_type=jnp.float32).astype(jnp.bfloat16),
        "ffn",
        scatter_dimension=0,
        tiled=True,
    )
    grad_going = grad_sent.reshape(n_batch, capacity, D)
    grad_home = lax.all_to_all(
        grad_going, "batch", split_axis=0, concat_axis=0, tiled=True
    ).reshape(slot_count, D)
    grad_normed_two = grad_home[slot_index].astype(jnp.float32)
    grad_middle_part, grad_gain_two = norm_backward(
        grad_normed_two, gain_two, normal_two, inverse_two
    )
    grad_middle = cotangent.astype(jnp.float32) + grad_middle_part
    grad_attended = grad_middle.astype(jnp.bfloat16)
    grad_w_proj = jnp.dot(context.T, grad_attended, preferred_element_type=jnp.float32)
    grad_context = jnp.dot(grad_attended, w_proj.T, preferred_element_type=jnp.float32).astype(
        jnp.bfloat16
    )
    grad_context = grad_context.reshape(SEQ_DEV // 2, 2, SEQ_LEN, HEADS, HEAD_DIM)
    grad_qkv = lax.map(attend_backward, (seq_pairs, visible, log_total, grad_context)).reshape(
        TOK_DEV, 3 * D
    )
    grad_w_qkv = jnp.dot(normed_low.T, grad_qkv, preferred_element_type=jnp.float32)
    grad_normed_one = jnp.dot(grad_qkv, w_qkv.T, preferred_element_type=jnp.float32)
    grad_rows_part, grad_gain_one = norm_backward(
        grad_normed_one, gain_one, normal_one, inverse_one
    )
    input_grad = grad_middle + grad_rows_part
    picked = (jnp.arange(EXPERTS, dtype=jnp.int32) == own_expert).astype(jnp.float32)
    spread_in = picked[:, None, None] * grad_in_own[None]
    spread_back = picked[:, None, None] * grad_back_own[None]
    share_in, share_back = (
        lax.psum_scatter(spread_in, "batch", scatter_dimension=1, tiled=True),
        lax.psum_scatter(spread_back, "batch", scatter_dimension=2, tiled=True),
    )
    summed_in, summed_back = (
        lax.all_gather(share_in.astype(jnp.bfloat16), "batch", axis=1, tiled=True).astype(
            share_in.dtype
        ),
        lax.all_gather(share_back.astype(jnp.bfloat16), "batch", axis=2, tiled=True).astype(
            share_back.dtype
        ),
    )
    grad_w_in = lax.dynamic_index_in_dim(summed_in, own_expert, 0, keepdims=True)
    grad_w_back = lax.dynamic_index_in_dim(summed_back, own_expert, 0, keepdims=True)
    summed_gain_one, summed_qkv, summed_proj, summed_gain_two = lax.psum(
        (grad_gain_one, grad_w_qkv, grad_w_proj, grad_gain_two), ("batch", "ffn")
    )
    return (
        block_out,
        input_grad,
        summed_gain_one,
        summed_qkv,
        summed_proj,
        summed_gain_two,
        grad_w_in,
        grad_w_back,
    )


def solution(mesh):
    placed = (
        P(("batch", "ffn"), None),
        P(("batch", "ffn")),
        P(("batch", "ffn"), None),
        P(),
        P(),
        P(),
        P(),
        P(),
        P("batch", None, "ffn"),
        P("batch", "ffn", None),
        P(("batch", "ffn"), None),
    )
    return jax.shard_map(
        body,
        mesh=mesh,
        in_specs=placed,
        out_specs=(
            P(("batch", "ffn"), None),
            P(("batch", "ffn"), None),
            P(),
            P(),
            P(),
            P(),
            P("batch", None, "ffn"),
            P("batch", "ffn", None),
        ),
        check_vma=False,
    )
```

profile of v0, /device:TPU:0, one launch (start us, length us, event | category | flops | bytes accessed | tf_op | source)
XLA Modules:
  0.0 1472.2 jit_solution(17247204716145680450)
XLA Ops:
  12.8 8.3 convolution_convert_fusion.3
  21.2 22.4 %reshape.253 = bf16[3,2,261,3,12,64]{5,4,3,2,1,0:T(8,128)(2,1)} reshape(bf16[1566,2304]{1,0:T(8,128)(2,1)} %convolution_convert_fusion.3) | data formatting | bytes 14432256 | tf_op jit(solution)/shard_map/reshape | solution.py:110
  43.6 26.3 %copy.57 = bf16[3,2,261,3,12,64]{2,5,4,1,3,0:T(8,128)(2,1)} copy(bf16[3,2,261,3,12,64]{5,4,3,2,1,0:T(8,128)(2,1)} %reshape.253) | data formatting | bytes 14432256 | tf_op jit(solution)/shard_map/while | solution.py:115
  70.0 39.4 %while.22 = (s32[]{:T(128)}, bf16[3,2,261,12,64]{2,1,0,4,3:T(2,128)(2,1)}, f32[3,2,12,261,1]{3,2,1,4,0:T(8,128)}, bf16[3,2,261,3,12,64]{2,5,4,1,3,0:T(8,128)(2,1)}, pred[3,2,261]{2,1,0:T(4,128)(4,1)S(1)}, /*index=5*/s32[]{:T(128)}) while((s32[]{:T(128)}, bf16[3,2,261,12,64]{2,1,0,4,3:T(2,128)(2,1)}, f32[3,2,12,261,1]{3,2,1,4,0:T(8,128)}, ...), condition=%wide.region_5.6_spmd, body=%wide.region_2.5_spmd.sunk | while | flops 436914016 | bytes 34198632 | solution.py:115
  141.4 14.8 %scatter_custom_fusion = bf16[2088,768]{1,0:T(8,128)(2,1)} fusion(s32[1566]{0:T(1024)} %fusion.90, f32[1566,768]{1,0:T(8,128)} %get-tuple-element.174, f32[768]{0:T(1024)} %param.22, f32[1566]{0:T(1024)S(1)} %add_rsqrt_fusion, f32[1566]{0:T(1024)S(1)} %broadcast_multiply_fusion.6, bf16[]{:T(256)} %constant.72.clone.1), kind=kCustom, calls=%fused_computation.123 | custom fusion | flops 4810752 | bytes 8041200 | tf_op jit(solution)/shard_map/scatter | solution.py:127
  160.7 80.7 %all_to_all.20 = bf16[8,261,768]{2,1,0:T(8,128)(2,1)} all-to-all(bf16[8,261,768]{2,1,0:T(8,128)(2,1)} %reshape.207), channel_id=1, replica_groups=mesh['batch'=8,'ffn'=4] {'batch'}, dimensions={0} | all-to-all | bytes 6414336 | tf_op jit(solution)/shard_map/all_to_all | solution.py:128
  246.0 13.0 all-gather.7.cloned.1.call-start
  259.0 13.4 scatter_custom_fusion.1
  276.9 76.8 %all_to_all.21 = bf16[8,261,768]{2,1,0:T(8,128)(2,1)} all-to-all(bf16[8,261,768]{2,1,0:T(8,128)(2,1)} %reshape.211), channel_id=1, replica_groups=mesh['batch'=8,'ffn'=4] {'batch'}, dimensions={0} | all-to-all | bytes 6414336 | tf_op jit(solution)/shard_map/all_to_all | solution.py:149
  358.4 65.1 %fusion.38 = (bf16[8352,768]{1,0:T(8,128)(2,1)}, f32[8352,768]{1,0:T(8,128)}) fusion(bf16[8352,768]{1,0:T(8,128)(2,1)} %all-gather.5.cloned.1.call-done, bf16[1,768,768]{2,1,0:T(8,128)(2,1)} %param.23), kind=kOutput, calls=%fused_computation.63 | convolution fusion | flops 10269351936 | bytes 52494336 | tf_op jit(solution)/shard_map/dot_general | solution.py:135
  423.6 16.9 %all-gather.7.cloned.1.call-done = bf16[8352,768]{1,0:T(8,128)(2,1)} async-done(((bf16[2088,768]{1,0:T(8,128)(2,1)}), bf16[8352,768]{1,0:T(8,128)(2,1)}) %all-gather.7.cloned.1.call-update) | async-done | bytes 12828688 | tf_op jit(solution)/shard_map/all_gather | solution.py:152
  440.5 23.6 %fusion.44 = bf16[8352,768]{1,0:T(8,128)(2,1)} fusion(f32[8352,768]{1,0:T(8,128)} %get-tuple-element.176, bf16[8352,768]{1,0:T(8,128)(2,1)} %all-gather.7.cloned.1.call-done, bf16[1,768,768]{2,1,0:T(8,128)(2,1)} %param.24), kind=kOutput, calls=%fused_computation.69 | convolution fusion | flops 9929392128 | bytes 52494336 | tf_op jit(solution)/shard_map/dot_general | solution.py:153
  464.1 17.6 %convolution_convert_fusion = bf16[8352,768]{1,0:T(8,128)(2,1)} fusion(bf16[8352,768]{1,0:T(8,128)(2,1)} %fusion.44, bf16[1,768,768]{2,1,0:T(8,128)(2,1)S(1)} %copy-done.18), kind=kOutput, calls=%fused_computation.85 | convolution fusion | flops 9858834432 | bytes 26836992 | tf_op jit(solution)/shard_map/dot_general | solution.py:160
  483.5 18.0 %fusion.95 = f32[768,768]{1,0:T(8,128)S(1)} fusion(bf16[8352,768]{1,0:T(8,128)(2,1)} %all-gather.5.cloned.1.call-done, bf16[8352,768]{1,0:T(8,128)(2,1)} %fusion.44), kind=kOutput, calls=%fused_computation.166 | convolution fusion | flops 9852420096 | bytes 28016640 | tf_op jit(solution)/shard_map/dot_general | solution.py:158
  501.5 15.9 %fusion.96 = f32[768,768]{1,0:T(8,128)S(1)} fusion(bf16[8352,768]{1,0:T(8,128)(2,1)} %get-tuple-element.175, bf16[8352,768]{1,0:T(8,128)(2,1)} %all-gather.7.cloned.1.call-done), kind=kOutput, calls=%fused_computation.167 | convolution fusion | flops 9852420096 | bytes 28016640 | tf_op jit(solution)/shard_map/dot_general | solution.py:157
  523.8 11.3 copy.72
  535.1 8.8 copy.82
  543.9 16.2 %convolution_convert_fusion.2 = bf16[8352,768]{1,0:T(8,128)(2,1)} fusion(bf16[8352,768]{1,0:T(8,128)(2,1)} %get-tuple-element.175, bf16[1,768,768]{2,1,0:T(8,128)(2,1)} %param.24), kind=kOutput, calls=%fused_computation.87 | convolution fusion | flops 9858834432 | bytes 26836992 | tf_op jit(solution)/shard_map/dot_general | solution.py:138
  560.7 22.2 %reduce-scatter.9.cloned.1.call-done = bf16[2088,768]{1,0:T(8,128)(2,1)} async-done(((bf16[8352,768]{1,0:T(8,128)(2,1)}), bf16[2088,768]{1,0:T(8,128)(2,1)}) %reduce-scatter.9.cloned.1.call-update) | async-done | bytes 3207184 | tf_op jit(solution)/shard_map/reduce_scatter | solution.py:159
  593.1 185.7 %reduce-scatter.13.cloned.1.call-done = f32[96,2304]{1,0:T(8,128)} async-done(((f32[768,2304]{1,0:T(8,128)}), f32[96,2304]{1,0:T(8,128)}) %reduce-scatter.13.cloned.1.call-update) | async-done | bytes 884752
  782.9 98.7 %reduce-scatter.7.cloned.1.call-done = bf16[2088,768]{1,0:T(8,128)(2,1)} async-done(((bf16[8352,768]{1,0:T(8,128)(2,1)}), bf16[2088,768]{1,0:T(8,128)(2,1)}) %reduce-scatter.7.cloned.1.call-update) | async-done | bytes 3207184 | tf_op jit(solution)/shard_map/reduce_scatter | solution.py:137
  892.4 184.8 %reduce-scatter.11.cloned.1.call-done = f32[3,96,768]{2,1,0:T(8,128)} async-done(((f32[3,768,768]{2,1,0:T(8,128)}), f32[3,96,768]{2,1,0:T(8,128)}) %reduce-scatter.11.cloned.1.call-update) | async-done | bytes 884752 | tf_op jit(solution)/shard_map/reduce_scatter | solution.py:193
  1083.9 10.2 gather_fusion.1
  1104.4 9.9 gather_fusion
  1127.9 8.3 reshape.250
  1136.2 9.5 copy.62
  1145.7 82.9 %while.23 = (s32[]{:T(128)}, bf16[3,2,261,3,12,64]{2,1,0,5,4,3:T(2,128)(2,1)}, bf16[3,2,261,3,12,64]{2,5,4,1,3,0:T(8,128)(2,1)}, pred[3,2,261]{2,1,0:T(4,128)(4,...) while((s32[]{:T(128)}, ...), condition=%wide.region_19.20_spmd, body=%wide.region_17.19_spmd.sunk | while | flops 1075265792 | bytes 81865552 | solution.py:180
  1228.6 19.7 %reshape.216 = bf16[1566,2304]{0,1:T(8,128)(2,1)} reshape(bf16[3,2,261,3,12,64]{2,1,0,5,4,3:T(2,128)(2,1)} %get-tuple-element.70) | data formatting | bytes 14432256 | tf_op jit(solution)/shard_map/reshape | solution.py:180
  1255.4 10.1 fusion.91
  1276.8 14.5 fusion.66
  1291.2 40.2 %all-reduce.1 = (f32[768]{0:T(1024)}, f32[768]{0:T(1024)}) all-reduce(f32[768]{0:T(1024)} %get-tuple-element.133, f32[768]{0:T(1024)} %get-tuple-element.131), channel_id=1, replica_groups=mesh['batch'=8,'ffn'=4] {'batch','ffn'}, use_global_device_ids=true, to_apply=%region_23.24 | all-reduce | flops 1536 | bytes 12288 | tf_op jit(solution)/shard_map/psum | solution.py:206
  1339.8 117.6 %all-reduce.5.cloned.1.call-done = (f32[768,2304]{1,0:T(8,128)}, f32[768,768]{1,0:T(8,128)}) async-done(((f32[768,2304]{1,0:T(8,128)}, f32[768,768]{1,0:T(8,128)}), (f32[768,2304]{1,0:T(8,128)}, f32[768,768]{1,0:T(8,128)})) %all-reduce.5.cloned.1.call-update) | async-done | bytes 9437200 | tf_op jit(solution)/shard_map/psum | solution.py:206
  (176 shorter events, 274.9 us)
Async XLA Ops:
  7.2 5.7 copy-start
  7.2 5.7 copy-start.16
  7.2 351.2 %all-gather.5.cloned.1.call-start = ((), (), s32[]{:S(2)}) async-start(), calls=%async_computation.8 | async-start | bytes 16035840 | tf_op jit(solution)/shard_map/all_gather | solution.py:134
  7.3 5.6 copy-start.1
  9.5 2.7 copy-start.11
  43.6 26.3 %copy-start.20 = (s32[6]{0:T(128)S(1)}, s32[6]{0:T(128)}, u32[]{:S(2)}) copy-start(s32[6]{0:T(128)} %param.16) | copy-start | bytes 76
  109.5 14.9 %copy-start.10 = (pred[3,2,261]{2,1,0:T(4,128)(4,1)}, pred[3,2,261]{2,1,0:T(4,128)(4,1)S(1)}, u32[]{:S(2)}) copy-start(pred[3,2,261]{2,1,0:T(4,128)(4,1)S(1)} %get-tuple-element.352) | copy-start | bytes 4702
  124.4 31.8 %copy-start.6 = (f32[1566]{0:T(1024)}, f32[1566]{0:T(1024)S(1)}, u32[]{:S(2)}) copy-start(f32[1566]{0:T(1024)S(1)} %broadcast_multiply_fusion.6) | copy-start | bytes 18796
  127.4 33.3 %copy-start.8 = (f32[1566]{0:T(1024)}, f32[1566]{0:T(1024)S(1)}, u32[]{:S(2)}) copy-start(f32[1566]{0:T(1024)S(1)} %add_rsqrt_fusion) | copy-start | bytes 18796
  246.0 194.5 %all-gather.7.cloned.1.call-start = ((), (), s32[]{:S(2)}) async-start(), calls=%async_computation.10 | async-start | bytes 16035840 | tf_op jit(solution)/shard_map/all_gather | solution.py:152
  358.3 224.6 %reduce-scatter.9.cloned.1.call-start = ((), (), s32[]{:S(2)}) async-start(), calls=%async_computation.11 | async-start | bytes 16035840 | tf_op jit(solution)/shard_map/reduce_scatter | solution.py:159
  440.5 23.6 %copy-start.18 = (bf16[1,768,768]{2,1,0:T(8,128)(2,1)S(1)}, bf16[1,768,768]{2,1,0:T(8,128)(2,1)}, u32[]{:S(2)}) copy-start(bf16[1,768,768]{2,1,0:T(8,128)(2,1)} %param.23) | copy-start | bytes 3538948
  481.7 0.7 copy-start.21
  481.7 297.0 %reduce-scatter.13.cloned.1.call-start = ((), (), s32[]{:S(2)}) async-start(), calls=%async_computation.15 | async-start | bytes 7962624
  543.9 337.7 %reduce-scatter.7.cloned.1.call-start = ((), (), s32[]{:S(2)}) async-start(), calls=%async_computation.9 | async-start | bytes 16035840 | tf_op jit(solution)/shard_map/reduce_scatter | solution.py:137
  560.1 517.1 %reduce-scatter.11.cloned.1.call-start = ((), (), s32[]{:S(2)}) async-start(), calls=%async_computation.12 | async-start | bytes 7962624 | tf_op jit(solution)/shard_map/reduce_scatter | solution.py:193
  587.5 298.6 %all-to-all-start.3 = ((bf16[8,261,768]{2,1,0:T(8,128)(2,1)}), bf16[8,261,768]{2,1,0:T(8,128)(2,1)}, u32[]{:S(2)}, u32[]{:S(2)}) async-start(bf16[8,261,768]{2,1,0:T(8,128)(2,1)} %reshape.213), calls=%async_computation.5 | async-start | bytes 6488064 | tf_op jit(solution)/shard_map/all_to_all | solution.py:166
  593.0 674.2 %all-gather.11.cloned.1.call-start = ((), (), s32[]{:S(2)}) async-start(), calls=%async_computation.14 | async-start | bytes 3981312 | tf_op jit(solution)/shard_map/all_gather | solution.py:200
  886.1 5.7 copy-start.15
  886.1 213.7 %all-to-all-start.1 = ((bf16[8,261,768]{2,1,0:T(8,128)(2,1)}), bf16[8,261,768]{2,1,0:T(8,128)(2,1)}, u32[]{:S(2)}, u32[]{:S(2)}) async-start(bf16[8,261,768]{2,1,0:T(8,128)(2,1)} %reshape.209), calls=%async_computation.2 | async-start | bytes 6488064 | tf_op jit(solution)/shard_map/all_to_all | solution.py:144
  891.8 382.2 %all-gather.9.cloned.1.call-start = ((), (), s32[]{:S(2)}) async-start(), calls=%async_computation.13 | async-start | bytes 3981312 | tf_op jit(solution)/shard_map/all_gather | solution.py:197
  1079.3 378.1 %all-reduce.5.cloned.1.call-start = ((), (), s32[]{:S(2)}) async-start(), calls=%async_computation.16 | async-start | bytes 18874368 | tf_op jit(solution)/shard_map/psum | solution.py:206
  1083.9 10.2 copy-start.7
  1083.9 10.2 copy-start.9
  1115.1 9.2 copy-start.19
  1122.1 2.2 copy-start.3
  1248.3 7.0 copy-start.2
  1248.4 7.0 copy-start.4
  1248.4 7.0 copy-start.12
  1248.4 7.0 copy-start.14
  1248.4 7.0 copy-start.17
  1457.4 6.6 copy-start.5
  (1 other events, 0.6 us)
Sparse Core Ops, SparseCore 0:
  246.1 81.9 all-gather.4
  358.4 81.9 all-gather.6
  481.8 101.0 reduce-scatter.8
  587.1 191.5 reduce-scatter.12
  781.4 100.1 reduce-scatter.6
  885.6 191.6 reduce-scatter.10
  1080.0 64.2 all-gather.10
  1146.5 63.6 all-gather.8
  1265.6 191.7 all-reduce.4
where the time goes:
time: 1480 us; the launch traced here: 1470 us
  waiting for transfers between devices  627 us (42%)
  matrix products  265 us (18%)
  local copies, waits for them, and re-layouts  249 us (17%)
  blocking collectives  198 us (13%)
  other arithmetic  92.5 us (6%)
  starting transfers between devices  24.4 us (2%)
  between operations  16 us (1%)
    unnamed x10, waiting for transfers between devices  186 us
    reduce_scatter x1, waiting for transfers between devices, body(): lax.psum_scatter(spread_in, 'batch', scatter_dimension=1, tiled=True)  185 us
    psum x1, waiting for transfers between devices, body(): lax.psum((grad_gain_one, grad_w_qkv, grad_w_proj, grad_gain_two), ('batch...  118 us
    reduce_scatter x1, waiting for transfers between devices, body(): lax.psum_scatter(jnp.dot(hidden, w_back_own, preferred_element_type=jnp.f...  98.7 us
    all_to_all x1, blocking collectives, body(): lax.all_to_all(outgoing.reshape(n_batch, capacity, D), 'batch', split_axi...  80.7 us
    all_to_all x1, blocking collectives, body(): lax.all_to_all(grad_slots.reshape(n_batch, capacity, D), 'batch', split_a...  76.8 us
    dot_general x1, matrix products, body(): inner_act = jnp.dot(gathered, w_in_own, preferred_element_type=jnp.float32)  65.1 us
    psum x1, blocking collectives, body(): lax.psum((grad_gain_one, grad_w_qkv, grad_w_proj, grad_gain_two), ('batch...  40.2 us
  transfers between devices with their start and end apart: 11, of which 6 were waited for; matrix products, arithmetic and copies ran while one was open for 27% of the time, Pallas kernels for 0%

commit v1 on v0

v1 whole, which is shorter than its diff:
```python
import functools
import math

import jax
import jax.numpy as jnp
from jax import lax
from jax.experimental import pallas as pl
from jax.experimental.pallas import tpu as pltpu
from jax.sharding import PartitionSpec as P

D = 768
HEADS = 12
HEAD_DIM = 64
EXPERTS = 3
PATCHES = 197
SEQ_DEV = 6
SEQ_LEN = 261
TOK_DEV = 1566
ROWS = 1584
SORTED = 1568
WIN = 288
TILE = 528
LANES = 1664
EPS = 1e-05
F32 = jnp.float32
BF16 = jnp.bfloat16
I32 = jnp.int32
CONTRACT_LANES = (((1,), (1,)), ((), ()))
CONTRACT_ROWS = (((0,), (0,)), ((), ()))


def params(**extra):
    return pltpu.CompilerParams(vmem_limit_bytes=60 << 20, **extra)


def cost(flops, moved):
    return pl.CostEstimate(flops=int(flops), bytes_accessed=int(moved), transcendentals=0)


def dot(a, b, dims=(((1,), (0,)), ((), ()))):
    return lax.dot_general(a, b, dims, preferred_element_type=F32)


def full(shape):
    zeros = (0,) * len(shape)
    return pl.BlockSpec(shape, lambda *_: zeros)


def once(shape):
    zeros = (0,) * len(shape)
    return pl.BlockSpec(shape, lambda *_: zeros, pipeline_mode=pl.Buffered(1))


def row_mask(start, rows, limit):
    return start + lax.broadcasted_iota(I32, (rows, 1), 0) < limit


def norm_parts(values):
    average = jnp.mean(values, axis=-1, keepdims=True)
    centred = values - average
    variance = jnp.mean(centred * centred, axis=-1, keepdims=True)
    inverse = lax.rsqrt(variance + EPS)
    return centred * inverse, inverse


def norm_pull(grad_normed, gain, normal, inverse):
    scaled = grad_normed * gain
    mean_grad = jnp.mean(scaled, axis=-1, keepdims=True)
    mean_proj = jnp.mean(scaled * normal, axis=-1, keepdims=True)
    return inverse * (scaled - mean_grad - normal * mean_proj)


def route_kernel(n_batch, gm_ref, routes_ref, pos_ref, offs_ref):
    routes = routes_ref[...]
    lane = lax.broadcasted_iota(I32, (8, LANES), 1)
    sub = lax.broadcasted_iota(I32, (8, LANES), 0)
    expert = jnp.zeros((1, LANES), I32)
    for b in range(n_batch):
        expert = jnp.where(routes == b, gm_ref[b], expert)
    live = lane < TOK_DEV
    hot = jnp.where((jnp.broadcast_to(expert, (8, LANES)) == sub) & live, 1, 0)
    count = hot
    step = 1
    while step < LANES:
        count = count + jnp.where(lane >= step, pltpu.roll(count, step, 1), 0)
        step *= 2
    totals = [jnp.sum(hot[e : e + 1, :], axis=1, keepdims=True) for e in range(EXPERTS)]
    starts = [jnp.zeros((1, 1), I32)]
    for e in range(EXPERTS):
        starts.append(starts[-1] + totals[e])
    pos = jnp.zeros((1, LANES), I32)
    for e in range(EXPERTS):
        pos = pos + jnp.where(hot[e : e + 1, :] > 0, count[e : e + 1, :] - 1 + starts[e], 0)
    pos_ref[...] = jnp.where(live[0:1, :], pos, -1)
    slot = lax.broadcasted_iota(I32, (1, 128), 1)
    offs = jnp.zeros((1, 128), I32)
    for e in range(EXPERTS + 1):
        offs = jnp.where(slot == e, starts[e], offs)
    offs_ref[...] = offs


def route_rows(routes_row, group_map):
    n_batch = group_map.shape[0]
    return pl.pallas_call(
        functools.partial(route_kernel, n_batch),
        out_shape=(
            jax.ShapeDtypeStruct((1, LANES), I32),
            jax.ShapeDtypeStruct((1, 128), I32),
        ),
        in_specs=[
            pl.BlockSpec(memory_space=pltpu.SMEM),
            pl.BlockSpec(memory_space=pltpu.VMEM),
        ],
        out_specs=(
            pl.BlockSpec(memory_space=pltpu.VMEM),
            pl.BlockSpec(memory_space=pltpu.VMEM),
        ),
        compiler_params=params(),
        name="route",
    )(group_map, routes_row)


SORT_TILE = 224


def sort_into(out_ref, rows_ref, pos_ref):
    pos = pos_ref[0:1, 0:ROWS]
    for i in range(SORTED // SORT_TILE):
        want = i * SORT_TILE + lax.broadcasted_iota(I32, (SORT_TILE, ROWS), 0)
        hot = jnp.where(pos == want, 1.0, 0.0).astype(BF16)
        out_ref[i * SORT_TILE : (i + 1) * SORT_TILE, :] = dot(hot, rows_ref[...]).astype(BF16)


def sort_kernel(rows_ref, pos_ref, out_ref, held):
    held[1552:ROWS, :] = jnp.zeros((ROWS - 1552, D), BF16)
    held[0:TOK_DEV, :] = rows_ref[...]
    sort_into(out_ref, held, pos_ref)


def sort_rows(rows, pos):
    return pl.pallas_call(
        sort_kernel,
        out_shape=jax.ShapeDtypeStruct((SORTED, D), BF16),
        scratch_shapes=[pltpu.VMEM((ROWS, D), BF16)],
        compiler_params=params(),
        cost_estimate=cost(2 * SORTED * ROWS * D, 4 * ROWS * D),
        name="sort_rows",
    )(rows, pos)


def qkv_kernel(tok_ref, gain_ref, w_ref, out_ref):
    normal, _ = norm_parts(tok_ref[...].astype(F32))
    keep = row_mask(pl.program_id(0) * TILE, TILE, TOK_DEV)
    normed = jnp.where(keep, normal * gain_ref[...], 0.0).astype(BF16)
    out_ref[...] = dot(normed, w_ref[...]).astype(BF16)


def qkv_rows(tokens, gain, w_qkv):
    return pl.pallas_call(
        qkv_kernel,
        grid=(ROWS // TILE,),
        out_shape=jax.ShapeDtypeStruct((ROWS, 3 * D), BF16),
        in_specs=[
            pl.BlockSpec((TILE, D), lambda i: (i, 0)),
            full((1, D)),
            once((D, 3 * D)),
        ],
        out_specs=pl.BlockSpec((TILE, 3 * D), lambda i: (i, 0)),
        compiler_params=params(),
        cost_estimate=cost(2 * ROWS * D * 3 * D, 2 * ROWS * D * 4),
        name="qkv",
    )(tokens, gain, w_qkv)


def window(pair):
    first = pair * SEQ_LEN
    start = first // 16 * 16
    return start, first - start


def attend_kernel(len_ref, qkv_ref, ctx_ref, lse_ref, stat):
    pair = pl.program_id(0)
    start, skip = window(pair)
    start = pl.multiple_of(start, 16)

    @pl.when(pair == 0)
    def _():
        ctx_ref[...] = jnp.zeros_like(ctx_ref)

    key = lax.broadcasted_iota(I32, (1, WIN), 1)
    seen = (key >= skip) & (key < skip + PATCHES + len_ref[pair])
    bias = jnp.where(seen, 0.0, -1e30)
    row = lax.broadcasted_iota(I32, (WIN, 1), 0)
    mine = (row >= skip) & (row < skip + SEQ_LEN)
    lane = lax.broadcasted_iota(I32, (WIN, 128), 1)
    stat[...] = jnp.zeros_like(stat)
    for hp in range(HEADS // 2):
        cols = slice(hp * 128, hp * 128 + 128)
        q = qkv_ref[pl.ds(start, WIN), hp * 128 : hp * 128 + 128]
        k = qkv_ref[pl.ds(start, WIN), D + hp * 128 : D + hp * 128 + 128]
        v = qkv_ref[pl.ds(start, WIN), 2 * D + hp * 128 : 2 * D + hp * 128 + 128]
        q = q * jnp.asarray(HEAD_DIM**-0.5, BF16)
        pieces = []
        for half in range(2):
            inside = (lane < 64) if half == 0 else (lane >= 64)
            qh = jnp.where(inside, q, jnp.zeros_like(q))
            scores = dot(qh, k, CONTRACT_LANES) + bias
            peak = jnp.max(scores, axis=1, keepdims=True)
            weight = jnp.exp(scores - peak).astype(BF16)
            vh = jnp.where(inside, v, jnp.ones_like(v))
            mixed = dot(weight, vh)
            total = pltpu.roll(mixed, 64, 1)
            pieces.append(mixed / total)
            one = total[:, 0:1] if half == 0 else mixed[:, 0:1]
            head = hp * 2 + half
            stat[0:WIN, :] = jnp.where(lane == head, peak + jnp.log(one), stat[0:WIN, :])
        ctx = jnp.where(lane < 64, pieces[0], pieces[1]).astype(BF16)
        old = ctx_ref[pl.ds(start, WIN), cols]
        ctx_ref[pl.ds(start, WIN), cols] = jnp.where(mine, ctx, old)
    lse_ref[0] = jnp.transpose(stat[...])[0:16, :]


def attend(qkv, lengths):
    return pl.pallas_call(
        attend_kernel,
        grid=(SEQ_DEV,),
        out_shape=(
            jax.ShapeDtypeStruct((ROWS, D), BF16),
            jax.ShapeDtypeStruct((SEQ_DEV, 16, 384), F32),
        ),
        in_specs=[
            pl.BlockSpec(memory_space=pltpu.SMEM),
            once((ROWS, 3 * D)),
        ],
        out_specs=(
            full((ROWS, D)),
            pl.BlockSpec((1, 16, 384), lambda s: (s, 0, 0)),
        ),
        scratch_shapes=[pltpu.VMEM((384, 128), F32)],
        compiler_params=params(),
        cost_estimate=cost(72 * 4 * WIN * 384 * 128, 2 * ROWS * D * 4),
        name="attend",
    )(lengths, qkv)


def middle_kernel(ctx_ref, w_ref, tok_ref, gain_ref, pos_ref, mid_ref, out_ref, held):
    held[1552:ROWS, :] = jnp.zeros((ROWS - 1552, D), BF16)
    for i in range(3):
        top = min(TILE * (i + 1), TOK_DEV)
        rows = slice(TILE * i, top)
        attended = dot(ctx_ref[rows, :], w_ref[...])
        middle = tok_ref[rows, :].astype(F32) + attended
        mid_ref[rows, :] = middle
        normal, _ = norm_parts(middle)
        held[rows, :] = (normal * gain_ref[...]).astype(BF16)
    sort_into(out_ref, held, pos_ref)


def middle_rows(ctx, w_proj, tokens, gain, pos):
    return pl.pallas_call(
        middle_kernel,
        out_shape=(
            jax.ShapeDtypeStruct((TOK_DEV, D), F32),
            jax.ShapeDtypeStruct((SORTED, D), BF16),
        ),
        scratch_shapes=[pltpu.VMEM((ROWS, D), BF16)],
        compiler_params=params(),
        cost_estimate=cost(2 * SORTED * ROWS * D + 2 * ROWS * D * D, 12 * ROWS * D),
        name="middle",
    )(ctx, w_proj, tokens, gain, pos)


HALF = 384
FF_DEV = 768


def gelu_both(u):
    below = 0.5 * (1.0 + lax.erf(u * (1.0 / math.sqrt(2.0))))
    density = jnp.exp(-0.5 * u * u) * (1.0 / math.sqrt(2.0 * math.pi))
    return u * below, below + u * density


def expert_kernel(
    n_src,
    offs_ref,
    hosts_ref,
    x_ref,
    g_ref,
    wi_hbm,
    wb_hbm,
    out_ref,
    gx_ref,
    dwi_hbm,
    dwb_hbm,
    wi,
    wb,
    acc_i,
    acc_b,
    sems,
):
    src = pl.program_id(0)

    def weight_copies():
        for e in range(EXPERTS):
            for p in range(2):
                host = hosts_ref[e * 2 + p]
                part = pl.ds(p * HALF, HALF)
                yield pltpu.make_async_copy(
                    wi_hbm.at[host], wi.at[e, :, part], sems.at[e * 4 + p * 2]
                )
                yield pltpu.make_async_copy(
                    wb_hbm.at[host], wb.at[e, part, :], sems.at[e * 4 + p * 2 + 1]
                )

    @pl.when(src == 0)
    def _():
        for copy in weight_copies():
            copy.start()
        acc_i[...] = jnp.zeros_like(acc_i)
        acc_b[...] = jnp.zeros_like(acc_b)
        for copy in weight_copies():
            copy.wait()

    tail = slice(SORTED - 16, SORTED)
    out_ref[0, tail, :] = jnp.zeros((16, D), BF16)
    gx_ref[0, tail, :] = jnp.zeros((16, D), BF16)

    def visit(e, low, first, last, size):
        start = pl.multiple_of(jnp.minimum(low, SORTED - size), 16)
        rows = pl.ds(start, size)
        row = start + lax.broadcasted_iota(I32, (size, 1), 0)
        mine = (row >= jnp.maximum(first, low)) & (row < last)
        x = jnp.where(mine, x_ref[0, rows, :], jnp.zeros((), BF16))
        g = jnp.where(mine, g_ref[0, rows, :], jnp.zeros((), BF16))
        inner = dot(x, wi[e])
        hidden, slope = gelu_both(inner)
        hidden = hidden.astype(BF16)
        branch = dot(hidden, wb[e]).astype(BF16)
        grad_hidden = dot(g, wb[e], CONTRACT_LANES).astype(BF16)
        grad_inner = (grad_hidden.astype(F32) * slope).astype(BF16)
        grad_x = dot(grad_inner, wi[e], CONTRACT_LANES).astype(BF16)
        out_ref[0, rows, :] = jnp.where(mine, branch, out_ref[0, rows, :])
        gx_ref[0, rows, :] = jnp.where(mine, grad_x, gx_ref[0, rows, :])
        acc_b[e] += dot(hidden, g, CONTRACT_ROWS)
        acc_i[e] += dot(x, grad_inner, CONTRACT_ROWS)

    for e in range(EXPERTS):
        first = offs_ref[src * 4 + e]
        last = offs_ref[src * 4 + e + 1]
        base = first // 16 * 16
        span = last - base
        span = jnp.where(last > first, span, 0)
        big = span // 256

        @pl.loop(0, big)
        def _(i):
            visit(e, base + i * 256, first, last, 256)

        rest = base + big * 256
        small = (span - big * 256 + 127) // 128

        @pl.loop(0, small)
        def _(i):
            visit(e, rest + i * 128, first, last, 128)

    @pl.when(src == n_src - 1)
    def _():
        copies = []
        for e in range(EXPERTS):
            wi[e] = acc_i[e].astype(BF16)
            wb[e] = acc_b[e].astype(BF16)
            copies.append(pltpu.make_async_copy(wi.at[e], dwi_hbm.at[e], sems.at[e * 2]))
            copies.append(pltpu.make_async_copy(wb.at[e], dwb_hbm.at[e], sems.at[e * 2 + 1]))
            copies[-2].start()
            copies[-1].start()
        for copy in copies:
            copy.wait()


def experts(offs, hosts, x, g, wi, wb):
    n_src = x.shape[0]
    block = pl.BlockSpec((1, SORTED, D), lambda s, *_: (s, 0, 0))
    any_space = pl.BlockSpec(memory_space=pl.ANY)
    return pl.pallas_call(
        functools.partial(expert_kernel, n_src),
        grid_spec=pltpu.PrefetchScalarGridSpec(
            num_scalar_prefetch=2,
            grid=(n_src,),
            in_specs=[block, block, any_space, any_space],
            out_specs=[block, block, any_space, any_space],
            scratch_shapes=[
                pltpu.VMEM((EXPERTS, D, FF_DEV), BF16),
                pltpu.VMEM((EXPERTS, FF_DEV, D), BF16),
                pltpu.VMEM((EXPERTS, D, FF_DEV), F32),
                pltpu.VMEM((EXPERTS, FF_DEV, D), F32),
                pltpu.SemaphoreType.DMA((EXPERTS * 4,)),
            ],
        ),
        out_shape=(
            jax.ShapeDtypeStruct((n_src, SORTED, D), BF16),
            jax.ShapeDtypeStruct((n_src, SORTED, D), BF16),
            jax.ShapeDtypeStruct((EXPERTS, D, FF_DEV), BF16),
            jax.ShapeDtypeStruct((EXPERTS, FF_DEV, D), BF16),
        ),
        compiler_params=params(),
        cost_estimate=cost(12 * n_src * SORTED * D * FF_DEV, 8 * n_src * SORTED * D),
        name="experts",
    )(offs, hosts, x, g, wi, wb)


def unsort(pos_col, src):
    want = lax.broadcasted_iota(I32, (pos_col.shape[0], SORTED), 1)
    hot = jnp.where(pos_col == want, 1.0, 0.0).astype(BF16)
    return dot(hot, src)


def back_kernel(
    a_ref,
    b_ref,
    c_ref,
    pos_ref,
    mid_ref,
    cot_ref,
    gain_ref,
    ctx_ref,
    w_ref,
    gm_ref,
    gctx_ref,
    dw_ref,
    dg_ref,
    total,
):
    step = pl.program_id(0)

    @pl.when(step == 0)
    def _():
        both = a_ref[...].astype(F32) + b_ref[...].astype(F32) + c_ref[...].astype(F32)
        total[...] = both.astype(BF16)
        dw_ref[...] = jnp.zeros_like(dw_ref)
        dg_ref[...] = jnp.zeros_like(dg_ref)

    keep = row_mask(step * TILE, TILE, TOK_DEV)
    grad_normed = unsort(pos_ref[...], total[...])
    middle = jnp.where(keep, mid_ref[...], 0.0)
    normal, inverse = norm_parts(middle)
    dg_ref[...] += jnp.sum(grad_normed * normal, axis=0, keepdims=True)
    part = norm_pull(grad_normed, gain_ref[...], normal, inverse)
    grad_middle = jnp.where(keep, cot_ref[...].astype(F32) + part, 0.0)
    gm_ref[...] = grad_middle
    low = grad_middle.astype(BF16)
    dw_ref[...] += dot(ctx_ref[...], low, CONTRACT_ROWS)
    gctx_ref[...] = dot(low, w_ref[...], CONTRACT_LANES).astype(BF16)


def back_rows(a, b, c, pos_col, middle, cot, gain, ctx, w_proj):
    tile = pl.BlockSpec((TILE, D), lambda i: (i, 0))
    return pl.pallas_call(
        back_kernel,
        grid=(ROWS // TILE,),
        out_shape=(
            jax.ShapeDtypeStruct((TOK_DEV, D), F32),
            jax.ShapeDtypeStruct((ROWS, D), BF16),
            jax.ShapeDtypeStruct((D, D), F32),
            jax.ShapeDtypeStruct((1, D), F32),
        ),
        in_specs=[
            once((SORTED, D)),
            once((SORTED, D)),
            once((SORTED, D)),
            pl.BlockSpec((TILE, 1), lambda i: (i, 0)),
            tile,
            tile,
            full((1, D)),
            tile,
            once((D, D)),
        ],
        out_specs=(tile, tile, full((D, D)), full((1, D))),
        scratch_shapes=[pltpu.VMEM((SORTED, D), BF16)],
        compiler_params=params(),
        cost_estimate=cost(2 * ROWS * D * (SORTED + 2 * D), 24 * ROWS * D),
        name="back",
    )(a, b, c, pos_col, middle, cot, gain, ctx, w_proj)


def finish_kernel(a_ref, b_ref, c_ref, pos_ref, mid_ref, out_ref, total):
    @pl.when(pl.program_id(0) == 0)
    def _():
        both = a_ref[...].astype(F32) + b_ref[...].astype(F32) + c_ref[...].astype(F32)
        total[...] = both.astype(BF16)

    out_ref[...] = mid_ref[...] + unsort(pos_ref[...], total[...])


def finish_rows(a, b, c, pos_col, middle):
    tile = pl.BlockSpec((TILE, D), lambda i: (i, 0))
    return pl.pallas_call(
        finish_kernel,
        grid=(ROWS // TILE,),
        out_shape=jax.ShapeDtypeStruct((TOK_DEV, D), F32),
        in_specs=[
            once((SORTED, D)),
            once((SORTED, D)),
            once((SORTED, D)),
            pl.BlockSpec((TILE, 1), lambda i: (i, 0)),
            tile,
        ],
        out_specs=tile,
        scratch_shapes=[pltpu.VMEM((SORTED, D), BF16)],
        compiler_params=params(),
        cost_estimate=cost(2 * ROWS * D * SORTED, 14 * ROWS * D),
        name="finish",
    )(a, b, c, pos_col, middle)


def attend_back_kernel(len_ref, qkv_ref, gctx_ref, lse_ref, out_ref):
    pair = pl.program_id(0)
    start, skip = window(pair)
    start = pl.multiple_of(start, 16)

    @pl.when(pair == 0)
    def _():
        out_ref[...] = jnp.zeros_like(out_ref)

    row = lax.broadcasted_iota(I32, (WIN, 1), 0)
    mine = (row >= skip) & (row < skip + SEQ_LEN)
    bias = jnp.where((row >= skip) & (row < skip + PATCHES + len_ref[pair]), 0.0, -1e30)
    lane = lax.broadcasted_iota(I32, (WIN, 128), 1)
    scale = jnp.asarray(HEAD_DIM**-0.5, BF16)
    for hp in range(HEADS // 2):
        spots = [slice(part * D + hp * 128, part * D + hp * 128 + 128) for part in range(3)]
        q, k, v = [qkv_ref[pl.ds(start, WIN), spot] for spot in spots]
        q = q * scale
        ks = k * scale
        go = gctx_ref[pl.ds(start, WIN), hp * 128 : hp * 128 + 128]
        q = jnp.where(mine, q, jnp.zeros_like(q))
        go = jnp.where(mine, go, jnp.zeros_like(go))
        grads = []
        for half in range(2):
            head = hp * 2 + half
            inside = (lane < 64) if half == 0 else (lane >= 64)
            qh = jnp.where(inside, q, jnp.zeros_like(q))
            gh = jnp.where(inside, go, jnp.zeros_like(go))
            scores = dot(k, qh, CONTRACT_LANES)
            probs = jnp.exp(scores + bias - lse_ref[0, head : head + 1, 0:WIN])
            grad_probs = dot(v, gh, CONTRACT_LANES)
            delta = jnp.sum(probs * grad_probs, axis=0, keepdims=True)
            grad_scores = (probs * (grad_probs - delta)).astype(BF16)
            grad_v = dot(probs.astype(BF16), go)
            grad_k = dot(grad_scores, q)
            grad_q = dot(grad_scores, ks, CONTRACT_ROWS)
            grads.append((grad_q, grad_k, grad_v))
        for spot, low, high in zip(spots, grads[0], grads[1]):
            new = jnp.where(lane < 64, low, high).astype(BF16)
            old = out_ref[pl.ds(start, WIN), spot]
            out_ref[pl.ds(start, WIN), spot] = jnp.where(mine, new, old)


def attend_back(qkv, gctx, lse, lengths):
    return pl.pallas_call(
        attend_back_kernel,
        grid=(SEQ_DEV,),
        out_shape=jax.ShapeDtypeStruct((ROWS, 3 * D), BF16),
        in_specs=[
            pl.BlockSpec(memory_space=pltpu.SMEM),
            once((ROWS, 3 * D)),
            once((ROWS, D)),
            pl.BlockSpec((1, 16, 384), lambda s: (s, 0, 0)),
        ],
        out_specs=full((ROWS, 3 * D)),
        compiler_params=params(),
        cost_estimate=cost(72 * 10 * WIN * 384 * 128, 2 * ROWS * D * 7),
        name="attend_back",
    )(lengths, qkv, gctx, lse)


def first_back_kernel(tok_ref, gain_ref, gq_ref, w_ref, gm_ref, ig_ref, dw_ref, dg_ref):
    step = pl.program_id(0)

    @pl.when(step == 0)
    def _():
        dw_ref[...] = jnp.zeros_like(dw_ref)
        dg_ref[...] = jnp.zeros_like(dg_ref)

    keep = row_mask(step * TILE, TILE, TOK_DEV)
    tokens = jnp.where(keep, tok_ref[...].astype(F32), 0.0)
    normal, inverse = norm_parts(tokens)
    normed = (normal * gain_ref[...]).astype(BF16)
    grad_qkv = gq_ref[...]
    dw_ref[...] += dot(normed, grad_qkv, CONTRACT_ROWS)
    grad_normed = dot(grad_qkv, w_ref[...], CONTRACT_LANES)
    dg_ref[...] += jnp.sum(grad_normed * normal, axis=0, keepdims=True)
    ig_ref[...] = gm_ref[...] + norm_pull(grad_normed, gain_ref[...], normal, inverse)


def first_back(tokens, gain, grad_qkv, w_qkv, grad_middle):
    tile = pl.BlockSpec((TILE, D), lambda i: (i, 0))
    return pl.pallas_call(
        first_back_kernel,
        grid=(ROWS // TILE,),
        out_shape=(
            jax.ShapeDtypeStruct((TOK_DEV, D), F32),
            jax.ShapeDtypeStruct((D, 3 * D), F32),
            jax.ShapeDtypeStruct((1, D), F32),
        ),
        in_specs=[
            tile,
            full((1, D)),
            pl.BlockSpec((TILE, 3 * D), lambda i: (i, 0)),
            once((D, 3 * D)),
            tile,
        ],
        out_specs=(tile, full((D, 3 * D)), full((1, D))),
        compiler_params=params(),
        cost_estimate=cost(4 * ROWS * D * 3 * D, 16 * ROWS * D),
        name="first_back",
    )(tokens, gain, grad_qkv, w_qkv, grad_middle)


def swap(rows, bit):
    pairs = [(f, f ^ bit) for f in range(4)]
    return lax.ppermute(rows, "ffn", pairs)


def spread(rows):
    near = swap(rows, 1)
    far = swap(rows, 2)
    return [rows, near, far, swap(far, 1)]


def body(
    tokens,
    text_lengths,
    routes,
    group_map,
    gain_one,
    w_qkv,
    w_proj,
    gain_two,
    w_in,
    w_back,
    cotangent,
):
    n_batch = lax.axis_size("batch")
    own = lax.axis_index("batch")
    gain_one = gain_one.reshape(1, D)
    gain_two = gain_two.reshape(1, D)
    own_expert = group_map[own]
    order = jnp.arange(n_batch, dtype=I32)
    rank = jnp.sum(jnp.where((group_map == own_expert) & (order < own), 1, 0))
    part = jnp.minimum(rank, 1)
    hosting = group_map[None, :] == jnp.arange(EXPERTS, dtype=I32)[:, None]
    first_host = jnp.min(jnp.where(hosting, order[None, :], n_batch), axis=1)
    later = hosting & (order[None, :] > first_host[:, None])
    second_host = jnp.min(jnp.where(later, order[None, :], n_batch), axis=1)
    hosts = jnp.stack([first_host, second_host], axis=1).reshape(2 * EXPERTS)

    wi_part = lax.dynamic_slice(w_in[0], (0, part * HALF), (D, HALF))
    wb_part = lax.dynamic_slice(w_back[0], (part * HALF, 0), (HALF, D))
    wi_all = lax.all_gather(wi_part, "batch", axis=0)
    wb_all = lax.all_gather(wb_part, "batch", axis=0)

    routes_row = jnp.pad(routes.reshape(1, TOK_DEV), ((0, 0), (0, LANES - TOK_DEV)))
    pos, offs = route_rows(routes_row, group_map)
    pos_col = pos.reshape(LANES, 1)[0:ROWS]
    offs_all = jnp.concatenate([o[0, 0:4] for o in spread(offs)])

    grads_sorted = sort_rows(cotangent, pos)
    g_all = jnp.stack(spread(grads_sorted))

    qkv = qkv_rows(tokens, gain_one, w_qkv)
    context, lse = attend(qkv, text_lengths)
    middle, sending = middle_rows(context, w_proj, tokens, gain_two, pos)
    x_all = jnp.stack(spread(sending))

    out, gx, dwi, dwb = experts(offs_all, hosts, x_all, g_all, wi_all, wb_all)

    def collect(parts):
        near = swap(parts[1], 1)
        far = (parts[2].astype(F32) + swap(parts[3], 1).astype(F32)).astype(BF16)
        return parts[0], near, swap(far, 2)

    grad_middle, gctx, dw_proj, dg_two = back_rows(
        *collect(gx), pos_col, middle, cotangent, gain_two, context, w_proj
    )
    block_out = finish_rows(*collect(out), pos_col, middle)
    grad_qkv = attend_back(qkv, gctx, lse, text_lengths)
    input_grad, dw_qkv, dg_one = first_back(tokens, gain_one, grad_qkv, w_qkv, grad_middle)

    def settle(grad, dim):
        share = lax.psum_scatter(grad, "batch", scatter_dimension=dim, tiled=True)
        whole = lax.all_gather(share, "batch", axis=dim, tiled=True)
        return lax.dynamic_index_in_dim(whole, own_expert, 0, keepdims=True).astype(F32)

    grad_w_in = settle(dwi, 1)
    grad_w_back = settle(dwb, 1)
    summed_qkv, summed_proj = lax.psum(
        (dw_qkv.astype(BF16), dw_proj.astype(BF16)), ("batch", "ffn")
    )
    gains = lax.psum(jnp.concatenate([dg_one, dg_two], axis=0), ("batch", "ffn"))
    return (
        block_out,
        input_grad,
        gains[0],
        summed_qkv.astype(F32),
        summed_proj.astype(F32),
        gains[1],
        grad_w_in,
        grad_w_back,
    )


def solution(mesh):
    placed = (
        P(("batch", "ffn"), None),
        P(("batch", "ffn")),
        P(("batch", "ffn"), None),
        P(),
        P(),
        P(),
        P(),
        P(),
        P("batch", None, "ffn"),
        P("batch", "ffn", None),
        P(("batch", "ffn"), None),
    )
    return jax.shard_map(
        body,
        mesh=mesh,
        in_specs=placed,
        out_specs=(
            P(("batch", "ffn"), None),
            P(("batch", "ffn"), None),
            P(),
            P(),
            P(),
            P(),
            P("batch", None, "ffn"),
            P("batch", "ffn", None),
        ),
        check_vma=False,
    )
```

time: 1480 us -> 759 us (0.51)
  waiting for transfers between devices: 627 us -> 313 us
  matrix products: 265 us -> 0 us
  Pallas kernels: 0 us -> 249 us
  local copies, waits for them, and re-layouts: 249 us -> 20.6 us
  blocking collectives: 198 us -> 92.8 us
  other arithmetic: 92.5 us -> 48.5 us
    reduce_scatter x3 -> x2, waiting for transfers between devices: 306 us -> 0.04 us  [settle(): share = lax.psum_scatter(grad, 'batch', scatter_dimension=dim, tiled=True)]
    dot_general x33 -> x0, matrix products: 265 us -> none  [the longest x1 65.1 us: body(): inner_act = jnp.dot(gathered, w_in_own, preferred_element_type=jnp.float32)]
    pallas_call x0 -> x10, Pallas kernels: none -> 249 us  [the longest x1 86.4 us: experts(): pl.pallas_call(functools.partial(expert_kernel, n_src), grid_spec=pltpu.P...]
    unnamed x10 -> x7, waiting for transfers between devices: 186 us -> 1.25 us
    ppermute x0 -> x15, waiting for transfers between devices: none -> 161 us  [swap(): return lax.ppermute(rows, 'ffn', pairs)]
    all_to_all x2 -> x0, blocking collectives: 158 us -> none  [the longest x1 80.7 us: body(): lax.all_to_all(outgoing.reshape(n_batch, capacity, D), 'batch', split_axi...]
    all_gather x4, waiting for transfers between devices: 17 us -> 122 us  [the longest x2 122 us: settle(): whole = lax.all_gather(share, 'batch', axis=dim, tiled=True)]
    reshape x12 -> x3, local copies, waits for them, and re-layouts: 94.5 us -> 1.77 us  [the longest x1 0.6 us: body(): hosts = jnp.stack([first_host, second_host], axis=1).reshape(2 * EXPERTS)]
  transfers between devices with their start and end apart: 11 -> 22, of which waited for: 6 -> 10; matrix products, arithmetic and copies ran while one was open for 27% -> 8% of each run, Pallas kernels for 0% -> 22%
where the time goes in v1:
time: 759 us; the launch traced here: 753 us
  waiting for transfers between devices  313 us (41%)
  Pallas kernels  249 us (33%)
  blocking collectives  92.8 us (12%)
  other arithmetic  48.5 us (6%)
  local copies, waits for them, and re-layouts  20.6 us (3%)
  between operations  17.3 us (2%)
  starting transfers between devices  11.1 us (1%)
    ppermute x15, waiting for transfers between devices, swap(): return lax.ppermute(rows, 'ffn', pairs)  161 us
    all_gather x2, waiting for transfers between devices, settle(): whole = lax.all_gather(share, 'batch', axis=dim, tiled=True)  122 us
    psum x1, blocking collectives, body(): lax.psum(jnp.concatenate([dg_one, dg_two], axis=0), ('batch', 'ffn'))  92.8 us
    pallas_call x1, Pallas kernels, experts(): pl.pallas_call(functools.partial(expert_kernel, n_src), grid_spec=pltpu.P...  86.4 us
    pallas_call x1, Pallas kernels, attend_back(): pl.pallas_call(attend_back_kernel, grid=(SEQ_DEV,), out_shape=jax.ShapeDt...  38.8 us
    pallas_call x1, Pallas kernels, attend(): pl.pallas_call(attend_kernel, grid=(SEQ_DEV,), out_shape=(jax.ShapeDtypeS...  32.7 us
    psum x1, waiting for transfers between devices, body(): lax.psum((dw_qkv.astype(BF16), dw_proj.astype(BF16)), ('batch', 'ffn'))  28.6 us
    pallas_call x1, Pallas kernels, first_back(): pl.pallas_call(first_back_kernel, grid=(ROWS // TILE,), out_shape=(jax.Sh...  25.1 us
  transfers between devices with their start and end apart: 22, of which 10 were waited for; matrix products, arithmetic and copies ran while one was open for 8% of the time, Pallas kernels for 22%

profile of v1, /device:TPU:0, one launch (start us, length us, event | category | flops | bytes accessed | tf_op | source)
XLA Modules:
  0.0 752.7 jit_solution(14092801740108611732)
XLA Ops:
  8.6 2.0 fusion.3
  14.8 11.0 %qkv.1.qkv_ref = bf16[1584,2304]{1,0:T(8,128)(2,1)} custom-call(bf16[1566,768]{1,0:T(8,128)(2,1)} %tok_ref.5, f32[1,768]{1,0:T(1,128)} %reshape.42.gain_ref, bf16[768,2304]{1,0:T(8,128)(2,1)} %w_ref.7), custom_call_target="tpu_custom_call" | custom-call | flops 5605687296 | bytes 9732096 | tf_op jit(solution)/shard_map/qkv/pallas_call | solution.py:159
  28.9 32.7 %attend.1 = (bf16[1584,768]{1,0:T(8,128)(2,1)}, f32[6,16,384]{2,1,0:T(8,128)}) custom-call(s32[6]{0:T(128)} %len_ref.3, bf16[1584,2304]{1,0:T(8,128)(2,1)} %qkv.1.qkv_ref), custom_call_target="tpu_custom_call" | custom-call | flops 4076863488 | bytes 9732096 | tf_op jit(solution)/shard_map/attend/pallas_call | solution.py:224
  61.7 11.5 %middle.1 = (f32[1566,768]{1,0:T(8,128)}, bf16[1568,768]{1,0:T(8,128)(2,1)}) custom-call(bf16[1584,768]{1,0:T(8,128)(2,1)} %get-tuple-element.26.ctx_ref, bf16[768,768]{1,0:T(8,128)(2,1)} %w_ref.6, bf16[1566,768]{1,0:T(8,128)(2,1)} %tok_ref.5, f32[1,768]{1,0:T(1,128)} %reshape.43.gain_ref, s32[1,1664]{1,0:T(1,128)} %get-tuple-element.27.pos_ref), custom_call_target="tpu_custom_call" | custom-call | flops 5683544064 | bytes 14598144 | tf_op jit(solution)/shard_map/middle/pallas_call | solution.py:260
  73.2 2.9 collective-permute-start.4
  76.2 7.7 %sort_rows.1 = bf16[1568,768]{1,0:T(8,128)(2,1)} custom-call(bf16[1566,768]{1,0:T(8,128)(2,1)} %cot_ref.1, s32[1,1664]{1,0:T(1,128)} %get-tuple-element.27.pos_ref), custom_call_target="tpu_custom_call" | custom-call | flops 3814981632 | bytes 4866048 | tf_op jit(solution)/shard_map/sort_rows/pallas_call | solution.py:141
  83.8 45.8 %collective-permute-done.4 = bf16[1568,768]{1,0:T(8,128)(2,1)} collective-permute-done((bf16[1568,768]{1,0:T(8,128)(2,1)}, bf16[1568,768]{1,0:T(8,128)(2,1)}, u32[]{:S(2)}, u32[]{:S(2)}) %collective-permute-start.4) | collective-permute-done | bytes 2408480 | tf_op jit(solution)/shard_map/ppermute | solution.py:621
  130.1 2.1 collective-permute-start.1
  132.2 48.2 %collective-permute-done.7 = bf16[1568,768]{1,0:T(8,128)(2,1)} collective-permute-done((bf16[1568,768]{1,0:T(8,128)(2,1)}, bf16[1568,768]{1,0:T(8,128)(2,1)}, u32[]{:S(2)}, u32[]{:S(2)}) %collective-permute-start.7) | collective-permute-done | bytes 2408480 | tf_op jit(solution)/shard_map/ppermute | solution.py:621
  181.9 3.0 collective-permute-done
  186.7 9.6 %pad_maximum_fusion.x_ref = bf16[4,1568,768]{2,1,0:T(8,128)(2,1)} fusion(bf16[1,1568,768]{2,1,0:T(8,128)(2,1)} %bitcast.10, bf16[1,1568,768]{2,1,0:T(8,128)(2,1)} %bitcast.9, bf16[1,1568,768]{2,1,0:T(8,128)(2,1)} %bitcast.8, bf16[1,1568,768]{2,1,0:T(8,128)(2,1)} %bitcast.7), kind=kLoop, calls=%fused_computation | loop fusion | flops 14450688 | bytes 19267584 | tf_op jit(solution)/shard_map/stack | solution.py:673
  196.3 8.3 %pad_maximum_fusion.1.g_ref = bf16[4,1568,768]{2,1,0:T(8,128)(2,1)} fusion(bf16[1,1568,768]{2,1,0:T(8,128)(2,1)} %bitcast.14, bf16[1,1568,768]{2,1,0:T(8,128)(2,1)} %bitcast.13, bf16[1,1568,768]{2,1,0:T(8,128)(2,1)} %bitcast.12, bf16[1,1568,768]{2,1,0:T(8,128)(2,1)S(1)} %bitcast.40), kind=kLoop, calls=%fused_computation.1 | loop fusion | flops 14450688 | bytes 19267584 | tf_op jit(solution)/shard_map/stack | solution.py:668
  204.7 86.4 %experts.1 = (bf16[4,1568,768]{2,1,0:T(8,128)(2,1)}, bf16[4,1568,768]{2,1,0:T(8,128)(2,1)}, bf16[3,768,768]{2,1,0:T(8,128)(2,1)}, bf16[3,768,768]{2,1,0:T(8,128)(2,1)}) custom-call(s32[16]{0:T(128)} %pad_add_fusion.1.offs_ref, s32[6]{0:T(128)} %reshape.41.hosts_ref, bf16[4,1568,768]{2,1,0:T(8,128)(2,1)} %pad_maximum_fusion.x_ref, ...), custom_call_target="tpu_custom_call" | custom-call | flops 44392513536 | bytes 38535168 | tf_op jit(solution)/shard_map/experts/pallas_call | solution.py:384
  291.1 6.3 slice_bitcast_fusion
  298.1 4.3 collective-permute-done.13
  302.4 4.4 fusion
  309.7 51.8 %collective-permute-done.14.c_ref = bf16[1568,768]{1,0:T(8,128)(2,1)} collective-permute-done((bf16[1568,768]{1,0:T(8,128)(2,1)}, bf16[1568,768]{1,0:T(8,128)(2,1)}, u32[]{:S(2)}, u32[]{:S(2)}) %collective-permute-start.14) | collective-permute-done | bytes 2408480 | tf_op jit(solution)/shard_map/ppermute | solution.py:621
  361.5 23.0 %back.1 = (f32[1566,768]{1,0:T(8,128)}, bf16[1584,768]{1,0:T(8,128)(2,1)}, f32[768,768]{1,0:T(8,128)}, f32[1,768]{1,0:T(1,128)}) custom-call(bf16[1568,768]{1,0:T(8,128)(2,1)} %get-tuple-element.48.a_ref, bf16[1568,768]{1,0:T(8,128)(2,1)} %collective-permute-done.12.b_ref, bf16[1568,768]{1,0:T(8,128)(2,1)} %collective-permute-done.14.c_ref, ...), custom_call_target="tpu_custom_call" | custom-call | flops 7552106496 | bytes 29196288 | tf_op jit(solution)/shard_map/back/pallas_call | solution.py:457
  384.5 38.8 %attend_back.1.gq_ref = bf16[1584,2304]{1,0:T(8,128)(2,1)} custom-call(s32[6]{0:T(128)} %len_ref.3, bf16[1584,2304]{1,0:T(8,128)(2,1)} %qkv.1.qkv_ref, bf16[1584,768]{1,0:T(8,128)(2,1)} %get-tuple-element.32.gctx_ref, f32[6,16,384]{2,1,0:T(8,128)} %get-tuple-element.33.lse_ref), custom_call_target="tpu_custom_call" | custom-call | flops 10192158720 | bytes 17031168 | tf_op jit(solution)/shard_map/attend_back/pallas_call | solution.py:559
  423.4 25.1 %first_back.1 = (f32[1566,768]{1,0:T(8,128)}, f32[768,2304]{1,0:T(8,128)}, f32[1,768]{1,0:T(1,128)}) custom-call(bf16[1566,768]{1,0:T(8,128)(2,1)} %tok_ref.5, f32[1,768]{1,0:T(1,128)} %reshape.42.gain_ref, bf16[1584,2304]{1,0:T(8,128)(2,1)} %attend_back.1.gq_ref, bf16[768,2304]{1,0:T(8,128)(2,1)} %w_ref.7, f32[1566,768]{1,0:T(8,128)} %get-tuple-element.34.gm_ref), custom_call_target="tpu_custom_call" | custom-call | flops 11211374592 | bytes 19464192 | tf_op jit(solution)/shard_map/first_back/pallas_call | solution.py:597
  448.5 5.3 convert_element_type.50
  456.2 5.8 slice_bitcast_fusion.3
  462.6 6.8 collective-permute-done.10
  469.4 3.8 fusion.1
  477.1 92.8 %psum.21 = f32[2,768]{1,0:T(2,128)S(1)} all-reduce(f32[2,768]{1,0:T(2,128)S(1)} %pad_maximum_fusion.2), channel_id=1, replica_groups=mesh['batch'=8,'ffn'=4] {'batch','ffn'}, use_global_device_ids=true, to_apply=%region_3.4 | all-reduce | flops 1536 | bytes 12288 | tf_op jit(solution)/shard_map/psum | solution.py:699
  570.5 11.2 %finish.1 = f32[1566,768]{1,0:T(8,128)} custom-call(bf16[1568,768]{1,0:T(8,128)(2,1)} %get-tuple-element.51.a_ref, bf16[1568,768]{1,0:T(8,128)(2,1)} %collective-permute-done.9.b_ref, bf16[1568,768]{1,0:T(8,128)(2,1)} %collective-permute-done.11.c_ref, s32[1584,1]{1,0:T(8,128)} %copy.27.pos_ref, f32[1566,768]{1,0:T(8,128)} %get-tuple-element.30.mid_ref), custom_call_target="tpu_custom_call" | custom-call | flops 3814981632 | bytes 17031168 | tf_op jit(solution)/shard_map/finish/pallas_call | solution.py:496
  581.7 28.6 %all-reduce.4.cloned.1.call-done = (bf16[768,2304]{1,0:T(8,128)(2,1)}, bf16[768,768]{1,0:T(8,128)(2,1)}) async-done(((bf16[768,2304]{1,0:T(8,128)(2,1)}, bf16[768,768]{1,0:T(8,128)(2,1)}), (bf16[768,2304]{1,0:T(8,128)(2,1)}, bf16[768,768]{1,0:T(8,128)(2,1)})) %all-reduce.4.cloned.1.call-update) | async-done | bytes 4718608 | tf_op jit(solution)/shard_map/psum | solution.py:696
  610.3 5.6 convert_element_type.51
  617.4 59.2 %all-gather.11.cloned.1.call-done = bf16[3,768,768]{2,1,0:T(8,128)(2,1)} async-done(((bf16[3,96,768]{2,1,0:T(8,128)(2,1)}), bf16[3,768,768]{2,1,0:T(8,128)(2,1)}) %all-gather.11.cloned.1.call-update) | async-done | bytes 3538960 | tf_op jit(solution)/shard_map/all_gather | solution.py:691
  676.6 2.9 dynamic-slice_convert_fusion
  679.6 63.2 %all-gather.9.cloned.1.call-done = bf16[3,768,768]{2,1,0:T(8,128)(2,1)} async-done(((bf16[3,96,768]{2,1,0:T(8,128)(2,1)}), bf16[3,768,768]{2,1,0:T(8,128)(2,1)}) %all-gather.9.cloned.1.call-update) | async-done | bytes 3538960 | tf_op jit(solution)/shard_map/all_gather | solution.py:691
  742.8 2.8 dynamic-slice_convert_fusion.1
  (89 shorter events, 22.4 us)
Async XLA Ops:
  7.2 7.1 copy-start.7
  7.2 197.5 %all-gather.5.cloned.1.call-start = ((), (), s32[]{:S(2)}) async-start(), calls=%async_computation.2 | async-start | bytes 5308416 | tf_op jit(solution)/shard_map/all_gather | solution.py:659
  12.2 192.5 %all-gather.7.cloned.1.call-start = ((), (), s32[]{:S(2)}) async-start(), calls=%async_computation.3 | async-start | bytes 5308416 | tf_op jit(solution)/shard_map/all_gather | solution.py:660
  14.2 440.8 %reduce-scatter.5.cloned.1.call-start = ((), (), s32[]{:S(2)}) async-start(), calls=%async_computation.6 | async-start | bytes 3981312 | tf_op jit(solution)/shard_map/reduce_scatter | solution.py:690
  14.8 11.0 %copy-start.5 = (s32[1566,1]{0,1:T(1,128)S(1)}, s32[1566,1]{0,1:T(1,128)}, u32[]{:S(2)}) copy-start(s32[1566,1]{0,1:T(1,128)} %param.13) | copy-start | bytes 18796
  14.8 13.5 %copy-start.8 = (f32[768]{0:T(1024)S(1)}, f32[768]{0:T(1024)}, u32[]{:S(2)}) copy-start(f32[768]{0:T(1024)} %param.18) | copy-start | bytes 9220
  73.2 56.9 %copy-start.12 = (s32[1,128]{1,0:T(1,128)S(1)}, s32[1,128]{1,0:T(1,128)}, u32[]{:S(2)}) copy-start(s32[1,128]{1,0:T(1,128)} %get-tuple-element.25) | copy-start | bytes 1540
  73.2 107.2 %copy-start.11 = (s32[8]{0:T(128)S(1)}, s32[8]{0:T(128)}, u32[]{:S(2)}) copy-start(s32[8]{0:T(128)} %gm_ref.1) | copy-start | bytes 100
  73.2 56.4 %collective-permute-start.4 = (bf16[1568,768]{1,0:T(8,128)(2,1)}, bf16[1568,768]{1,0:T(8,128)(2,1)}, u32[]{:S(2)}, u32[]{:S(2)}) collective-permute-start(bf16[1568,768]{1,0:T(8,128)(2,1)} %get-tuple-element.28), channel_id=1, source_target_pairs={{0,2},{1,3},{2,0},{3,1},{4,6},{5,7},{6,4},{7,5},{8,10},{9,11},{10,... | collective-permute-start | bytes 7225352 | tf_op jit(solution)/shard_map/ppermute | solution.py:621
  83.8 96.6 %collective-permute-start.7 = (bf16[1568,768]{1,0:T(8,128)(2,1)}, bf16[1568,768]{1,0:T(8,128)(2,1)}, u32[]{:S(2)}, u32[]{:S(2)}) collective-permute-start(bf16[1568,768]{1,0:T(8,128)(2,1)} %sort_rows.1), channel_id=1, source_target_pairs={{0,2},{1,3},{2,0},{3,1},{4,6},{5,7},{6,4},{7,5},{8,10},{9,11},{10,... | collective-permute-start | bytes 7225352 | tf_op jit(solution)/shard_map/ppermute | solution.py:621
  83.8 102.9 %collective-permute-start.3 = (bf16[1568,768]{1,0:T(8,128)(2,1)}, bf16[1568,768]{1,0:T(8,128)(2,1)}, u32[]{:S(2)}, u32[]{:S(2)}) collective-permute-start(bf16[1568,768]{1,0:T(8,128)(2,1)} %get-tuple-element.28), channel_id=1, source_target_pairs={{0,1},{1,0},{2,3},{3,2},{4,5},{5,4},{6,7},{7,6},{8,9},{9,8},{10,11... | collective-permute-start | bytes 7225352 | tf_op jit(solution)/shard_map/ppermute | solution.py:621
  129.6 57.1 %collective-permute-start.5 = (bf16[1568,768]{1,0:T(8,128)(2,1)}, bf16[1568,768]{1,0:T(8,128)(2,1)}, u32[]{:S(2)}, u32[]{:S(2)}) collective-permute-start(bf16[1568,768]{1,0:T(8,128)(2,1)} %collective-permute-done.4), channel_id=1, source_target_pairs={{0,1},{1,0},{2,3},{3,2},{4,5},{5,4},{6,7},{7,6},{8,9},{9,8},{10,11... | collective-permute-start | bytes 7225352 | tf_op jit(solution)/shard_map/ppermute | solution.py:621
  129.6 66.7 %collective-permute-start.6 = (bf16[1568,768]{1,0:T(8,128)(2,1)}, bf16[1568,768]{1,0:T(8,128)(2,1)}, u32[]{:S(2)}, u32[]{:S(2)}) collective-permute-start(bf16[1568,768]{1,0:T(8,128)(2,1)} %sort_rows.1), channel_id=1, source_target_pairs={{0,1},{1,0},{2,3},{3,2},{4,5},{5,4},{6,7},{7,6},{8,9},{9,8},{10,11... | collective-permute-start | bytes 7225352 | tf_op jit(solution)/shard_map/ppermute | solution.py:621
  130.1 51.3 %collective-permute-start.1 = (s32[1,128]{1,0:T(1,128)S(1)}, s32[1,128]{1,0:T(1,128)S(1)}, u32[]{:S(2)}, u32[]{:S(2)}) collective-permute-start(s32[1,128]{1,0:T(1,128)S(1)} %copy-done.12), channel_id=1, source_target_pairs={{0,2},{1,3},{2,0},{3,1},{4,6},{5,7},{6,4},{7,5},{8,10},{9,11},{10,... | collective-permute-start | bytes 1544 | tf_op jit(solution)/shard_map/ppermute | solution.py:621
  180.4 15.9 %collective-permute-start.8 = (bf16[1568,768]{1,0:T(8,128)(2,1)}, bf16[1568,768]{1,0:T(8,128)(2,1)}, u32[]{:S(2)}, u32[]{:S(2)}) collective-permute-start(bf16[1568,768]{1,0:T(8,128)(2,1)} %collective-permute-done.7), channel_id=1, source_target_pairs={{0,1},{1,0},{2,3},{3,2},{4,5},{5,4},{6,7},{7,6},{8,9},{9,8},{10,11... | collective-permute-start | bytes 7225352 | tf_op jit(solution)/shard_map/ppermute | solution.py:621
  181.4 3.5 collective-permute-start
  184.9 1.1 collective-permute-start.2
  186.7 9.6 %copy-start.2 = (bf16[1568,768]{1,0:T(8,128)(2,1)S(1)}, bf16[1568,768]{1,0:T(8,128)(2,1)}, u32[]{:S(2)}) copy-start(bf16[1568,768]{1,0:T(8,128)(2,1)} %sort_rows.1) | copy-start | bytes 7225348
  291.1 164.5 %reduce-scatter.3.cloned.1.call-start = ((), (), s32[]{:S(2)}) async-start(), calls=%async_computation.4 | async-start | bytes 3981312 | tf_op jit(solution)/shard_map/reduce_scatter | solution.py:690
  297.4 4.9 collective-permute-start.13
  297.6 312.6 %all-reduce.4.cloned.1.call-start = ((), (), s32[]{:S(2)}) async-start(), calls=%async_computation.8 | async-start | bytes 9437184 | tf_op jit(solution)/shard_map/psum | solution.py:696
  297.7 10.8 %copy-start.6 = (s32[1,1664]{1,0:T(1,128)S(1)}, s32[1,1664]{1,0:T(1,128)}, u32[]{:S(2)}) copy-start(s32[1,1664]{1,0:T(1,128)} %get-tuple-element.27.pos_ref) | copy-start | bytes 19972
  297.7 12.0 %collective-permute-start.12 = (bf16[1568,768]{1,0:T(8,128)(2,1)}, bf16[1568,768]{1,0:T(8,128)(2,1)}, u32[]{:S(2)}, u32[]{:S(2)}) collective-permute-start(bf16[1568,768]{1,0:T(8,128)(2,1)} %get-tuple-element.47), channel_id=1, source_target_pairs={{0,1},{1,0},{2,3},{3,2},{4,5},{5,4},{6,7},{7,6},{8,9},{9,8},{10,11... | collective-permute-start | bytes 7225352 | tf_op jit(solution)/shard_map/ppermute | solution.py:621
  306.8 54.8 %collective-permute-start.14 = (bf16[1568,768]{1,0:T(8,128)(2,1)}, bf16[1568,768]{1,0:T(8,128)(2,1)}, u32[]{:S(2)}, u32[]{:S(2)}) collective-permute-start(bf16[1568,768]{1,0:T(8,128)(2,1)} %fusion), channel_id=1, source_target_pairs={{0,2},{1,3},{2,0},{3,1},{4,6},{5,7},{6,4},{7,5},{8,10},{9,11},{10,... | collective-permute-start | bytes 7225352 | tf_op jit(solution)/shard_map/ppermute | solution.py:621
  454.9 221.7 %all-gather.11.cloned.1.call-start = ((), (), s32[]{:S(2)}) async-start(), calls=%async_computation.7 | async-start | bytes 3981312 | tf_op jit(solution)/shard_map/all_gather | solution.py:691
  455.5 287.3 %all-gather.9.cloned.1.call-start = ((), (), s32[]{:S(2)}) async-start(), calls=%async_computation.5 | async-start | bytes 3981312 | tf_op jit(solution)/shard_map/all_gather | solution.py:691
  462.1 7.3 collective-permute-start.10
  462.1 15.0 %copy-start.9 = (f32[1,768]{1,0:T(1,128)S(1)}, f32[1,768]{1,0:T(1,128)}, u32[]{:S(2)}) copy-start(f32[1,768]{1,0:T(1,128)} %get-tuple-element.37) | copy-start | bytes 9220
  462.1 15.0 %copy-start.10 = (f32[1,768]{1,0:T(1,128)S(1)}, f32[1,768]{1,0:T(1,128)}, u32[]{:S(2)}) copy-start(f32[1,768]{1,0:T(1,128)} %get-tuple-element.36) | copy-start | bytes 9220
  462.1 108.4 %collective-permute-start.9 = (bf16[1568,768]{1,0:T(8,128)(2,1)}, bf16[1568,768]{1,0:T(8,128)(2,1)}, u32[]{:S(2)}, u32[]{:S(2)}) collective-permute-start(bf16[1568,768]{1,0:T(8,128)(2,1)} %get-tuple-element.50), channel_id=1, source_target_pairs={{0,1},{1,0},{2,3},{3,2},{4,5},{5,4},{6,7},{7,6},{8,9},{9,8},{10,11... | collective-permute-start | bytes 7225352 | tf_op jit(solution)/shard_map/ppermute | solution.py:621
  473.2 97.3 %collective-permute-start.11 = (bf16[1568,768]{1,0:T(8,128)(2,1)}, bf16[1568,768]{1,0:T(8,128)(2,1)}, u32[]{:S(2)}, u32[]{:S(2)}) collective-permute-start(bf16[1568,768]{1,0:T(8,128)(2,1)} %fusion.1), channel_id=1, source_target_pairs={{0,2},{1,3},{2,0},{3,1},{4,6},{5,7},{6,4},{7,5},{8,10},{9,11},{10,... | collective-permute-start | bytes 7225352 | tf_op jit(solution)/shard_map/ppermute | solution.py:621
  676.6 69.0 %copy-start.1 = (bf16[1,768,768]{2,1,0:T(8,128)(2,1)S(1)}, bf16[1,768,768]{2,1,0:T(8,128)(2,1)}, u32[]{:S(2)}) copy-start(bf16[1,768,768]{2,1,0:T(8,128)(2,1)} %param.19) | copy-start | bytes 3538948
  (3 other events, 15.0 us)
Sparse Core Ops, SparseCore 0:
  12.3 82.5 all-gather.4
  97.7 78.0 all-gather.6
  291.2 80.4 reduce-scatter.4
  375.2 78.7 reduce-scatter.2
  460.2 150.0 all-reduce.3
  612.6 64.0 all-gather.10
  679.1 63.6 all-gather.8

commit v2 on v1

--- a/solution.py
+++ b/solution.py
@@ -17,7 +17,7 @@
 SEQ_LEN = 261
 TOK_DEV = 1566
 ROWS = 1584
-SORTED = 1568
+SORTED = 1616
 WIN = 288
 TILE = 528
 LANES = 1664
@@ -87,7 +87,7 @@
     totals = [jnp.sum(hot[e : e + 1, :], axis=1, keepdims=True) for e in range(EXPERTS)]
     starts = [jnp.zeros((1, 1), I32)]
     for e in range(EXPERTS):
-        starts.append(starts[-1] + totals[e])
+        starts.append(starts[-1] + (totals[e] + 15) // 16 * 16)
     pos = jnp.zeros((1, LANES), I32)
     for e in range(EXPERTS):
         pos = pos + jnp.where(hot[e : e + 1, :] > 0, count[e : e + 1, :] - 1 + starts[e], 0)
@@ -120,15 +120,17 @@
     )(group_map, routes_row)
 
 
-SORT_TILE = 224
+SORT_TILES = (336, 336, 336, 336, 272)
 
 
 def sort_into(out_ref, rows_ref, pos_ref):
     pos = pos_ref[0:1, 0:ROWS]
-    for i in range(SORTED // SORT_TILE):
-        want = i * SORT_TILE + lax.broadcasted_iota(I32, (SORT_TILE, ROWS), 0)
+    top = 0
+    for size in SORT_TILES:
+        want = top + lax.broadcasted_iota(I32, (size, ROWS), 0)
         hot = jnp.where(pos == want, 1.0, 0.0).astype(BF16)
-        out_ref[i * SORT_TILE : (i + 1) * SORT_TILE, :] = dot(hot, rows_ref[...]).astype(BF16)
+        out_ref[top : top + size, :] = dot(hot, rows_ref[...]).astype(BF16)
+        top += size
 
 
 def sort_kernel(rows_ref, pos_ref, out_ref, held):
@@ -280,132 +282,173 @@
     return u * below, below + u * density
 
 
-def expert_kernel(
-    n_src,
-    offs_ref,
-    hosts_ref,
-    x_ref,
-    g_ref,
-    wi_hbm,
-    wb_hbm,
-    out_ref,
-    gx_ref,
-    dwi_hbm,
-    dwb_hbm,
-    wi,
-    wb,
-    acc_i,
-    acc_b,
-    sems,
-):
-    src = pl.program_id(0)
-
-    def weight_copies():
-        for e in range(EXPERTS):
-            for p in range(2):
-                host = hosts_ref[e * 2 + p]
-                part = pl.ds(p * HALF, HALF)
-                yield pltpu.make_async_copy(
-                    wi_hbm.at[host], wi.at[e, :, part], sems.at[e * 4 + p * 2]
+MERGED = 2 * SORTED + 256
+
+
+def expert_kernel(n_slots, carried, offs_ref, hosts_ref, *refs):
+    refs = list(refs)
+
+    def take(count):
+        head = refs[:count]
+        del refs[:count]
+        return head
+
+    xs, gs = take(2), take(2)
+    wi_hbm, wb_hbm = take(1), take(n_slots)
+    before = take(2) if carried else None
+    outs, gxs = take(2), take(2)
+    dwi_ref, dwb_ref = take(2)
+    xm, gm, wi, wb, acc_i, acc_b, sems = refs
+    expert = pl.program_id(0)
+    slot = expert % 2
+
+    def weight_copies(e, buffer, start):
+        for p in range(2):
+            host = hosts_ref[e * 4 + p]
+            part = pl.ds(p * HALF, HALF)
+            copy = pltpu.make_async_copy(
+                wi_hbm[0].at[host], wi.at[buffer, :, part], sems.at[buffer, p, 0]
+            )
+            if start:
+                copy.start()
+            else:
+                copy.wait()
+            if not start or n_slots == 1:
+                source = wb_hbm[0].at[host if n_slots == 1 else 0]
+                copy = pltpu.make_async_copy(
+                    source, wb.at[buffer, part, :], sems.at[buffer, p, 1]
                 )
-                yield pltpu.make_async_copy(
-                    wb_hbm.at[host], wb.at[e, part, :], sems.at[e * 4 + p * 2 + 1]
-                )
-
-    @pl.when(src == 0)
+                if start:
+                    copy.start()
+                else:
+                    copy.wait()
+            else:
+                for j in range(n_slots):
+
+                    slot = hosts_ref[e * 4 + 2 + p]
+
+                    @pl.when(slot // 2 == j)
+                    def _(j=j, slot=slot):
+                        pltpu.make_async_copy(
+                            wb_hbm[j].at[slot % 2], wb.at[buffer, part, :], sems.at[buffer, p, 1]
+                        ).start()
+
+    @pl.when(expert == 0)
     def _():
-        for copy in weight_copies():
-            copy.start()
+        weight_copies(0, 0, True)
+
+    @pl.when(expert + 1 < EXPERTS)
+    def _():
+        weight_copies(expert + 1, 1 - slot, True)
+
+    def blocks(count, act):
+        @pl.loop(0, count)
+        def _(i):
+            act(pl.multiple_of(i * 16, 16))
+
+    @pl.when(expert == 0)
+    def _():
+        for s in range(2):
+            live = pl.multiple_of(offs_ref[s * 4 + EXPERTS], 16)
+
+            def clear(at, s=s, live=live):
+                rows = pl.ds(pl.multiple_of(live + at, 16), 16)
+                outs[s][rows, :] = jnp.zeros((16, D), BF16)
+                gxs[s][rows, :] = jnp.zeros((16, D), BF16)
+
+            blocks((SORTED - live) // 16, clear)
+
+    if carried:
+        acc_i[...] = before[0][0].astype(F32)
+        acc_b[...] = before[1][0].astype(F32)
+    else:
         acc_i[...] = jnp.zeros_like(acc_i)
         acc_b[...] = jnp.zeros_like(acc_b)
-        for copy in weight_copies():
-            copy.wait()
-
-    tail = slice(SORTED - 16, SORTED)
-    out_ref[0, tail, :] = jnp.zeros((16, D), BF16)
-    gx_ref[0, tail, :] = jnp.zeros((16, D), BF16)
-
-    def visit(e, low, first, last, size):
-        start = pl.multiple_of(jnp.minimum(low, SORTED - size), 16)
-        rows = pl.ds(start, size)
-        row = start + lax.broadcasted_iota(I32, (size, 1), 0)
-        mine = (row >= jnp.maximum(first, low)) & (row < last)
-        x = jnp.where(mine, x_ref[0, rows, :], jnp.zeros((), BF16))
-        g = jnp.where(mine, g_ref[0, rows, :], jnp.zeros((), BF16))
-        inner = dot(x, wi[e])
+
+    places = []
+    total = jnp.int32(0)
+    for s in range(2):
+        first = pl.multiple_of(offs_ref[s * 4 + expert], 16)
+        size = offs_ref[s * 4 + expert + 1] - first
+        places.append((first, total, size // 16))
+
+        def gather(at, s=s, first=first, total=total):
+            here = pl.ds(pl.multiple_of(first + at, 16), 16)
+            there = pl.ds(pl.multiple_of(total + at, 16), 16)
+            xm[there, :] = xs[s][here, :]
+            gm[there, :] = gs[s][here, :]
+
+        blocks(size // 16, gather)
+        total = total + size
+    span = pl.multiple_of(total, 16)
+
+    def blank(at):
+        there = pl.ds(pl.multiple_of(span + at, 16), 16)
+        xm[there, :] = jnp.zeros((16, D), BF16)
+        gm[there, :] = jnp.zeros((16, D), BF16)
+
+    blocks((256 - span % 256) // 16, blank)
+    weight_copies(expert, slot, False)
+    w_in, w_back = wi.at[slot], wb.at[slot]
+
+    @pl.loop(0, (span + 255) // 256)
+    def _(i):
+        rows = pl.ds(pl.multiple_of(i * 256, 256), 256)
+        x, g = xm[rows, :], gm[rows, :]
+        inner = dot(x, w_in[...])
         hidden, slope = gelu_both(inner)
         hidden = hidden.astype(BF16)
-        branch = dot(hidden, wb[e]).astype(BF16)
-        grad_hidden = dot(g, wb[e], CONTRACT_LANES).astype(BF16)
+        grad_hidden = dot(g, w_back[...], CONTRACT_LANES).astype(BF16)
         grad_inner = (grad_hidden.astype(F32) * slope).astype(BF16)
-        grad_x = dot(grad_inner, wi[e], CONTRACT_LANES).astype(BF16)
-        out_ref[0, rows, :] = jnp.where(mine, branch, out_ref[0, rows, :])
-        gx_ref[0, rows, :] = jnp.where(mine, grad_x, gx_ref[0, rows, :])
-        acc_b[e] += dot(hidden, g, CONTRACT_ROWS)
-        acc_i[e] += dot(x, grad_inner, CONTRACT_ROWS)
-
-    for e in range(EXPERTS):
-        first = offs_ref[src * 4 + e]
-        last = offs_ref[src * 4 + e + 1]
-        base = first // 16 * 16
-        span = last - base
-        span = jnp.where(last > first, span, 0)
-        big = span // 256
-
-        @pl.loop(0, big)
-        def _(i):
-            visit(e, base + i * 256, first, last, 256)
-
-        rest = base + big * 256
-        small = (span - big * 256 + 127) // 128
-
-        @pl.loop(0, small)
-        def _(i):
-            visit(e, rest + i * 128, first, last, 128)
-
-    @pl.when(src == n_src - 1)
-    def _():
-        copies = []
-        for e in range(EXPERTS):
-            wi[e] = acc_i[e].astype(BF16)
-            wb[e] = acc_b[e].astype(BF16)
-            copies.append(pltpu.make_async_copy(wi.at[e], dwi_hbm.at[e], sems.at[e * 2]))
-            copies.append(pltpu.make_async_copy(wb.at[e], dwb_hbm.at[e], sems.at[e * 2 + 1]))
-            copies[-2].start()
-            copies[-1].start()
-        for copy in copies:
-            copy.wait()
-
-
-def experts(offs, hosts, x, g, wi, wb):
-    n_src = x.shape[0]
-    block = pl.BlockSpec((1, SORTED, D), lambda s, *_: (s, 0, 0))
+        xm[rows, :] = dot(hidden, w_back[...]).astype(BF16)
+        gm[rows, :] = dot(grad_inner, w_in[...], CONTRACT_LANES).astype(BF16)
+        acc_b[...] += dot(hidden, g, CONTRACT_ROWS)
+        acc_i[...] += dot(x, grad_inner, CONTRACT_ROWS)
+
+    dwi_ref[0] = acc_i[...].astype(BF16)
+    dwb_ref[0] = acc_b[...].astype(BF16)
+    for s in range(2):
+        first, base, count = places[s]
+
+        def hand_back(at, s=s, first=first, base=base):
+            here = pl.ds(pl.multiple_of(first + at, 16), 16)
+            there = pl.ds(pl.multiple_of(base + at, 16), 16)
+            outs[s][here, :] = xm[there, :]
+            gxs[s][here, :] = gm[there, :]
+
+        blocks(count, hand_back)
+
+
+def experts(offs, hosts, xs, gs, wi, wb, before=None):
+    whole = once((SORTED, D))
     any_space = pl.BlockSpec(memory_space=pl.ANY)
-    return pl.pallas_call(
-        functools.partial(expert_kernel, n_src),
+    weight = pl.BlockSpec((1, D, FF_DEV), lambda e, *_: (e, 0, 0))
+    carried = before is not None
+    n_slots = len(wb)
+    rows = jax.ShapeDtypeStruct((SORTED, D), BF16)
+    grad = jax.ShapeDtypeStruct((EXPERTS, D, FF_DEV), BF16)
+    return pl.pallas_call(
+        functools.partial(expert_kernel, n_slots, carried),
         grid_spec=pltpu.PrefetchScalarGridSpec(
             num_scalar_prefetch=2,
-            grid=(n_src,),
-            in_specs=[block, block, any_space, any_space],
-            out_specs=[block, block, any_space, any_space],
+            grid=(EXPERTS,),
+            in_specs=[whole] * 4 + [any_space] * (1 + n_slots) + [weight] * (2 * carried),
+            out_specs=[whole] * 4 + [weight] * 2,
             scratch_shapes=[
-                pltpu.VMEM((EXPERTS, D, FF_DEV), BF16),
-                pltpu.VMEM((EXPERTS, FF_DEV, D), BF16),
-                pltpu.VMEM((EXPERTS, D, FF_DEV), F32),
-                pltpu.VMEM((EXPERTS, FF_DEV, D), F32),
-                pltpu.SemaphoreType.DMA((EXPERTS * 4,)),
+                pltpu.VMEM((MERGED, D), BF16),
+                pltpu.VMEM((MERGED, D), BF16),
+                pltpu.VMEM((2, D, FF_DEV), BF16),
+                pltpu.VMEM((2, FF_DEV, D), BF16),
+                pltpu.VMEM((D, FF_DEV), F32),
+                pltpu.VMEM((FF_DEV, D), F32),
+                pltpu.SemaphoreType.DMA((2, 2, 2)),
             ],
         ),
-        out_shape=(
-            jax.ShapeDtypeStruct((n_src, SORTED, D), BF16),
-            jax.ShapeDtypeStruct((n_src, SORTED, D), BF16),
-            jax.ShapeDtypeStruct((EXPERTS, D, FF_DEV), BF16),
-            jax.ShapeDtypeStruct((EXPERTS, FF_DEV, D), BF16),
-        ),
+        out_shape=(rows,) * 4 + (grad,) * 2,
         compiler_params=params(),
-        cost_estimate=cost(12 * n_src * SORTED * D * FF_DEV, 8 * n_src * SORTED * D),
+        cost_estimate=cost(24 * SORTED * D * FF_DEV, 16 * SORTED * D),
         name="experts",
-    )(offs, hosts, x, g, wi, wb)
+    )(offs, hosts, *xs, *gs, wi, *wb, *(before or ()))
 
 
 def unsort(pos_col, src):
@@ -429,6 +472,7 @@
     dw_ref,
     dg_ref,
     total,
+    acc,
 ):
     step = pl.program_id(0)
 
@@ -436,7 +480,7 @@
     def _():
         both = a_ref[...].astype(F32) + b_ref[...].astype(F32) + c_ref[...].astype(F32)
         total[...] = both.astype(BF16)
-        dw_ref[...] = jnp.zeros_like(dw_ref)
+        acc[...] = jnp.zeros_like(acc)
         dg_ref[...] = jnp.zeros_like(dg_ref)
 
     keep = row_mask(step * TILE, TILE, TOK_DEV)
@@ -448,7 +492,8 @@
     grad_middle = jnp.where(keep, cot_ref[...].astype(F32) + part, 0.0)
     gm_ref[...] = grad_middle
     low = grad_middle.astype(BF16)
-    dw_ref[...] += dot(ctx_ref[...], low, CONTRACT_ROWS)
+    acc[...] += dot(ctx_ref[...], low, CONTRACT_ROWS)
+    dw_ref[...] = acc[...].astype(BF16)
     gctx_ref[...] = dot(low, w_ref[...], CONTRACT_LANES).astype(BF16)
 
 
@@ -460,7 +505,7 @@
         out_shape=(
             jax.ShapeDtypeStruct((TOK_DEV, D), F32),
             jax.ShapeDtypeStruct((ROWS, D), BF16),
-            jax.ShapeDtypeStruct((D, D), F32),
+            jax.ShapeDtypeStruct((D, D), BF16),
             jax.ShapeDtypeStruct((1, D), F32),
         ),
         in_specs=[
@@ -475,7 +520,7 @@
             once((D, D)),
         ],
         out_specs=(tile, tile, full((D, D)), full((1, D))),
-        scratch_shapes=[pltpu.VMEM((SORTED, D), BF16)],
+        scratch_shapes=[pltpu.VMEM((SORTED, D), BF16), pltpu.VMEM((D, D), F32)],
         compiler_params=params(),
         cost_estimate=cost(2 * ROWS * D * (SORTED + 2 * D), 24 * ROWS * D),
         name="back",
@@ -573,12 +618,12 @@
     )(lengths, qkv, gctx, lse)
 
 
-def first_back_kernel(tok_ref, gain_ref, gq_ref, w_ref, gm_ref, ig_ref, dw_ref, dg_ref):
+def first_back_kernel(tok_ref, gain_ref, gq_ref, w_ref, gm_ref, ig_ref, dw_ref, dg_ref, acc):
     step = pl.program_id(0)
 
     @pl.when(step == 0)
     def _():
-        dw_ref[...] = jnp.zeros_like(dw_ref)
+        acc[...] = jnp.zeros_like(acc)
         dg_ref[...] = jnp.zeros_like(dg_ref)
 
     keep = row_mask(step * TILE, TILE, TOK_DEV)
@@ -586,7 +631,12 @@
     normal, inverse = norm_parts(tokens)
     normed = (normal * gain_ref[...]).astype(BF16)
     grad_qkv = gq_ref[...]
-    dw_ref[...] += dot(normed, grad_qkv, CONTRACT_ROWS)
+    acc[...] += dot(normed, grad_qkv, CONTRACT_ROWS)
+
+    @pl.when(step == ROWS // TILE - 1)
+    def _():
+        dw_ref[...] = acc[...].astype(BF16)
+
     grad_normed = dot(grad_qkv, w_ref[...], CONTRACT_LANES)
     dg_ref[...] += jnp.sum(grad_normed * normal, axis=0, keepdims=True)
     ig_ref[...] = gm_ref[...] + norm_pull(grad_normed, gain_ref[...], normal, inverse)
@@ -599,7 +649,7 @@
         grid=(ROWS // TILE,),
         out_shape=(
             jax.ShapeDtypeStruct((TOK_DEV, D), F32),
-            jax.ShapeDtypeStruct((D, 3 * D), F32),
+            jax.ShapeDtypeStruct((D, 3 * D), BF16),
             jax.ShapeDtypeStruct((1, D), F32),
         ),
         in_specs=[
@@ -610,6 +660,7 @@
             tile,
         ],
         out_specs=(tile, full((D, 3 * D)), full((1, D))),
+        scratch_shapes=[pltpu.VMEM((D, 3 * D), F32)],
         compiler_params=params(),
         cost_estimate=cost(4 * ROWS * D * 3 * D, 16 * ROWS * D),
         name="first_back",
@@ -625,6 +676,234 @@
     near = swap(rows, 1)
     far = swap(rows, 2)
     return [rows, near, far, swap(far, 1)]
+
+
+def cross(rows, bits):
+    return lax.ppermute(rows, "batch", [(b, b ^ bits) for b in range(8)])
+
+
+def tie(value, *others):
+    return lax.optimization_barrier((value, *others))[0]
+
+
+CHUNK = D // 8
+
+
+Z_GROUPS = [[0, 2, 4, 6], [1, 3, 5, 7]]
+
+
+def deliver_kernel(gm_ref, in_ref, back_ref, out_ref):
+    for b in range(8):
+        e = gm_ref[b]
+        out_ref[b, 0] = in_ref[e]
+        total = sum(back_ref[e, z].astype(F32) for z in range(4))
+        out_ref[b, 1] = total.astype(BF16)
+
+
+def deliver(grad_in, grad_back, group_map):
+    vmem = pl.BlockSpec(memory_space=pltpu.VMEM)
+    return pl.pallas_call(
+        deliver_kernel,
+        out_shape=jax.ShapeDtypeStruct((8, 2, CHUNK, D), BF16),
+        in_specs=[pl.BlockSpec(memory_space=pltpu.SMEM), vmem, vmem],
+        out_specs=vmem,
+        compiler_params=params(),
+        cost_estimate=cost(0, 6 << 20),
+        name="deliver",
+    )(group_map, grad_in, grad_back)
+
+
+def cross_y(dwb, own):
+    y = own % 2
+    cut = dwb.reshape(EXPERTS, 4, 2, CHUNK, D)
+    there = cross(lax.dynamic_index_in_dim(cut, 1 - y, 2, keepdims=False), 1)
+    mine = lax.dynamic_index_in_dim(cut, y, 2, keepdims=False)
+    return (mine.astype(F32) + there.astype(F32)).astype(BF16)
+
+
+def cross_z(rows):
+    return lax.all_to_all(
+        rows, "batch", split_axis=1, concat_axis=1, axis_index_groups=Z_GROUPS, tiled=True
+    )
+
+
+AXES = ("x", "y", "z")
+ORDERS = (("x", "y", "z"), ("y", "z", "x"), ("z", "x", "y"))
+WIDE = 4 * D
+COLOUR = WIDE // 3
+QUARTER = COLOUR // 4
+GAIN_ROWS = 8
+
+
+def total_kernel(
+    qkv_ref, proj_ref, gain_ref, out_ref, gain_out_ref, near, held, came, gain_in, send_sems, recv_sems
+):
+    batch, ffn = lax.axis_index("batch"), lax.axis_index("ffn")
+    z, y, x, c = batch // 2, batch % 2, ffn // 2, ffn % 2
+    place = {"x": x, "y": y, "z": z}
+
+    def peer(axis, k=1):
+        if axis == "c":
+            return (batch, ffn ^ 1)
+        if axis == "x":
+            return (batch, ffn ^ 2)
+        if axis == "y":
+            return (batch ^ 1, ffn)
+        return (batch ^ (2 * k), ffn)
+
+    peers = [peer("c"), peer("x"), peer("y")] + [peer("z", k) for k in (1, 2, 3)]
+    barrier = pltpu.get_barrier_semaphore()
+    for device in peers:
+        pl.semaphore_signal(barrier, inc=1, device_id=device, device_id_type=pl.DeviceIdType.MESH)
+    pl.semaphore_wait(barrier, len(peers))
+
+    used = [0]
+
+    def send(src, dst, device):
+        number = used[0]
+        used[0] += 1
+        copy = pltpu.make_async_remote_copy(
+            src_ref=src,
+            dst_ref=dst,
+            send_sem=send_sems.at[number],
+            recv_sem=recv_sems.at[number],
+            device_id=device,
+            device_id_type=pl.DeviceIdType.MESH,
+        )
+        copy.start()
+        return copy
+
+    give = pl.ds(pl.multiple_of((1 - c) * 384, 16), 384)
+    keep = pl.ds(pl.multiple_of(c * 384, 16), 384)
+    first = [
+        send(qkv_ref.at[give, :], near.at[:, 0 : 3 * D], peer("c")),
+        send(proj_ref.at[give, :], near.at[:, 3 * D : WIDE], peer("c")),
+        send(gain_ref, gain_in.at[0], peer("c")),
+    ]
+    for copy in first:
+        copy.wait()
+    held[:, 0 : 3 * D] = (
+        qkv_ref[keep, :].astype(F32) + near[:, 0 : 3 * D].astype(F32)
+    ).astype(BF16)
+    held[:, 3 * D : WIDE] = (
+        proj_ref[keep, :].astype(F32) + near[:, 3 * D : WIDE].astype(F32)
+    ).astype(BF16)
+    gain_out_ref[...] = gain_ref[...] + gain_in[0]
+
+    top = [0, 0, 0]
+    left = [COLOUR * i for i in range(3)]
+    rows, cols = [384] * 3, [COLOUR] * 3
+    gain_slot = 1
+    for step in range(3):
+        flying = []
+        for i in range(3):
+            axis = ORDERS[i][step]
+            if axis == "z":
+                for k in (1, 2, 3):
+                    there = pl.ds(pl.multiple_of(left[i] + (z ^ k) * QUARTER, 128), QUARTER)
+                    live = pl.ds(top[i], rows[i])
+                    flying.append(
+                        send(
+                            held.at[live, there],
+                            came.at[i, k - 1, 0 : rows[i], 0:QUARTER],
+                            peer("z", k),
+                        )
+                    )
+            else:
+                half = rows[i] // 2
+                there = pl.ds(pl.multiple_of(top[i] + (1 - place[axis]) * half, 16), half)
+                flying.append(
+                    send(
+                        held.at[there, pl.ds(left[i], cols[i])],
+                        came.at[i, 3 if axis == "x" else 4, 0:half, 0 : cols[i]],
+                        peer(axis),
+                    )
+                )
+        gain_axis = AXES[step]
+        if gain_axis == "z":
+            flying += [send(gain_out_ref, gain_in.at[gain_slot + k - 1], peer("z", k)) for k in (1, 2, 3)]
+        else:
+            flying.append(send(gain_out_ref, gain_in.at[gain_slot], peer(gain_axis)))
+        for copy in flying:
+            copy.wait()
+        for i in range(3):
+            axis = ORDERS[i][step]
+            if axis == "z":
+                left[i] = pl.multiple_of(left[i] + z * QUARTER, 128)
+                cols[i] = QUARTER
+                spots = (0, 1, 2)
+            else:
+                rows[i] = rows[i] // 2
+                top[i] = pl.multiple_of(top[i] + place[axis] * rows[i], 16)
+                spots = (3,) if axis == "x" else (4,)
+            spot = (pl.ds(top[i], rows[i]), pl.ds(left[i], cols[i]))
+            total = held[spot].astype(F32)
+            for number in spots:
+                total = total + came[i, number, 0 : rows[i], 0 : cols[i]].astype(F32)
+            held[spot] = total.astype(BF16)
+        if gain_axis == "z":
+            gain_out_ref[...] = (
+                (gain_out_ref[...] + gain_in[gain_slot])
+                + gain_in[gain_slot + 1]
+                + gain_in[gain_slot + 2]
+            )
+        else:
+            gain_out_ref[...] = gain_out_ref[...] + gain_in[gain_slot]
+            gain_slot += 1
+
+    base = c * 384
+    for i in range(3):
+        spot = (pl.ds(top[i], rows[i]), pl.ds(left[i], cols[i]))
+        out_ref[pl.ds(pl.multiple_of(base + top[i], 16), rows[i]), spot[1]] = held[spot]
+    for step in (2, 1, 0):
+        flying = []
+        for i in range(3):
+            axis = ORDERS[i][step]
+            mine = out_ref.at[
+                pl.ds(pl.multiple_of(base + top[i], 16), rows[i]), pl.ds(left[i], cols[i])
+            ]
+            for k in (1, 2, 3) if axis == "z" else (1,):
+                flying.append(send(mine, mine, peer(axis, k)))
+        for copy in flying:
+            copy.wait()
+        for i in range(3):
+            axis = ORDERS[i][step]
+            if axis == "z":
+                left[i] = COLOUR * i
+                cols[i] = COLOUR
+            else:
+                top[i] = top[i] - place[axis] * rows[i]
+                rows[i] = rows[i] * 2
+                if rows[i] == 384:
+                    top[i] = 0
+    mine = out_ref.at[pl.ds(pl.multiple_of(base, 16), 384), :]
+    send(mine, mine, peer("c")).wait()
+
+
+COPIES = 3 + 2 * (2 + 3 + 2 + 3 + 2 + 3) // 2 + 5 + 15 + 1
+
+
+def total_over_all(dw_qkv, dw_proj, gains):
+    vmem = pl.BlockSpec(memory_space=pltpu.VMEM)
+    return pl.pallas_call(
+        total_kernel,
+        out_shape=(
+            jax.ShapeDtypeStruct((D, WIDE), BF16),
+            jax.ShapeDtypeStruct((GAIN_ROWS, D), F32),
+        ),
+        in_specs=[vmem] * 3,
+        out_specs=(vmem, vmem),
+        scratch_shapes=[
+            pltpu.VMEM((384, WIDE), BF16),
+            pltpu.VMEM((384, WIDE), BF16),
+            pltpu.VMEM((3, 5, 384, COLOUR), BF16),
+            pltpu.VMEM((6, GAIN_ROWS, D), F32),
+            pltpu.SemaphoreType.DMA((COPIES,)),
+            pltpu.SemaphoreType.DMA((COPIES,)),
+        ],
+        compiler_params=params(collective_id=0, has_side_effects=True),
+        name="total",
+    )(dw_qkv, dw_proj, gains)
 
 
 def body(
@@ -656,47 +935,95 @@
 
     wi_part = lax.dynamic_slice(w_in[0], (0, part * HALF), (D, HALF))
     wb_part = lax.dynamic_slice(w_back[0], (part * HALF, 0), (HALF, D))
+    small = n_batch == 8
     wi_all = lax.all_gather(wi_part, "batch", axis=0)
-    wb_all = lax.all_gather(wb_part, "batch", axis=0)
+    if small:
+        column = jnp.stack([wb_part, cross(wb_part, 1)])
+        wb_all = [column] + [cross(column, 2 * k) for k in (1, 2, 3)]
+        slots = hosts ^ own
+    else:
+        wb_all = [lax.all_gather(wb_part, "batch", axis=0)]
+        slots = hosts
+    hosts = jnp.stack([hosts.reshape(EXPERTS, 2), slots.reshape(EXPERTS, 2)], axis=1).reshape(-1)
 
     routes_row = jnp.pad(routes.reshape(1, TOK_DEV), ((0, 0), (0, LANES - TOK_DEV)))
     pos, offs = route_rows(routes_row, group_map)
     pos_col = pos.reshape(LANES, 1)[0:ROWS]
-    offs_all = jnp.concatenate([o[0, 0:4] for o in spread(offs)])
+    offs_at = [o[0, 0:4] for o in spread(offs)]
 
     grads_sorted = sort_rows(cotangent, pos)
-    g_all = jnp.stack(spread(grads_sorted))
+    g = spread(grads_sorted)
+    tokens = tie(tokens, grads_sorted)
 
     qkv = qkv_rows(tokens, gain_one, w_qkv)
+    if small:
+        qkv = tie(qkv, column)
     context, lse = attend(qkv, text_lengths)
+    context = tie(context, g[2], g[1], *(wb_all[1:2] if small else []))
     middle, sending = middle_rows(context, w_proj, tokens, gain_two, pos)
-    x_all = jnp.stack(spread(sending))
-
-    out, gx, dwi, dwb = experts(offs_all, hosts, x_all, g_all, wi_all, wb_all)
-
-    def collect(parts):
-        near = swap(parts[1], 1)
-        far = (parts[2].astype(F32) + swap(parts[3], 1).astype(F32)).astype(BF16)
-        return parts[0], near, swap(far, 2)
+    x = spread(sending)
+
+    def run(pair, before):
+        return experts(
+            jnp.concatenate([offs_at[i] for i in pair]),
+            hosts,
+            [x[i] for i in pair],
+            [g[i] for i in pair],
+            wi_all,
+            wb_all,
+            before,
+        )
+
+    def add(a, b):
+        return (a.astype(F32) + b.astype(F32)).astype(BF16)
+
+    out2, out3, gx2, gx3, dwi, dwb = run((2, 3), None)
+    gx_half = add(gx2, swap(gx3, 1))
+    x[0] = tie(x[0], gx_half)
+    gx_far = swap(gx_half, 2)
+    out0, out1, gx0, gx1, dwi, dwb = run((0, 1), (dwi, dwb))
+    gx_near = swap(gx1, 1)
+    out_near = swap(out1, 1)
+    out_far = swap(tie(add(out2, swap(out3, 1)), gx_far), 2)
+    if small:
+        share_in = lax.psum_scatter(dwi, "batch", scatter_dimension=1, tiled=True)
+        share_back = cross_y(dwb, own)
 
     grad_middle, gctx, dw_proj, dg_two = back_rows(
-        *collect(gx), pos_col, middle, cotangent, gain_two, context, w_proj
+        gx0, gx_near, gx_far, pos_col, middle, cotangent, gain_two, context, w_proj
     )
-    block_out = finish_rows(*collect(out), pos_col, middle)
+    if small:
+        gctx = tie(gctx, share_back)
+        share_back = cross_z(share_back)
     grad_qkv = attend_back(qkv, gctx, lse, text_lengths)
     input_grad, dw_qkv, dg_one = first_back(tokens, gain_one, grad_qkv, w_qkv, grad_middle)
-
-    def settle(grad, dim):
-        share = lax.psum_scatter(grad, "batch", scatter_dimension=dim, tiled=True)
-        whole = lax.all_gather(share, "batch", axis=dim, tiled=True)
-        return lax.dynamic_index_in_dim(whole, own_expert, 0, keepdims=True).astype(F32)
-
-    grad_w_in = settle(dwi, 1)
-    grad_w_back = settle(dwb, 1)
-    summed_qkv, summed_proj = lax.psum(
-        (dw_qkv.astype(BF16), dw_proj.astype(BF16)), ("batch", "ffn")
-    )
-    gains = lax.psum(jnp.concatenate([dg_one, dg_two], axis=0), ("batch", "ffn"))
+    block_out = finish_rows(out0, out_near, out_far, pos_col, middle)
+
+    if small:
+        share_in = tie(share_in, grad_qkv)
+        pieces = lax.all_to_all(
+            deliver(share_in, share_back, group_map),
+            "batch",
+            split_axis=0,
+            concat_axis=0,
+            tiled=True,
+        )
+        grad_w_in = pieces[:, 0].reshape(1, D, D).astype(F32)
+        grad_w_back = pieces[:, 1].reshape(1, D, D).astype(F32)
+        gains = jnp.concatenate([dg_one, dg_two, jnp.zeros((GAIN_ROWS - 2, D), F32)], axis=0)
+        summed, gains = total_over_all(dw_qkv, dw_proj, gains)
+        summed_qkv, summed_proj = summed[:, 0 : 3 * D], summed[:, 3 * D : WIDE]
+    else:
+
+        def settle_any(grad):
+            share = lax.psum_scatter(grad, "batch", scatter_dimension=1, tiled=True)
+            whole = lax.all_gather(share, "batch", axis=1, tiled=True)
+            return lax.dynamic_index_in_dim(whole, own_expert, 0, keepdims=True).astype(F32)
+
+        grad_w_in = settle_any(dwi)
+        grad_w_back = settle_any(dwb)
+        summed_qkv, summed_proj = lax.psum((dw_qkv, dw_proj), ("batch", "ffn"))
+        gains = lax.psum(jnp.concatenate([dg_one, dg_two], axis=0), ("batch", "ffn"))
     return (
         block_out,
         input_grad,

time: 759 us -> 694 us (0.914)
  waiting for transfers between devices: 313 us -> 202 us
  Pallas kernels: 249 us -> 357 us
  blocking collectives: 92.8 us -> 0 us
  starting transfers between devices: 11.1 us -> 62.4 us
  other arithmetic: 48.5 us -> 26.8 us
    ppermute x0 -> x5, waiting for transfers between devices: none -> 142 us  [cross(): return lax.ppermute(rows, 'batch', [(b, b ^ bits) for b in range(8)])]
    all_gather x3 -> x0, waiting for transfers between devices: 122 us -> none  [the longest x2 122 us: settle(): whole = lax.all_gather(share, 'batch', axis=dim, tiled=True)]
    ppermute x15, waiting for transfers between devices: 161 us -> 60 us  [swap(): return lax.ppermute(rows, 'ffn', pairs)]
    pallas_call x1 -> x4, Pallas kernels: 86.4 us -> 181 us  [the longest x1 89.7 us: total_over_all(): pl.pallas_call(total_kernel, out_shape=(jax.ShapeDtypeStruct((D, WIDE), B...]
    psum x1 -> x0, blocking collectives: 92.8 us -> none  [body(): lax.psum(jnp.concatenate([dg_one, dg_two], axis=0), ('batch', 'ffn'))]
    all_to_all x0 -> x2, starting transfers between devices: none -> 45.6 us  [the longest x1 40.3 us: cross_z(): lax.all_to_all(rows, 'batch', split_axis=1, concat_axis=1, axis_index_gro...]
    psum x1 -> x0, waiting for transfers between devices: 28.6 us -> none  [body(): lax.psum((dw_qkv.astype(BF16), dw_proj.astype(BF16)), ('batch', 'ffn'))]
    another operation x3, other arithmetic: 17.9 us -> 0.12 us  [the longest x1 0.11 us: body(): column = jnp.stack([wb_part, cross(wb_part, 1)])]
  transfers between devices with their start and end apart: 22 -> 24, of which waited for: 10 -> 8; matrix products, arithmetic and copies ran while one was open for 8% -> 5% of each run, Pallas kernels for 22% -> 39%
where the time goes in v2:
time: 694 us; the launch traced here: 682 us
  Pallas kernels  357 us (51%)
  waiting for transfers between devices  202 us (29%)
  starting transfers between devices  62.4 us (9%)
  other arithmetic  26.8 us (4%)
  local copies, waits for them, and re-layouts  18.9 us (3%)
  between operations  15.1 us (2%)
    ppermute x5, waiting for transfers between devices, cross(): return lax.ppermute(rows, 'batch', [(b, b ^ bits) for b in range(8)])  142 us
    pallas_call x1, Pallas kernels, total_over_all(): pl.pallas_call(total_kernel, out_shape=(jax.ShapeDtypeStruct((D, WIDE), B...  89.7 us
    pallas_call x2, Pallas kernels, experts(): pl.pallas_call(functools.partial(expert_kernel, n_slots, carried), grid_s...  87.8 us
    ppermute x15, waiting for transfers between devices, swap(): return lax.ppermute(rows, 'ffn', pairs)  60 us
    pallas_call x1, Pallas kernels, attend(): pl.pallas_call(attend_kernel, grid=(SEQ_DEV,), out_shape=(jax.ShapeDtypeS...  42.9 us
    all_to_all x1, starting transfers between devices, cross_z(): lax.all_to_all(rows, 'batch', split_axis=1, concat_axis=1, axis_index_gro...  40.3 us
    pallas_call x1, Pallas kernels, attend_back(): pl.pallas_call(attend_back_kernel, grid=(SEQ_DEV,), out_shape=jax.ShapeDt...  38.9 us
    pallas_call x1, Pallas kernels, first_back(): pl.pallas_call(first_back_kernel, grid=(ROWS // TILE,), out_shape=(jax.Sh...  27.9 us
  transfers between devices with their start and end apart: 24, of which 8 were waited for; matrix products, arithmetic and copies ran while one was open for 5% of the time, Pallas kernels for 39%

profile of v2, /device:TPU:0, one launch (start us, length us, event | category | flops | bytes accessed | tf_op | source)
XLA Modules:
  0.0 682.2 jit_solution(13275431097357160145)
XLA Ops:
  8.6 1.9 fusion.2
  11.2 1.9 constant_dynamic-slice_fusion
  14.5 1.9 route.1
  16.3 7.8 %sort_rows.1.refs_2_ = bf16[1616,768]{1,0:T(8,128)(2,1)} custom-call(bf16[1566,768]{1,0:T(8,128)(2,1)} %cot_ref.1, s32[1,1664]{1,0:T(1,128)} %get-tuple-element.43.pos_ref), custom_call_target="tpu_custom_call" | custom-call | flops 3931766784 | bytes 4866048 | tf_op jit(solution)/shard_map/sort_rows/pallas_call | solution.py:143
  24.1 2.9 collective-permute-start.2
  28.7 17.0 %collective-permute-done.1 = bf16[384,768]{1,0:T(8,128)(2,1)S(1)} collective-permute-done((bf16[384,768]{1,0:T(8,128)(2,1)S(1)}, bf16[384,768]{1,0:T(8,128)(2,1)S(1)}, u32[]{:S(2)}, u32[]{:S(2)}) %collective-permute-start.1) | collective-permute-done | bytes 589856 | tf_op jit(solution)/shard_map/ppermute | solution.py:682
  48.6 11.0 %qkv.1.qkv_ref = bf16[1584,2304]{1,0:T(8,128)(2,1)} custom-call(bf16[1566,768]{1,0:T(8,128)(2,1)} %tok_ref.2, f32[1,768]{1,0:T(1,128)} %reshape.96.gain_ref, bf16[768,2304]{1,0:T(8,128)(2,1)} %w_ref.7), custom_call_target="tpu_custom_call" | custom-call | flops 5605687296 | bytes 9732096 | tf_op jit(solution)/shard_map/qkv/pallas_call | solution.py:161
  59.6 42.9 %attend.1 = (bf16[1584,768]{1,0:T(8,128)(2,1)}, f32[6,16,384]{2,1,0:T(8,128)}) custom-call(s32[6]{0:T(128)} %len_ref.3, bf16[1584,2304]{1,0:T(8,128)(2,1)} %qkv.1.qkv_ref), custom_call_target="tpu_custom_call" | custom-call | flops 4076863488 | bytes 9732096 | tf_op jit(solution)/shard_map/attend/pallas_call | solution.py:226
  102.5 9.4 %collective-permute-done.4.refs_6_ = bf16[2,384,768]{2,1,0:T(8,128)(2,1)} collective-permute-done((bf16[2,384,768]{2,1,0:T(8,128)(2,1)S(1)}, bf16[2,384,768]{2,1,0:T(8,128)(2,1)}, u32[]{:S(2)}, u32[]{:S(2)}) %collective-permute-start.4) | collective-permute-done | bytes 1179680 | tf_op jit(solution)/shard_map/ppermute | solution.py:682
  113.4 11.6 %middle.1 = (f32[1566,768]{1,0:T(8,128)}, bf16[1616,768]{1,0:T(8,128)(2,1)}) custom-call(bf16[1584,768]{1,0:T(8,128)(2,1)} %get-tuple-element.47.ctx_ref, bf16[768,768]{1,0:T(8,128)(2,1)} %w_ref.6, bf16[1566,768]{1,0:T(8,128)(2,1)} %tok_ref.2, f32[1,768]{1,0:T(1,128)} %reshape.97.gain_ref, s32[1,1664]{1,0:T(1,128)} %get-tuple-element.43.pos_ref), custom_call_target="tpu_custom_call" | custom-call | flops 5800329216 | bytes 14598144 | tf_op jit(solution)/shard_map/middle/pallas_call | solution.py:262
  126.6 53.8 %collective-permute-done.7.refs_0_ = bf16[1616,768]{1,0:T(8,128)(2,1)} collective-permute-done((bf16[1616,768]{1,0:T(8,128)(2,1)}, bf16[1616,768]{1,0:T(8,128)(2,1)}, u32[]{:S(2)}, u32[]{:S(2)}) %collective-permute-start.7) | collective-permute-done | bytes 2482208 | tf_op jit(solution)/shard_map/ppermute | solution.py:672
  181.7 2.1 collective-permute-start.11
  189.0 71.5 %collective-permute-done.10.refs_7_ = bf16[2,384,768]{2,1,0:T(8,128)(2,1)S(1)} collective-permute-done((bf16[2,384,768]{2,1,0:T(8,128)(2,1)S(1)}, bf16[2,384,768]{2,1,0:T(8,128)(2,1)S(1)}, u32[]{:S(2)}, u32[]{:S(2)}) %collective-permute-start.10) | collective-permute-done | bytes 1179680 | tf_op jit(solution)/shard_map/ppermute | solution.py:682
  261.6 43.4 %experts.2 = (bf16[1616,768]{1,0:T(8,128)(2,1)}, bf16[1616,768]{1,0:T(8,128)(2,1)}, bf16[1616,768]{1,0:T(8,128)(2,1)}, bf16[1616,768]{1,0:T(8,128)(2,1)}, bf16[3...) custom-call(s32[8]{0:T(128)} %pad_add_fusion.2.offs_ref, s32[12]{0:T(128)} %reshape.95.hosts_ref, ...), custom_call_target="tpu_custom_call" | custom-call | flops 22875734016 | bytes 19857408 | tf_op jit(solution)/shard_map/experts/pallas_call | solution.py:430
  305.7 4.1 collective-permute-done
  310.4 3.9 add_convert_fusion.1
  315.7 44.3 %experts.3 = (bf16[1616,768]{1,0:T(8,128)(2,1)}, bf16[1616,768]{1,0:T(8,128)(2,1)}, bf16[1616,768]{1,0:T(8,128)(2,1)}, bf16[1616,768]{1,0:T(8,128)(2,1)}, bf16[3...) custom-call(s32[8]{0:T(128)} %pad_add_fusion.1.offs_ref, s32[12]{0:T(128)} %reshape.95.hosts_ref, ...), custom_call_target="tpu_custom_call" | custom-call | flops 22875734016 | bytes 19857408 | tf_op jit(solution)/shard_map/experts/pallas_call | solution.py:430
  360.1 2.8 dynamic-slice_bitcast_fusion
  363.1 1.6 collective-permute-start.16
  364.7 43.8 %collective-permute-done.19 = bf16[3,4,96,768]{3,2,1,0:T(8,128)(2,1)S(1)} collective-permute-done((bf16[3,4,96,768]{3,2,1,0:T(8,128)(2,1)}, bf16[3,4,96,768]{3,2,1,0:T(8,128)(2,1)S(1)}, u32[]{:S(2)}, u32[]{:S(2)}) %collective-permute-start.19) | collective-permute-done | bytes 1769504 | tf_op jit(solution)/shard_map/ppermute | solution.py:682
  408.5 2.0 fusion
  411.8 40.3 %all-to-all-start = ((bf16[3,4,96,768]{3,2,0,1:T(8,128)(2,1)}), bf16[3,4,96,768]{3,2,0,1:T(8,128)(2,1)S(1)}, u32[]{:S(2)}, u32[]{:S(2)}) async-start(bf16[3,4,96,768]{3,2,0,1:T(8,128)(2,1)} %copy.32), calls=%async_computation.1 | async-start | bytes 3538944 | tf_op jit(solution)/shard_map/all_to_all | solution.py:725
  453.5 22.9 %back.1 = (f32[1566,768]{1,0:T(8,128)}, bf16[1584,768]{1,0:T(8,128)(2,1)}, bf16[768,768]{1,0:T(8,128)(2,1)}, f32[1,768]{1,0:T(1,128)}) custom-call(bf16[1616,768]{1,0:T(8,128)(2,1)} %get-tuple-element.60.a_ref, bf16[1616,768]{1,0:T(8,128)(2,1)} %collective-permute-done.18.b_ref, bf16[1616,768]{1,0:T(8,128)(2,1)} %collective-permute-done.16.c_ref, ...), custom_call_target="tpu_custom_call" | custom-call | flops 7668891648 | bytes 29196288 | tf_op jit(solution)/shard_map/back/pallas_call | solution.py:502
  476.5 38.9 %attend_back.1.gq_ref = bf16[1584,2304]{1,0:T(8,128)(2,1)} custom-call(s32[6]{0:T(128)} %len_ref.3, bf16[1584,2304]{1,0:T(8,128)(2,1)} %qkv.1.qkv_ref, bf16[1584,768]{1,0:T(8,128)(2,1)} %get-tuple-element.64.gctx_ref, f32[6,16,384]{2,1,0:T(8,128)} %get-tuple-element.65.lse_ref), custom_call_target="tpu_custom_call" | custom-call | flops 10192158720 | bytes 17031168 | tf_op jit(solution)/shard_map/attend_back/pallas_call | solution.py:604
  516.7 3.6 deliver.1
  520.3 5.2 all-to-all-start.1
  525.9 4.5 add_convert_fusion
  531.9 27.9 %first_back.1 = (f32[1566,768]{1,0:T(8,128)}, bf16[768,2304]{1,0:T(8,128)(2,1)}, f32[1,768]{1,0:T(1,128)}) custom-call(bf16[1566,768]{1,0:T(8,128)(2,1)} %tok_ref.2, f32[1,768]{1,0:T(1,128)} %reshape.96.gain_ref, bf16[1584,2304]{1,0:T(8,128)(2,1)} %attend_back.1.gq_ref, bf16[768,2304]{1,0:T(8,128)(2,1)} %w_ref.7, f32[1566,768]{1,0:T(8,128)} %get-tuple-element.66.gm_ref), custom_call_target="tpu_custom_call" | custom-call | flops 11211374592 | bytes 19464192 | tf_op jit(solution)/shard_map/first_back/pallas_call | solution.py:647
  561.1 89.7 %total.1 = (bf16[768,3072]{1,0:T(8,128)(2,1)}, f32[8,768]{1,0:T(8,128)}) custom-call(bf16[768,2304]{1,0:T(8,128)(2,1)} %get-tuple-element.68.qkv_ref, bf16[768,768]{1,0:T(8,128)(2,1)} %get-tuple-element.69.proj_ref, f32[8,768]{1,0:T(8,128)} %maximum_maximum_fusion.gain_ref), custom_call_target="tpu_custom_call" | custom-call | tf_op jit(solution)/shard_map/total/pallas_call | solution.py:888
  652.2 2.8 slice_convert_fusion.1
  655.1 5.5 slice_convert_fusion
  660.6 11.2 %finish.1 = f32[1566,768]{1,0:T(8,128)} custom-call(bf16[1616,768]{1,0:T(8,128)(2,1)} %get-tuple-element.54.a_ref, bf16[1616,768]{1,0:T(8,128)(2,1)} %collective-permute-done.14.b_ref, bf16[1616,768]{1,0:T(8,128)(2,1)} %collective-permute-done.17.c_ref, s32[1584,1]{1,0:T(8,128)} %copy.30.pos_ref, f32[1566,768]{1,0:T(8,128)} %get-tuple-element.59.mid_ref), custom_call_target="tpu_custom_call" | custom-call | flops 3931766784 | bytes 17031168 | tf_op jit(solution)/shard_map/finish/pallas_call | solution.py:541
  (94 shorter events, 32.6 us)
Async XLA Ops:
  7.2 19.9 %copy-start = (bf16[1,768,768]{2,1,0:T(8,128)(2,1)S(1)}, bf16[1,768,768]{2,1,0:T(8,128)(2,1)}, u32[]{:S(2)}) copy-start(bf16[1,768,768]{2,1,0:T(8,128)(2,1)} %param.20) | copy-start | bytes 3538948
  7.2 253.4 %all-gather.2.cloned.1.call-start = ((), (), s32[]{:S(2)}) async-start(), calls=%async_computation.3 | async-start | bytes 5308416 | tf_op jit(solution)/shard_map/all_gather | solution.py:939
  13.1 503.6 %reduce-scatter.2.cloned.1.call-start = ((), (), s32[]{:S(2)}) async-start(), calls=%async_computation.4 | async-start | bytes 3981312 | tf_op jit(solution)/shard_map/reduce_scatter | solution.py:989
  24.1 23.3 %copy-start.5 = (f32[768]{0:T(1024)S(1)}, f32[768]{0:T(1024)}, u32[]{:S(2)}) copy-start(f32[768]{0:T(1024)} %param.15) | copy-start | bytes 9220
  24.1 23.9 %copy-start.6 = (f32[768]{0:T(1024)S(1)}, f32[768]{0:T(1024)}, u32[]{:S(2)}) copy-start(f32[768]{0:T(1024)} %param.18) | copy-start | bytes 9220
  24.1 87.8 %collective-permute-start.2 = (bf16[1616,768]{1,0:T(8,128)(2,1)}, bf16[1616,768]{1,0:T(8,128)(2,1)}, u32[]{:S(2)}, u32[]{:S(2)}) collective-permute-start(bf16[1616,768]{1,0:T(8,128)(2,1)} %sort_rows.1.refs_2_), channel_id=1, source_target_pairs={{0,2},{1,3},{2,0},{3,1},{4,6},{5,7},{6,4},{7,5},{8,10},{9,11},{10,... | collective-permute-start | bytes 7446536 | tf_op jit(solution)/shard_map/ppermute | solution.py:672
  27.0 84.9 %collective-permute-start.3 = (bf16[1616,768]{1,0:T(8,128)(2,1)}, bf16[1616,768]{1,0:T(8,128)(2,1)S(1)}, u32[]{:S(2)}, u32[]{:S(2)}) collective-permute-start(bf16[1616,768]{1,0:T(8,128)(2,1)} %sort_rows.1.refs_2_), channel_id=1, source_target_pairs={{0,1},{1,0},{2,3},{3,2},{4,5},{5,4},{6,7},{7,6},{8,9},{9,8},{10,11... | collective-permute-start | bytes 7446536 | tf_op jit(solution)/shard_map/ppermute | solution.py:672
  27.1 18.7 %collective-permute-start.1 = (bf16[384,768]{1,0:T(8,128)(2,1)S(1)}, bf16[384,768]{1,0:T(8,128)(2,1)S(1)}, u32[]{:S(2)}, u32[]{:S(2)}) collective-permute-start(bf16[384,768]{1,0:T(8,128)(2,1)S(1)} %fusion.4), channel_id=1, source_target_pairs={{0,4},{4,0},{8,12},{12,8},{16,20},{20,16},{24,28},{28,24},{1,5},{5... | collective-permute-start | bytes 1769480 | tf_op jit(solution)/shard_map/ppermute | solution.py:682
  45.9 135.8 %copy-start.2 = (bf16[2,384,768]{2,1,0:T(8,128)(2,1)}, bf16[2,384,768]{2,1,0:T(8,128)(2,1)S(1)}, u32[]{:S(2)}) copy-start(bf16[2,384,768]{2,1,0:T(8,128)(2,1)S(1)} %pad_maximum_fusion.refs_5_) | copy-start | bytes 3538948
  45.9 66.0 %collective-permute-start.4 = (bf16[2,384,768]{2,1,0:T(8,128)(2,1)S(1)}, bf16[2,384,768]{2,1,0:T(8,128)(2,1)}, u32[]{:S(2)}, u32[]{:S(2)}) collective-permute-start(bf16[2,384,768]{2,1,0:T(8,128)(2,1)S(1)} %pad_maximum_fusion.refs_5_), channel_id=1, source_target_pairs={{0,8},{4,12},{8,0},{12,4},{16,24},{20,28},{24,16},{28,20},{1,9},{5... | collective-permute-start | bytes 3538952 | tf_op jit(solution)/shard_map/ppermute | solution.py:682
  113.4 70.3 %copy-start.11 = (s32[1,128]{1,0:T(1,128)S(1)}, s32[1,128]{1,0:T(1,128)}, u32[]{:S(2)}) copy-start(s32[1,128]{1,0:T(1,128)} %get-tuple-element.42) | copy-start | bytes 1540
  113.4 71.8 %copy-start.4 = (s32[8]{0:T(128)S(1)}, s32[8]{0:T(128)}, u32[]{:S(2)}) copy-start(s32[8]{0:T(128)} %gm_ref.3) | copy-start | bytes 100
  125.0 55.3 %collective-permute-start.7 = (bf16[1616,768]{1,0:T(8,128)(2,1)}, bf16[1616,768]{1,0:T(8,128)(2,1)}, u32[]{:S(2)}, u32[]{:S(2)}) collective-permute-start(bf16[1616,768]{1,0:T(8,128)(2,1)} %get-tuple-element.51.refs_0_), channel_id=1, source_target_pairs={{0,2},{1,3},{2,0},{3,1},{4,6},{5,7},{6,4},{7,5},{8,10},{9,11},{10,... | collective-permute-start | bytes 7446536 | tf_op jit(solution)/shard_map/ppermute | solution.py:672
  126.6 134.0 %collective-permute-start.9 = (bf16[1616,768]{1,0:T(8,128)(2,1)}, bf16[1616,768]{1,0:T(8,128)(2,1)}, u32[]{:S(2)}, u32[]{:S(2)}) collective-permute-start(bf16[1616,768]{1,0:T(8,128)(2,1)} %collective-permute-done.2.refs_2_), channel_id=1, source_target_pairs={{0,1},{1,0},{2,3},{3,2},{4,5},{5,4},{6,7},{7,6},{8,9},{9,8},{10,11... | collective-permute-start | bytes 7446536 | tf_op jit(solution)/shard_map/ppermute | solution.py:672
  180.3 80.2 %collective-permute-start.8 = (bf16[1616,768]{1,0:T(8,128)(2,1)}, bf16[1616,768]{1,0:T(8,128)(2,1)}, u32[]{:S(2)}, u32[]{:S(2)}) collective-permute-start(bf16[1616,768]{1,0:T(8,128)(2,1)} %collective-permute-done.7.refs_0_), channel_id=1, source_target_pairs={{0,1},{1,0},{2,3},{3,2},{4,5},{5,4},{6,7},{7,6},{8,9},{9,8},{10,11... | collective-permute-start | bytes 7446536 | tf_op jit(solution)/shard_map/ppermute | solution.py:672
  180.4 80.2 %collective-permute-start.10 = (bf16[2,384,768]{2,1,0:T(8,128)(2,1)S(1)}, bf16[2,384,768]{2,1,0:T(8,128)(2,1)S(1)}, u32[]{:S(2)}, u32[]{:S(2)}) collective-permute-start(bf16[2,384,768]{2,1,0:T(8,128)(2,1)S(1)} %pad_maximum_fusion.refs_5_), channel_id=1, source_target_pairs={{0,16},{4,20},{8,24},{12,28},{16,0},{20,4},{24,8},{28,12},{1,17},{... | collective-permute-start | bytes 3538952 | tf_op jit(solution)/shard_map/ppermute | solution.py:682
  181.7 78.9 %collective-permute-start.11 = (bf16[2,384,768]{2,1,0:T(8,128)(2,1)S(1)}, bf16[2,384,768]{2,1,0:T(8,128)(2,1)}, u32[]{:S(2)}, u32[]{:S(2)}) collective-permute-start(bf16[2,384,768]{2,1,0:T(8,128)(2,1)S(1)} %pad_maximum_fusion.refs_5_), channel_id=1, source_target_pairs={{0,24},{4,28},{8,16},{12,20},{16,8},{20,12},{24,0},{28,4},{1,25},{... | collective-permute-start | bytes 3538952 | tf_op jit(solution)/shard_map/ppermute | solution.py:682
  183.8 3.5 collective-permute-start.5
  187.3 1.1 collective-permute-start.6
  305.0 5.3 collective-permute-start.12
  305.1 9.1 %collective-permute-start.13 = (bf16[1616,768]{1,0:T(8,128)(2,1)}, bf16[1616,768]{1,0:T(8,128)(2,1)S(1)}, u32[]{:S(2)}, u32[]{:S(2)}) collective-permute-start(bf16[1616,768]{1,0:T(8,128)(2,1)} %get-tuple-element.51.refs_0_), channel_id=1, source_target_pairs={{0,1},{1,0},{2,3},{3,2},{4,5},{5,4},{6,7},{7,6},{8,9},{9,8},{10,11... | collective-permute-start | bytes 7446536 | tf_op jit(solution)/shard_map/ppermute | solution.py:672
  305.6 4.2 collective-permute-start
  362.9 45.6 %collective-permute-start.19 = (bf16[3,4,96,768]{3,2,1,0:T(8,128)(2,1)}, bf16[3,4,96,768]{3,2,1,0:T(8,128)(2,1)S(1)}, u32[]{:S(2)}, u32[]{:S(2)}) collective-permute-start(bf16[3,4,96,768]{3,2,1,0:T(8,128)(2,1)} %dynamic-slice_bitcast_fusion), channel_id=1, source_target_pairs={{0,4},{4,0},{8,12},{12,8},{16,20},{20,16},{24,28},{28,24},{1,5},{5... | collective-permute-start | bytes 5308424 | tf_op jit(solution)/shard_map/ppermute | solution.py:682
  362.9 90.7 %collective-permute-start.18 = (bf16[1616,768]{1,0:T(8,128)(2,1)}, bf16[1616,768]{1,0:T(8,128)(2,1)}, u32[]{:S(2)}, u32[]{:S(2)}) collective-permute-start(bf16[1616,768]{1,0:T(8,128)(2,1)} %get-tuple-element.61), channel_id=1, source_target_pairs={{0,1},{1,0},{2,3},{3,2},{4,5},{5,4},{6,7},{7,6},{8,9},{9,8},{10,11... | collective-permute-start | bytes 7446536 | tf_op jit(solution)/shard_map/ppermute | solution.py:672
  363.1 90.5 %collective-permute-start.16 = (bf16[1616,768]{1,0:T(8,128)(2,1)}, bf16[1616,768]{1,0:T(8,128)(2,1)}, u32[]{:S(2)}, u32[]{:S(2)}) collective-permute-start(bf16[1616,768]{1,0:T(8,128)(2,1)} %add_convert_fusion.1), channel_id=1, source_target_pairs={{0,2},{1,3},{2,0},{3,1},{4,6},{5,7},{6,4},{7,5},{8,10},{9,11},{10,... | collective-permute-start | bytes 7446536 | tf_op jit(solution)/shard_map/ppermute | solution.py:672
  411.8 40.4 %copy-start.3 = (s32[1,1664]{1,0:T(1,128)S(1)}, s32[1,1664]{1,0:T(1,128)}, u32[]{:S(2)}) copy-start(s32[1,1664]{1,0:T(1,128)} %get-tuple-element.43.pos_ref) | copy-start | bytes 19972
  411.8 103.5 %all-to-all-start = ((bf16[3,4,96,768]{3,2,0,1:T(8,128)(2,1)}), bf16[3,4,96,768]{3,2,0,1:T(8,128)(2,1)S(1)}, u32[]{:S(2)}, u32[]{:S(2)}) async-start(bf16[3,4,96,768]{3,2,0,1:T(8,128)(2,1)} %copy.32), calls=%async_computation.1 | async-start | bytes 3538944 | tf_op jit(solution)/shard_map/all_to_all | solution.py:725
  452.2 73.7 %collective-permute-start.15 = (bf16[1616,768]{1,0:T(8,128)(2,1)}, bf16[1616,768]{1,0:T(8,128)(2,1)}, u32[]{:S(2)}, u32[]{:S(2)}) collective-permute-start(bf16[1616,768]{1,0:T(8,128)(2,1)} %get-tuple-element.57), channel_id=1, source_target_pairs={{0,1},{1,0},{2,3},{3,2},{4,5},{5,4},{6,7},{7,6},{8,9},{9,8},{10,11... | collective-permute-start | bytes 7446536 | tf_op jit(solution)/shard_map/ppermute | solution.py:672
  520.3 151.5 %all-to-all-start.1 = ((bf16[8,2,96,768]{3,2,1,0:T(8,128)(2,1)}), bf16[8,2,96,768]{3,2,1,0:T(8,128)(2,1)S(1)}, u32[]{:S(2)}, u32[]{:S(2)}) async-start(bf16[8,2,96,768]{3,2,1,0:T(8,128)(2,1)} %deliver.1), calls=%async_computation.2 | async-start | bytes 4718592 | tf_op jit(solution)/shard_map/all_to_all | solution.py:1004
  525.7 134.9 %collective-permute-start.14 = (bf16[1616,768]{1,0:T(8,128)(2,1)}, bf16[1616,768]{1,0:T(8,128)(2,1)}, u32[]{:S(2)}, u32[]{:S(2)}) collective-permute-start(bf16[1616,768]{1,0:T(8,128)(2,1)} %get-tuple-element.55), channel_id=1, source_target_pairs={{0,1},{1,0},{2,3},{3,2},{4,5},{5,4},{6,7},{7,6},{8,9},{9,8},{10,11... | collective-permute-start | bytes 7446536 | tf_op jit(solution)/shard_map/ppermute | solution.py:672
  530.4 130.2 %collective-permute-start.17 = (bf16[1616,768]{1,0:T(8,128)(2,1)}, bf16[1616,768]{1,0:T(8,128)(2,1)}, u32[]{:S(2)}, u32[]{:S(2)}) collective-permute-start(bf16[1616,768]{1,0:T(8,128)(2,1)} %add_convert_fusion), channel_id=1, source_target_pairs={{0,2},{1,3},{2,0},{3,1},{4,6},{5,7},{6,4},{7,5},{8,10},{9,11},{10,... | collective-permute-start | bytes 7446536 | tf_op jit(solution)/shard_map/ppermute | solution.py:672
  531.9 27.9 %copy-start.7 = (f32[1,768]{1,0:T(1,128)S(1)}, f32[1,768]{1,0:T(1,128)}, u32[]{:S(2)}) copy-start(f32[1,768]{1,0:T(1,128)} %get-tuple-element.71) | copy-start | bytes 9220
  (4 other events, 7.1 us)
Sparse Core Ops, SparseCore 0:
  13.2 98.1 all-gather.1
  360.2 127.6 reduce-scatter.1

commit v3 on v2

--- a/solution.py
+++ b/solution.py
@@ -123,74 +123,17 @@
 SORT_TILES = (336, 336, 336, 336, 272)
 
 
-def sort_into(out_ref, rows_ref, pos_ref):
-    pos = pos_ref[0:1, 0:ROWS]
-    top = 0
-    for size in SORT_TILES:
-        want = top + lax.broadcasted_iota(I32, (size, ROWS), 0)
-        hot = jnp.where(pos == want, 1.0, 0.0).astype(BF16)
-        out_ref[top : top + size, :] = dot(hot, rows_ref[...]).astype(BF16)
-        top += size
-
-
-def sort_kernel(rows_ref, pos_ref, out_ref, held):
-    held[1552:ROWS, :] = jnp.zeros((ROWS - 1552, D), BF16)
-    held[0:TOK_DEV, :] = rows_ref[...]
-    sort_into(out_ref, held, pos_ref)
-
-
-def sort_rows(rows, pos):
-    return pl.pallas_call(
-        sort_kernel,
-        out_shape=jax.ShapeDtypeStruct((SORTED, D), BF16),
-        scratch_shapes=[pltpu.VMEM((ROWS, D), BF16)],
-        compiler_params=params(),
-        cost_estimate=cost(2 * SORTED * ROWS * D, 4 * ROWS * D),
-        name="sort_rows",
-    )(rows, pos)
-
-
-def qkv_kernel(tok_ref, gain_ref, w_ref, out_ref):
-    normal, _ = norm_parts(tok_ref[...].astype(F32))
-    keep = row_mask(pl.program_id(0) * TILE, TILE, TOK_DEV)
-    normed = jnp.where(keep, normal * gain_ref[...], 0.0).astype(BF16)
-    out_ref[...] = dot(normed, w_ref[...]).astype(BF16)
-
-
-def qkv_rows(tokens, gain, w_qkv):
-    return pl.pallas_call(
-        qkv_kernel,
-        grid=(ROWS // TILE,),
-        out_shape=jax.ShapeDtypeStruct((ROWS, 3 * D), BF16),
-        in_specs=[
-            pl.BlockSpec((TILE, D), lambda i: (i, 0)),
-            full((1, D)),
-            once((D, 3 * D)),
-        ],
-        out_specs=pl.BlockSpec((TILE, 3 * D), lambda i: (i, 0)),
-        compiler_params=params(),
-        cost_estimate=cost(2 * ROWS * D * 3 * D, 2 * ROWS * D * 4),
-        name="qkv",
-    )(tokens, gain, w_qkv)
-
-
 def window(pair):
     first = pair * SEQ_LEN
     start = first // 16 * 16
     return start, first - start
 
 
-def attend_kernel(len_ref, qkv_ref, ctx_ref, lse_ref, stat):
-    pair = pl.program_id(0)
+def attend_pair(pair, length, qkv_ref, ctx_ref, lse_ref, stat):
     start, skip = window(pair)
     start = pl.multiple_of(start, 16)
-
-    @pl.when(pair == 0)
-    def _():
-        ctx_ref[...] = jnp.zeros_like(ctx_ref)
-
     key = lax.broadcasted_iota(I32, (1, WIN), 1)
-    seen = (key >= skip) & (key < skip + PATCHES + len_ref[pair])
+    seen = (key >= skip) & (key < skip + PATCHES + length)
     bias = jnp.where(seen, 0.0, -1e30)
     row = lax.broadcasted_iota(I32, (WIN, 1), 0)
     mine = (row >= skip) & (row < skip + SEQ_LEN)
@@ -219,61 +162,295 @@
         ctx = jnp.where(lane < 64, pieces[0], pieces[1]).astype(BF16)
         old = ctx_ref[pl.ds(start, WIN), cols]
         ctx_ref[pl.ds(start, WIN), cols] = jnp.where(mine, ctx, old)
-    lse_ref[0] = jnp.transpose(stat[...])[0:16, :]
-
-
-def attend(qkv, lengths):
-    return pl.pallas_call(
-        attend_kernel,
-        grid=(SEQ_DEV,),
-        out_shape=(
-            jax.ShapeDtypeStruct((ROWS, D), BF16),
-            jax.ShapeDtypeStruct((SEQ_DEV, 16, 384), F32),
-        ),
-        in_specs=[
-            pl.BlockSpec(memory_space=pltpu.SMEM),
-            once((ROWS, 3 * D)),
-        ],
-        out_specs=(
-            full((ROWS, D)),
-            pl.BlockSpec((1, 16, 384), lambda s: (s, 0, 0)),
-        ),
-        scratch_shapes=[pltpu.VMEM((384, 128), F32)],
-        compiler_params=params(),
-        cost_estimate=cost(72 * 4 * WIN * 384 * 128, 2 * ROWS * D * 4),
-        name="attend",
-    )(lengths, qkv)
-
-
-def middle_kernel(ctx_ref, w_ref, tok_ref, gain_ref, pos_ref, mid_ref, out_ref, held):
+    lse_ref[pair] = jnp.transpose(stat[...])[0:16, :]
+
+
+MESH = pl.DeviceIdType.MESH
+HALF = 384
+FF_DEV = 768
+HOPS = [(way, hop) for hop in (1, 2, 3) for way in (1, -1)]
+
+
+def front_kernel(
+    small,
+    len_ref,
+    pos_ref,
+    tok_ref,
+    cot_ref,
+    gain_one_ref,
+    w_qkv_ref,
+    w_proj_ref,
+    gain_two_ref,
+    wi_hbm,
+    wb_hbm,
+    qkv_hbm,
+    ctx_hbm,
+    lse_hbm,
+    mid_hbm,
+    g_hbm,
+    x_hbm,
+    wi_all,
+    wb_all,
+    qkv,
+    ctx,
+    lse,
+    mid,
+    g_sorted,
+    x_sorted,
+    held,
+    stat,
+    local_sems,
+    send_sems,
+    recv_sems,
+    hop_send,
+    hop_recv,
+    pass_send,
+    pass_recv,
+):
+    batch, ffn = lax.axis_index("batch"), lax.axis_index("ffn")
+    z, y = batch // 2, batch % 2
+    near, far = (batch, ffn ^ 1), (batch, ffn ^ 2)
+    across = (batch ^ 1, ffn)
+
+    barrier = pltpu.get_barrier_semaphore()
+    for device in [near, far] + ([across] if small else []):
+        pl.semaphore_signal(barrier, inc=1, device_id=device, device_id_type=MESH)
+    if small:
+        for way in (1, -1):
+
+            @pl.when((z + way >= 0) & (z + way <= 3))
+            def _(way=way):
+                pl.semaphore_signal(
+                    barrier, inc=1, device_id=(batch + 2 * way, ffn), device_id_type=MESH
+                )
+
+        inner = jnp.where((z == 0) | (z == 3), 1, 2)
+        pl.semaphore_wait(barrier, 3 + inner)
+    else:
+        pl.semaphore_wait(barrier, 2)
+
+    local_count = [0]
+    waiting = []
+
+    def local(src, dst):
+        number = local_count[0]
+        local_count[0] += 1
+        copy = pltpu.make_async_copy(src, dst, local_sems.at[number])
+        copy.start()
+        waiting.append(copy)
+
+    used = [0]
+
+    def send(src, dst, device):
+        number = used[0]
+        used[0] += 1
+        copy = pltpu.make_async_remote_copy(
+            src_ref=src,
+            dst_ref=dst,
+            send_sem=send_sems.at[number],
+            recv_sem=recv_sems.at[number],
+            device_id=device,
+            device_id_type=MESH,
+        )
+        copy.start()
+        return copy
+
+    part, whole = (wi_hbm, wb_hbm), (wi_all, wb_all)
+
+    def valid(origin):
+        return (origin >= 0) & (origin <= 3)
+
+    def hop_copy(a, way, hop, origin, device):
+        slot = whole[a].at[origin * 2 + y]
+        number = HOPS.index((way, hop))
+        return pltpu.make_async_remote_copy(
+            src_ref=part[a] if hop == 1 else slot,
+            dst_ref=slot,
+            send_sem=hop_send.at[a, number],
+            recv_sem=hop_recv.at[a, number],
+            device_id=device,
+            device_id_type=MESH,
+        )
+
+    def hop_go(a, hop, finish=False):
+        for way in (1, -1):
+            origin = z - way * (hop - 1)
+
+            @pl.when(valid(origin) & valid(z + way))
+            def _(way=way, origin=origin):
+                copy = hop_copy(a, way, hop, origin, (batch + 2 * way, ffn))
+                if finish:
+                    copy.wait_send()
+                else:
+                    copy.start()
+
+    def pass_copy(a, way, hop, origin, column):
+        slot = whole[a].at[origin * 2 + column]
+        number = HOPS.index((way, hop))
+        return pltpu.make_async_remote_copy(
+            src_ref=slot,
+            dst_ref=slot,
+            send_sem=pass_send.at[a, number],
+            recv_sem=pass_recv.at[a, number],
+            device_id=across,
+            device_id_type=MESH,
+        )
+
+    def hop_came(a, hop):
+        for way in (1, -1):
+            origin = z - way * hop
+
+            @pl.when(valid(origin))
+            def _(way=way, origin=origin):
+                hop_copy(a, way, hop, origin, (batch, ffn)).wait_recv()
+
+        if hop < 3:
+            hop_go(a, hop + 1)
+        for way in (1, -1):
+            origin = z - way * hop
+
+            @pl.when(valid(origin))
+            def _(way=way, origin=origin):
+                pass_copy(a, way, hop, origin, y).start()
+
+    own_over = []
+    if small:
+        for a in range(2):
+            hop_go(a, 1)
+            own_over.append(send(part[a], whole[a].at[batch], across))
+            local(part[a], whole[a].at[batch])
+
+    exchanged = []
+
+    def sort_and_send(rows_ref, out_ref, out_hbm):
+        pos = pos_ref[0:1, 0:ROWS]
+        top = 0
+        sent = []
+        for size in SORT_TILES:
+            want = top + lax.broadcasted_iota(I32, (size, ROWS), 0)
+            hot = jnp.where(pos == want, 1.0, 0.0).astype(BF16)
+            rows = pl.ds(top, size)
+            out_ref[rows, :] = dot(hot, rows_ref[...]).astype(BF16)
+            sent.append(send(out_ref.at[rows], out_hbm.at[2, rows], far))
+            exchanged.append(send(out_ref.at[rows], out_hbm.at[1, rows], near))
+            local(out_ref.at[rows], out_hbm.at[0, rows])
+            top += size
+        return sent
+
+    def hand_on(sent, out_hbm):
+        top = 0
+        for copy, size in zip(sent, SORT_TILES):
+            rows = pl.ds(top, size)
+            copy.wait()
+            exchanged.append(send(out_hbm.at[2, rows], out_hbm.at[3, rows], near))
+            top += size
+
     held[1552:ROWS, :] = jnp.zeros((ROWS - 1552, D), BF16)
+    held[0:TOK_DEV, :] = cot_ref[...]
+    g_sent = sort_and_send(held, g_sorted, g_hbm)
+
     for i in range(3):
         top = min(TILE * (i + 1), TOK_DEV)
         rows = slice(TILE * i, top)
-        attended = dot(ctx_ref[rows, :], w_ref[...])
-        middle = tok_ref[rows, :].astype(F32) + attended
-        mid_ref[rows, :] = middle
+        normal, _ = norm_parts(tok_ref[rows, :].astype(F32))
+        normed = (normal * gain_one_ref[...]).astype(BF16)
+        qkv[rows, :] = dot(normed, w_qkv_ref[...]).astype(BF16)
+    tail = slice(TOK_DEV, ROWS)
+    qkv[tail, :] = jnp.zeros((ROWS - TOK_DEV, 3 * D), BF16)
+    ctx[1552:ROWS, :] = jnp.zeros((ROWS - 1552, D), BF16)
+    local(qkv, qkv_hbm)
+    if small:
+        hop_came(0, 1)
+
+    @pl.loop(0, SEQ_DEV)
+    def _(pair):
+        attend_pair(pair, len_ref[pair], qkv, ctx, lse, stat)
+        if small:
+
+            @pl.when(pair == 1)
+            def _():
+                hop_came(1, 1)
+
+            @pl.when(pair == 4)
+            def _():
+                hop_came(0, 2)
+
+    local(ctx, ctx_hbm)
+    local(lse, lse_hbm)
+    for i in range(3):
+        top = min(TILE * (i + 1), TOK_DEV)
+        rows = slice(TILE * i, top)
+        middle = tok_ref[rows, :].astype(F32) + dot(ctx[rows, :], w_proj_ref[...])
+        mid[rows, :] = middle
         normal, _ = norm_parts(middle)
-        held[rows, :] = (normal * gain_ref[...]).astype(BF16)
-    sort_into(out_ref, held, pos_ref)
-
-
-def middle_rows(ctx, w_proj, tokens, gain, pos):
+        held[rows, :] = (normal * gain_two_ref[...]).astype(BF16)
+    local(mid, mid_hbm)
+    if small:
+        hop_came(1, 2)
+    x_sent = sort_and_send(held, x_sorted, x_hbm)
+    hand_on(g_sent, g_hbm)
+    if small:
+        hop_came(0, 3)
+        hop_came(1, 3)
+    hand_on(x_sent, x_hbm)
+    for copy in exchanged + own_over:
+        copy.wait()
+    if small:
+        for a in range(2):
+            for hop in (1, 2, 3):
+                hop_go(a, hop, finish=True)
+            for way, hop in HOPS:
+                origin = z - way * hop
+
+                @pl.when(valid(origin))
+                def _(a=a, way=way, hop=hop, origin=origin):
+                    pass_copy(a, way, hop, origin, y).wait_send()
+                    pass_copy(a, way, hop, origin, 1 - y).wait_recv()
+
+    for copy in waiting:
+        copy.wait()
+
+
+def front(small, lengths, pos, tokens, cot, gain_one, w_qkv, w_proj, gain_two, wi, wb):
+    vmem = pl.BlockSpec(memory_space=pltpu.VMEM)
+    any_space = pl.BlockSpec(memory_space=pl.ANY)
+    tiles = len(SORT_TILES)
+    copies = 6 * tiles + 2
+    dma = pltpu.SemaphoreType.DMA
     return pl.pallas_call(
-        middle_kernel,
+        functools.partial(front_kernel, small),
         out_shape=(
+            jax.ShapeDtypeStruct((ROWS, 3 * D), BF16),
+            jax.ShapeDtypeStruct((ROWS, D), BF16),
+            jax.ShapeDtypeStruct((SEQ_DEV, 16, 384), F32),
             jax.ShapeDtypeStruct((TOK_DEV, D), F32),
-            jax.ShapeDtypeStruct((SORTED, D), BF16),
+            jax.ShapeDtypeStruct((4, SORTED, D), BF16),
+            jax.ShapeDtypeStruct((4, SORTED, D), BF16),
+            jax.ShapeDtypeStruct((8, D, HALF), BF16),
+            jax.ShapeDtypeStruct((8, HALF, D), BF16),
         ),
-        scratch_shapes=[pltpu.VMEM((ROWS, D), BF16)],
-        compiler_params=params(),
-        cost_estimate=cost(2 * SORTED * ROWS * D + 2 * ROWS * D * D, 12 * ROWS * D),
-        name="middle",
-    )(ctx, w_proj, tokens, gain, pos)
-
-
-HALF = 384
-FF_DEV = 768
+        in_specs=[pl.BlockSpec(memory_space=pltpu.SMEM)] + [vmem] * 7 + [any_space] * 2,
+        out_specs=(any_space,) * 8,
+        scratch_shapes=[
+            pltpu.VMEM((ROWS, 3 * D), BF16),
+            pltpu.VMEM((ROWS, D), BF16),
+            pltpu.VMEM((SEQ_DEV, 16, 384), F32),
+            pltpu.VMEM((TOK_DEV, D), F32),
+            pltpu.VMEM((SORTED, D), BF16),
+            pltpu.VMEM((SORTED, D), BF16),
+            pltpu.VMEM((ROWS, D), BF16),
+            pltpu.VMEM((384, 128), F32),
+            dma((2 * tiles + 6,)),
+            dma((copies,)),
+            dma((copies,)),
+            dma((2, 6)),
+            dma((2, 6)),
+            dma((2, 6)),
+            dma((2, 6)),
+        ],
+        compiler_params=params(collective_id=1, has_side_effects=True),
+        name="front",
+    )(lengths, pos, tokens, cot, gain_one, w_qkv, w_proj, gain_two, wi, wb)
 
 
 def gelu_both(u):
@@ -285,7 +462,7 @@
 MERGED = 2 * SORTED + 256
 
 
-def expert_kernel(n_slots, carried, offs_ref, hosts_ref, *refs):
+def expert_kernel(carried, offs_ref, hosts_ref, *refs):
     refs = list(refs)
 
     def take(count):
@@ -294,7 +471,7 @@
         return head
 
     xs, gs = take(2), take(2)
-    wi_hbm, wb_hbm = take(1), take(n_slots)
+    wi_hbm, wb_hbm = take(2)
     before = take(2) if carried else None
     outs, gxs = take(2), take(2)
     dwi_ref, dwb_ref = take(2)
@@ -304,34 +481,17 @@
 
     def weight_copies(e, buffer, start):
         for p in range(2):
-            host = hosts_ref[e * 4 + p]
+            host = hosts_ref[e * 2 + p]
             part = pl.ds(p * HALF, HALF)
-            copy = pltpu.make_async_copy(
-                wi_hbm[0].at[host], wi.at[buffer, :, part], sems.at[buffer, p, 0]
-            )
-            if start:
-                copy.start()
-            else:
-                copy.wait()
-            if not start or n_slots == 1:
-                source = wb_hbm[0].at[host if n_slots == 1 else 0]
-                copy = pltpu.make_async_copy(
-                    source, wb.at[buffer, part, :], sems.at[buffer, p, 1]
-                )
+            for number, source, target in (
+                (0, wi_hbm.at[host], wi.at[buffer, :, part]),
+                (1, wb_hbm.at[host], wb.at[buffer, part, :]),
+            ):
+                copy = pltpu.make_async_copy(source, target, sems.at[buffer, p, number])
                 if start:
                     copy.start()
                 else:
                     copy.wait()
-            else:
-                for j in range(n_slots):
-
-                    slot = hosts_ref[e * 4 + 2 + p]
-
-                    @pl.when(slot // 2 == j)
-                    def _(j=j, slot=slot):
-                        pltpu.make_async_copy(
-                            wb_hbm[j].at[slot % 2], wb.at[buffer, part, :], sems.at[buffer, p, 1]
-                        ).start()
 
     @pl.when(expert == 0)
     def _():
@@ -375,8 +535,8 @@
         def gather(at, s=s, first=first, total=total):
             here = pl.ds(pl.multiple_of(first + at, 16), 16)
             there = pl.ds(pl.multiple_of(total + at, 16), 16)
-            xm[there, :] = xs[s][here, :]
-            gm[there, :] = gs[s][here, :]
+            xm[there, :] = xs[s][0, here, :]
+            gm[there, :] = gs[s][0, here, :]
 
         blocks(size // 16, gather)
         total = total + size
@@ -419,20 +579,26 @@
         blocks(count, hand_back)
 
 
-def experts(offs, hosts, xs, gs, wi, wb, before=None):
+def experts(sources, offs, hosts, x, g, wi, wb, before=None):
     whole = once((SORTED, D))
     any_space = pl.BlockSpec(memory_space=pl.ANY)
     weight = pl.BlockSpec((1, D, FF_DEV), lambda e, *_: (e, 0, 0))
     carried = before is not None
-    n_slots = len(wb)
     rows = jax.ShapeDtypeStruct((SORTED, D), BF16)
     grad = jax.ShapeDtypeStruct((EXPERTS, D, FF_DEV), BF16)
+
+    def source(i):
+        return pl.BlockSpec(
+            (1, SORTED, D), lambda e, *_: (i, 0, 0), pipeline_mode=pl.Buffered(1)
+        )
+
+    picked = [source(i) for i in sources]
     return pl.pallas_call(
-        functools.partial(expert_kernel, n_slots, carried),
+        functools.partial(expert_kernel, carried),
         grid_spec=pltpu.PrefetchScalarGridSpec(
             num_scalar_prefetch=2,
             grid=(EXPERTS,),
-            in_specs=[whole] * 4 + [any_space] * (1 + n_slots) + [weight] * (2 * carried),
+            in_specs=picked + picked + [any_space] * 2 + [weight] * (2 * carried),
             out_specs=[whole] * 4 + [weight] * 2,
             scratch_shapes=[
                 pltpu.VMEM((MERGED, D), BF16),
@@ -448,7 +614,7 @@
         compiler_params=params(),
         cost_estimate=cost(24 * SORTED * D * FF_DEV, 16 * SORTED * D),
         name="experts",
-    )(offs, hosts, *xs, *gs, wi, *wb, *(before or ()))
+    )(offs, hosts, x, x, g, g, wi, wb, *(before or ()))
 
 
 def unsort(pos_col, src):
@@ -936,39 +1102,26 @@
     wi_part = lax.dynamic_slice(w_in[0], (0, part * HALF), (D, HALF))
     wb_part = lax.dynamic_slice(w_back[0], (part * HALF, 0), (HALF, D))
     small = n_batch == 8
-    wi_all = lax.all_gather(wi_part, "batch", axis=0)
-    if small:
-        column = jnp.stack([wb_part, cross(wb_part, 1)])
-        wb_all = [column] + [cross(column, 2 * k) for k in (1, 2, 3)]
-        slots = hosts ^ own
-    else:
-        wb_all = [lax.all_gather(wb_part, "batch", axis=0)]
-        slots = hosts
-    hosts = jnp.stack([hosts.reshape(EXPERTS, 2), slots.reshape(EXPERTS, 2)], axis=1).reshape(-1)
 
     routes_row = jnp.pad(routes.reshape(1, TOK_DEV), ((0, 0), (0, LANES - TOK_DEV)))
     pos, offs = route_rows(routes_row, group_map)
     pos_col = pos.reshape(LANES, 1)[0:ROWS]
     offs_at = [o[0, 0:4] for o in spread(offs)]
 
-    grads_sorted = sort_rows(cotangent, pos)
-    g = spread(grads_sorted)
-    tokens = tie(tokens, grads_sorted)
-
-    qkv = qkv_rows(tokens, gain_one, w_qkv)
-    if small:
-        qkv = tie(qkv, column)
-    context, lse = attend(qkv, text_lengths)
-    context = tie(context, g[2], g[1], *(wb_all[1:2] if small else []))
-    middle, sending = middle_rows(context, w_proj, tokens, gain_two, pos)
-    x = spread(sending)
-
-    def run(pair, before):
+    qkv, context, lse, middle, g, x, wi_all, wb_all = front(
+        small, text_lengths, pos, tokens, cotangent, gain_one, w_qkv, w_proj, gain_two, wi_part, wb_part
+    )
+    if not small:
+        wi_all = lax.all_gather(wi_part, "batch", axis=0)
+        wb_all = lax.all_gather(wb_part, "batch", axis=0)
+
+    def run(pair, x, before):
         return experts(
+            pair,
             jnp.concatenate([offs_at[i] for i in pair]),
             hosts,
-            [x[i] for i in pair],
-            [g[i] for i in pair],
+            x,
+            g,
             wi_all,
             wb_all,
             before,
@@ -977,11 +1130,10 @@
     def add(a, b):
         return (a.astype(F32) + b.astype(F32)).astype(BF16)
 
-    out2, out3, gx2, gx3, dwi, dwb = run((2, 3), None)
+    out2, out3, gx2, gx3, dwi, dwb = run((2, 3), x, None)
     gx_half = add(gx2, swap(gx3, 1))
-    x[0] = tie(x[0], gx_half)
     gx_far = swap(gx_half, 2)
-    out0, out1, gx0, gx1, dwi, dwb = run((0, 1), (dwi, dwb))
+    out0, out1, gx0, gx1, dwi, dwb = run((0, 1), tie(x, gx_half), (dwi, dwb))
     gx_near = swap(gx1, 1)
     out_near = swap(out1, 1)
     out_far = swap(tie(add(out2, swap(out3, 1)), gx_far), 2)

time: 694 us -> 550 us (0.79)
  the two profiles are of different devices: /device:TPU:0 before, /device:TPU:9 now
where the time goes in v3:
time: 550 us; the launch traced here: 540 us
  Pallas kernels  404 us (73%)
  waiting for transfers between devices  57 us (10%)
  other arithmetic  27.9 us (5%)
  starting transfers between devices  19.4 us (4%)
  local copies, waits for them, and re-layouts  17.1 us (3%)
  between operations  15.3 us (3%)
    pallas_call x1, Pallas kernels, front(): pl.pallas_call(functools.partial(front_kernel, small), out_shape=(jax.Sha...  118 us
    pallas_call x1, Pallas kernels, total_over_all(): pl.pallas_call(total_kernel, out_shape=(jax.ShapeDtypeStruct((D, WIDE), B...  92 us
    pallas_call x2, Pallas kernels, experts(): pl.pallas_call(functools.partial(expert_kernel, carried), grid_spec=pltpu...  87.7 us
    ppermute x1, waiting for transfers between devices, cross(): return lax.ppermute(rows, 'batch', [(b, b ^ bits) for b in range(8)])  52.1 us
    pallas_call x1, Pallas kernels, attend_back(): pl.pallas_call(attend_back_kernel, grid=(SEQ_DEV,), out_shape=jax.ShapeDt...  38.9 us
    pallas_call x1, Pallas kernels, first_back(): pl.pallas_call(first_back_kernel, grid=(ROWS // TILE,), out_shape=(jax.Sh...  27.9 us
    pallas_call x1, Pallas kernels, back_rows(): pl.pallas_call(back_kernel, grid=(ROWS // TILE,), out_shape=(jax.ShapeDty...  22.7 us
    pallas_call x1, Pallas kernels, finish_rows(): pl.pallas_call(finish_kernel, grid=(ROWS // TILE,), out_shape=jax.ShapeDt...  11.2 us
  transfers between devices with their start and end apart: 13, of which 4 were waited for; matrix products, arithmetic and copies ran while one was open for 7% of the time, Pallas kernels for 58%

profile of v3, /device:TPU:9, one launch (start us, length us, event | category | flops | bytes accessed | tf_op | source)
XLA Modules:
  0.0 540.2 jit_solution(17111344500121162222)
XLA Ops:
  7.2 1.4 pad.4.routes_ref
  8.6 1.8 route.1
  13.7 1.9 fusion.2
  17.2 1.9 dynamic-slice_bitcast_fusion.2.wi_hbm
  19.1 1.3 reshape.69.gain_one_ref.gain_ref
  21.2 1.3 reshape.70.gain_two_ref.gain_ref
  23.2 117.7 %front.1 = (bf16[1584,2304]{1,0:T(8,128)(2,1)}, bf16[1584,768]{1,0:T(8,128)(2,1)}, f32[6,16,384]{2,1,0:T(8,128)}, f32[1566,768]{1,0:T(8,128)}, bf16[4,1616,768]{...) custom-call(s32[6]{0:T(128)} %len_ref.3, ...), custom_call_target="tpu_custom_call" | custom-call | tf_op jit(solution)/shard_map/front/pallas_call | solution.py:420
  142.7 43.5 %experts.2 = (bf16[1616,768]{1,0:T(8,128)(2,1)}, bf16[1616,768]{1,0:T(8,128)(2,1)}, bf16[1616,768]{1,0:T(8,128)(2,1)}, bf16[1616,768]{1,0:T(8,128)(2,1)}, bf16[3...) custom-call(s32[8]{0:T(128)} %pad_add_fusion.2.offs_ref, s32[6]{0:T(128)} %reshape.68.hosts_ref, ...), custom_call_target="tpu_custom_call" | custom-call | flops 22875734016 | bytes 19857408 | tf_op jit(solution)/shard_map/experts/pallas_call | solution.py:596
  186.8 3.5 collective-permute-done
  191.2 3.9 add_convert_fusion.1
  195.1 44.1 %experts.3 = (bf16[1616,768]{1,0:T(8,128)(2,1)}, bf16[1616,768]{1,0:T(8,128)(2,1)}, bf16[1616,768]{1,0:T(8,128)(2,1)}, bf16[1616,768]{1,0:T(8,128)(2,1)}, bf16[3...) custom-call(s32[8]{0:T(128)} %pad_add_fusion.1.offs_ref, s32[6]{0:T(128)} %reshape.68.hosts_ref, ...), custom_call_target="tpu_custom_call" | custom-call | flops 22875734016 | bytes 19857408 | tf_op jit(solution)/shard_map/experts/pallas_call | solution.py:596
  239.2 2.8 dynamic-slice_bitcast_fusion
  245.0 52.1 %collective-permute-done.9 = bf16[3,4,96,768]{3,2,1,0:T(8,128)(2,1)S(1)} collective-permute-done((bf16[3,4,96,768]{3,2,1,0:T(8,128)(2,1)}, bf16[3,4,96,768]{3,2,1,0:T(8,128)(2,1)S(1)}, u32[]{:S(2)}, u32[]{:S(2)}) %collective-permute-start.9) | collective-permute-done | bytes 1769504 | tf_op jit(solution)/shard_map/ppermute | solution.py:848
  297.1 1.9 fusion
  299.1 1.3 copy.32
  300.4 5.4 all-to-all-start
  305.8 2.1 collective-permute-start.5
  309.2 22.7 %back.1 = (f32[1566,768]{1,0:T(8,128)}, bf16[1584,768]{1,0:T(8,128)(2,1)}, bf16[768,768]{1,0:T(8,128)(2,1)}, f32[1,768]{1,0:T(1,128)}) custom-call(bf16[1616,768]{1,0:T(8,128)(2,1)} %get-tuple-element.61.a_ref, bf16[1616,768]{1,0:T(8,128)(2,1)} %collective-permute-done.8.b_ref, bf16[1616,768]{1,0:T(8,128)(2,1)} %collective-permute-done.6.c_ref, ...), custom_call_target="tpu_custom_call" | custom-call | flops 7668891648 | bytes 29196288 | tf_op jit(solution)/shard_map/back/pallas_call | solution.py:668
  331.9 38.9 %attend_back.1.gq_ref = bf16[1584,2304]{1,0:T(8,128)(2,1)} custom-call(s32[6]{0:T(128)} %len_ref.3, bf16[1584,2304]{1,0:T(8,128)(2,1)} %get-tuple-element.60.qkv_ref, bf16[1584,768]{1,0:T(8,128)(2,1)} %get-tuple-element.66.gctx_ref, f32[6,16,384]{2,1,0:T(8,128)} %get-tuple-element.67.lse_ref), custom_call_target="tpu_custom_call" | custom-call | flops 10192158720 | bytes 17031168 | tf_op jit(solution)/shard_map/attend_back/pallas_call | solution.py:770
  370.8 1.3 copy.33.back_ref
  372.1 3.6 deliver.1
  375.7 5.5 %all-to-all-start.1 = ((bf16[8,2,96,768]{3,2,1,0:T(8,128)(2,1)}), bf16[8,2,96,768]{3,2,1,0:T(8,128)(2,1)S(1)}, u32[]{:S(2)}, u32[]{:S(2)}) async-start(bf16[8,2,96,768]{3,2,1,0:T(8,128)(2,1)} %deliver.1), calls=%async_computation.2 | async-start | bytes 4718592 | tf_op jit(solution)/shard_map/all_to_all | solution.py:1156
  381.9 4.5 add_convert_fusion
  387.3 27.9 %first_back.1 = (f32[1566,768]{1,0:T(8,128)}, bf16[768,2304]{1,0:T(8,128)(2,1)}, f32[1,768]{1,0:T(1,128)}) custom-call(bf16[1566,768]{1,0:T(8,128)(2,1)} %tok_ref.3, f32[1,768]{1,0:T(1,128)} %reshape.69.gain_one_ref.gain_ref, bf16[1584,2304]{1,0:T(8,128)(2,1)} %attend_back.1.gq_ref, bf16[768,2304]{1,0:T(8,128)(2,1)} %w_ref.3, ...), custom_call_target="tpu_custom_call" | custom-call | flops 11211374592 | bytes 19464192 | tf_op jit(solution)/shard_map/first_back/pallas_call | solution.py:813
  415.2 1.4 maximum_maximum_fusion.gain_ref
  416.5 92.0 %total.1 = (bf16[768,3072]{1,0:T(8,128)(2,1)}, f32[8,768]{1,0:T(8,128)}) custom-call(bf16[768,2304]{1,0:T(8,128)(2,1)} %get-tuple-element.70.qkv_ref, bf16[768,768]{1,0:T(8,128)(2,1)} %get-tuple-element.71.proj_ref, f32[8,768]{1,0:T(8,128)} %maximum_maximum_fusion.gain_ref), custom_call_target="tpu_custom_call" | custom-call | tf_op jit(solution)/shard_map/total/pallas_call | solution.py:1054
  508.5 1.4 slice_reduce_fusion
  510.0 2.8 slice_convert_fusion.1
  512.8 5.5 %slice_convert_fusion = f32[768,2304]{1,0:T(8,128)} fusion(bf16[768,3072]{1,0:T(8,128)(2,1)} %get-tuple-element.75), kind=kLoop, calls=%fused_computation.4 | loop fusion | flops 1769472 | bytes 10616832 | tf_op jit(solution)/shard_map/convert_element_type | solution.py:1183
  518.3 11.2 %finish.1 = f32[1566,768]{1,0:T(8,128)} custom-call(bf16[1616,768]{1,0:T(8,128)(2,1)} %get-tuple-element.54.a_ref, bf16[1616,768]{1,0:T(8,128)(2,1)} %collective-permute-done.4.b_ref, bf16[1616,768]{1,0:T(8,128)(2,1)} %collective-permute-done.7.c_ref, s32[1584,1]{1,0:T(8,128)} %copy.30.pos_ref, f32[1566,768]{1,0:T(8,128)} %get-tuple-element.59.mid_ref), custom_call_target="tpu_custom_call" | custom-call | flops 3931766784 | bytes 17031168 | tf_op jit(solution)/shard_map/finish/pallas_call | solution.py:707
  529.7 1.6 convert.4
  531.3 1.6 convert.5
  (50 shorter events, 14.8 us)
Async XLA Ops:
  7.2 9.1 %copy-start = (bf16[1,768,768]{2,1,0:T(8,128)(2,1)S(1)}, bf16[1,768,768]{2,1,0:T(8,128)(2,1)}, u32[]{:S(2)}) copy-start(bf16[1,768,768]{2,1,0:T(8,128)(2,1)} %param.20) | copy-start | bytes 3538948
  7.2 364.9 %reduce-scatter.2.cloned.1.call-start = ((), (), s32[]{:S(2)}) async-start(), calls=%async_computation.3 | async-start | bytes 3981312 | tf_op jit(solution)/shard_map/reduce_scatter | solution.py:1141
  10.5 130.4 %collective-permute-start.1 = (s32[1,128]{1,0:T(1,128)}, s32[1,128]{1,0:T(1,128)S(1)}, u32[]{:S(2)}, u32[]{:S(2)}) collective-permute-start(s32[1,128]{1,0:T(1,128)} %get-tuple-element.43), channel_id=1, source_target_pairs={{0,2},{1,3},{2,0},{3,1},{4,6},{5,7},{6,4},{7,5},{8,10},{9,11},{10,... | collective-permute-start | bytes 1544 | tf_op jit(solution)/shard_map/ppermute | solution.py:838
  140.9 1.2 collective-permute-start.2
  142.7 43.8 %copy-start.4 = (s32[1,128]{1,0:T(1,128)S(1)}, s32[1,128]{1,0:T(1,128)}, u32[]{:S(2)}) copy-start(s32[1,128]{1,0:T(1,128)} %get-tuple-element.43) | copy-start | bytes 1540
  186.2 5.0 collective-permute-start.3
  186.5 3.8 collective-permute-start
  242.0 55.1 %collective-permute-start.9 = (bf16[3,4,96,768]{3,2,1,0:T(8,128)(2,1)}, bf16[3,4,96,768]{3,2,1,0:T(8,128)(2,1)S(1)}, u32[]{:S(2)}, u32[]{:S(2)}) collective-permute-start(bf16[3,4,96,768]{3,2,1,0:T(8,128)(2,1)} %dynamic-slice_bitcast_fusion), channel_id=1, source_target_pairs={{0,4},{4,0},{8,12},{12,8},{16,20},{20,16},{24,28},{28,24},{1,5},{5... | collective-permute-start | bytes 5308424 | tf_op jit(solution)/shard_map/ppermute | solution.py:848
  243.3 65.9 %collective-permute-start.8 = (bf16[1616,768]{1,0:T(8,128)(2,1)}, bf16[1616,768]{1,0:T(8,128)(2,1)}, u32[]{:S(2)}, u32[]{:S(2)}) collective-permute-start(bf16[1616,768]{1,0:T(8,128)(2,1)} %get-tuple-element.62), channel_id=1, source_target_pairs={{0,1},{1,0},{2,3},{3,2},{4,5},{5,4},{6,7},{7,6},{8,9},{9,8},{10,11... | collective-permute-start | bytes 7446536 | tf_op jit(solution)/shard_map/ppermute | solution.py:838
  243.8 65.4 %collective-permute-start.6 = (bf16[1616,768]{1,0:T(8,128)(2,1)}, bf16[1616,768]{1,0:T(8,128)(2,1)}, u32[]{:S(2)}, u32[]{:S(2)}) collective-permute-start(bf16[1616,768]{1,0:T(8,128)(2,1)} %add_convert_fusion.1), channel_id=1, source_target_pairs={{0,2},{1,3},{2,0},{3,1},{4,6},{5,7},{6,4},{7,5},{8,10},{9,11},{10,... | collective-permute-start | bytes 7446536 | tf_op jit(solution)/shard_map/ppermute | solution.py:838
  300.4 7.5 %copy-start.2 = (s32[1,1664]{1,0:T(1,128)S(1)}, s32[1,1664]{1,0:T(1,128)}, u32[]{:S(2)}) copy-start(s32[1,1664]{1,0:T(1,128)} %get-tuple-element.44.pos_ref) | copy-start | bytes 19972
  300.4 70.3 %all-to-all-start = ((bf16[3,4,96,768]{3,2,0,1:T(8,128)(2,1)}), bf16[3,4,96,768]{3,2,0,1:T(8,128)(2,1)S(1)}, u32[]{:S(2)}, u32[]{:S(2)}) async-start(bf16[3,4,96,768]{3,2,0,1:T(8,128)(2,1)} %copy.32), calls=%async_computation.1 | async-start | bytes 3538944 | tf_op jit(solution)/shard_map/all_to_all | solution.py:891
  305.8 76.1 %collective-permute-start.5 = (bf16[1616,768]{1,0:T(8,128)(2,1)}, bf16[1616,768]{1,0:T(8,128)(2,1)}, u32[]{:S(2)}, u32[]{:S(2)}) collective-permute-start(bf16[1616,768]{1,0:T(8,128)(2,1)} %get-tuple-element.57), channel_id=1, source_target_pairs={{0,1},{1,0},{2,3},{3,2},{4,5},{5,4},{6,7},{7,6},{8,9},{9,8},{10,11... | collective-permute-start | bytes 7446536 | tf_op jit(solution)/shard_map/ppermute | solution.py:838
  375.7 153.8 %all-to-all-start.1 = ((bf16[8,2,96,768]{3,2,1,0:T(8,128)(2,1)}), bf16[8,2,96,768]{3,2,1,0:T(8,128)(2,1)S(1)}, u32[]{:S(2)}, u32[]{:S(2)}) async-start(bf16[8,2,96,768]{3,2,1,0:T(8,128)(2,1)} %deliver.1), calls=%async_computation.2 | async-start | bytes 4718592 | tf_op jit(solution)/shard_map/all_to_all | solution.py:1156
  381.4 136.9 %collective-permute-start.4 = (bf16[1616,768]{1,0:T(8,128)(2,1)}, bf16[1616,768]{1,0:T(8,128)(2,1)}, u32[]{:S(2)}, u32[]{:S(2)}) collective-permute-start(bf16[1616,768]{1,0:T(8,128)(2,1)} %get-tuple-element.55), channel_id=1, source_target_pairs={{0,1},{1,0},{2,3},{3,2},{4,5},{5,4},{6,7},{7,6},{8,9},{9,8},{10,11... | collective-permute-start | bytes 7446536 | tf_op jit(solution)/shard_map/ppermute | solution.py:838
  386.4 131.9 %collective-permute-start.7 = (bf16[1616,768]{1,0:T(8,128)(2,1)}, bf16[1616,768]{1,0:T(8,128)(2,1)}, u32[]{:S(2)}, u32[]{:S(2)}) collective-permute-start(bf16[1616,768]{1,0:T(8,128)(2,1)} %add_convert_fusion), channel_id=1, source_target_pairs={{0,2},{1,3},{2,0},{3,1},{4,6},{5,7},{6,4},{7,5},{8,10},{9,11},{10,... | collective-permute-start | bytes 7446536 | tf_op jit(solution)/shard_map/ppermute | solution.py:838
  387.3 27.9 %copy-start.3 = (f32[1,768]{1,0:T(1,128)S(1)}, f32[1,768]{1,0:T(1,128)}, u32[]{:S(2)}) copy-start(f32[1,768]{1,0:T(1,128)} %get-tuple-element.73) | copy-start | bytes 9220
  529.7 3.2 copy-start.1
Sparse Core Ops, SparseCore 0:
  239.3 115.3 reduce-scatter.1

commit v4 on v3

--- a/solution.py
+++ b/solution.py
@@ -617,124 +617,81 @@
     )(offs, hosts, x, x, g, g, wi, wb, *(before or ()))
 
 
+def swap(rows, bit):
+    pairs = [(f, f ^ bit) for f in range(4)]
+    return lax.ppermute(rows, "ffn", pairs)
+
+
+def spread(rows):
+    near = swap(rows, 1)
+    far = swap(rows, 2)
+    return [rows, near, far, swap(far, 1)]
+
+
+def tie(value, *others):
+    return lax.optimization_barrier((value, *others))[0]
+
+
+class Wire:
+    def __init__(self, send_sems, recv_sems):
+        self.send_sems, self.recv_sems, self.used = send_sems, recv_sems, 0
+
+    def send(self, src, dst, device):
+        number = self.used
+        self.used += 1
+        copy = pltpu.make_async_remote_copy(
+            src_ref=src,
+            dst_ref=dst,
+            send_sem=self.send_sems.at[number],
+            recv_sem=self.recv_sems.at[number],
+            device_id=device,
+            device_id_type=MESH,
+        )
+        copy.start()
+        return copy
+
+
+class Mover:
+    def __init__(self, sems):
+        self.sems, self.used = sems, 0
+
+    def go(self, src, dst):
+        number = self.used
+        self.used += 1
+        copy = pltpu.make_async_copy(src, dst, self.sems.at[number])
+        copy.start()
+        return copy
+
+
+def greet(peers):
+    barrier = pltpu.get_barrier_semaphore()
+    for device in peers:
+        pl.semaphore_signal(barrier, inc=1, device_id=device, device_id_type=MESH)
+    pl.semaphore_wait(barrier, len(peers))
+
+
+def wait_all(copies):
+    for copy in copies:
+        copy.wait()
+
+
+def token_tiles():
+    for i in range(3):
+        yield slice(TILE * i, min(TILE * (i + 1), TOK_DEV))
+
+
 def unsort(pos_col, src):
     want = lax.broadcasted_iota(I32, (pos_col.shape[0], SORTED), 1)
     hot = jnp.where(pos_col == want, 1.0, 0.0).astype(BF16)
     return dot(hot, src)
 
 
-def back_kernel(
-    a_ref,
-    b_ref,
-    c_ref,
-    pos_ref,
-    mid_ref,
-    cot_ref,
-    gain_ref,
-    ctx_ref,
-    w_ref,
-    gm_ref,
-    gctx_ref,
-    dw_ref,
-    dg_ref,
-    total,
-    acc,
-):
-    step = pl.program_id(0)
-
-    @pl.when(step == 0)
-    def _():
-        both = a_ref[...].astype(F32) + b_ref[...].astype(F32) + c_ref[...].astype(F32)
-        total[...] = both.astype(BF16)
-        acc[...] = jnp.zeros_like(acc)
-        dg_ref[...] = jnp.zeros_like(dg_ref)
-
-    keep = row_mask(step * TILE, TILE, TOK_DEV)
-    grad_normed = unsort(pos_ref[...], total[...])
-    middle = jnp.where(keep, mid_ref[...], 0.0)
-    normal, inverse = norm_parts(middle)
-    dg_ref[...] += jnp.sum(grad_normed * normal, axis=0, keepdims=True)
-    part = norm_pull(grad_normed, gain_ref[...], normal, inverse)
-    grad_middle = jnp.where(keep, cot_ref[...].astype(F32) + part, 0.0)
-    gm_ref[...] = grad_middle
-    low = grad_middle.astype(BF16)
-    acc[...] += dot(ctx_ref[...], low, CONTRACT_ROWS)
-    dw_ref[...] = acc[...].astype(BF16)
-    gctx_ref[...] = dot(low, w_ref[...], CONTRACT_LANES).astype(BF16)
-
-
-def back_rows(a, b, c, pos_col, middle, cot, gain, ctx, w_proj):
-    tile = pl.BlockSpec((TILE, D), lambda i: (i, 0))
-    return pl.pallas_call(
-        back_kernel,
-        grid=(ROWS // TILE,),
-        out_shape=(
-            jax.ShapeDtypeStruct((TOK_DEV, D), F32),
-            jax.ShapeDtypeStruct((ROWS, D), BF16),
-            jax.ShapeDtypeStruct((D, D), BF16),
-            jax.ShapeDtypeStruct((1, D), F32),
-        ),
-        in_specs=[
-            once((SORTED, D)),
-            once((SORTED, D)),
-            once((SORTED, D)),
-            pl.BlockSpec((TILE, 1), lambda i: (i, 0)),
-            tile,
-            tile,
-            full((1, D)),
-            tile,
-            once((D, D)),
-        ],
-        out_specs=(tile, tile, full((D, D)), full((1, D))),
-        scratch_shapes=[pltpu.VMEM((SORTED, D), BF16), pltpu.VMEM((D, D), F32)],
-        compiler_params=params(),
-        cost_estimate=cost(2 * ROWS * D * (SORTED + 2 * D), 24 * ROWS * D),
-        name="back",
-    )(a, b, c, pos_col, middle, cot, gain, ctx, w_proj)
-
-
-def finish_kernel(a_ref, b_ref, c_ref, pos_ref, mid_ref, out_ref, total):
-    @pl.when(pl.program_id(0) == 0)
-    def _():
-        both = a_ref[...].astype(F32) + b_ref[...].astype(F32) + c_ref[...].astype(F32)
-        total[...] = both.astype(BF16)
-
-    out_ref[...] = mid_ref[...] + unsort(pos_ref[...], total[...])
-
-
-def finish_rows(a, b, c, pos_col, middle):
-    tile = pl.BlockSpec((TILE, D), lambda i: (i, 0))
-    return pl.pallas_call(
-        finish_kernel,
-        grid=(ROWS // TILE,),
-        out_shape=jax.ShapeDtypeStruct((TOK_DEV, D), F32),
-        in_specs=[
-            once((SORTED, D)),
-            once((SORTED, D)),
-            once((SORTED, D)),
-            pl.BlockSpec((TILE, 1), lambda i: (i, 0)),
-            tile,
-        ],
-        out_specs=tile,
-        scratch_shapes=[pltpu.VMEM((SORTED, D), BF16)],
-        compiler_params=params(),
-        cost_estimate=cost(2 * ROWS * D * SORTED, 14 * ROWS * D),
-        name="finish",
-    )(a, b, c, pos_col, middle)
-
-
-def attend_back_kernel(len_ref, qkv_ref, gctx_ref, lse_ref, out_ref):
-    pair = pl.program_id(0)
+def attend_back_pair(pair, length, qkv_ref, gctx_ref, lse_ref, out_ref):
     start, skip = window(pair)
     start = pl.multiple_of(start, 16)
-
-    @pl.when(pair == 0)
-    def _():
-        out_ref[...] = jnp.zeros_like(out_ref)
-
     row = lax.broadcasted_iota(I32, (WIN, 1), 0)
     mine = (row >= skip) & (row < skip + SEQ_LEN)
-    bias = jnp.where((row >= skip) & (row < skip + PATCHES + len_ref[pair]), 0.0, -1e30)
+    bias = jnp.where((row >= skip) & (row < skip + PATCHES + length), 0.0, -1e30)
     lane = lax.broadcasted_iota(I32, (WIN, 128), 1)
     scale = jnp.asarray(HEAD_DIM**-0.5, BF16)
     for hp in range(HEADS // 2):
@@ -752,7 +709,7 @@
             qh = jnp.where(inside, q, jnp.zeros_like(q))
             gh = jnp.where(inside, go, jnp.zeros_like(go))
             scores = dot(k, qh, CONTRACT_LANES)
-            probs = jnp.exp(scores + bias - lse_ref[0, head : head + 1, 0:WIN])
+            probs = jnp.exp(scores + bias - lse_ref[pair, head : head + 1, 0:WIN])
             grad_probs = dot(v, gh, CONTRACT_LANES)
             delta = jnp.sum(probs * grad_probs, axis=0, keepdims=True)
             grad_scores = (probs * (grad_probs - delta)).astype(BF16)
@@ -766,147 +723,283 @@
             out_ref[pl.ds(start, WIN), spot] = jnp.where(mine, new, old)
 
 
-def attend_back(qkv, gctx, lse, lengths):
+CHUNK = D // 8
+TURNS = (2, 3, 1, 0)
+
+
+def rear_kernel(
+    small,
+    len_ref,
+    pos_ref,
+    gain_one_ref,
+    gain_two_ref,
+    w_ref,
+    lse_ref,
+    gx0_hbm,
+    gx1_hbm,
+    gx2_hbm,
+    mid_hbm,
+    cot_hbm,
+    ctx_hbm,
+    qkv_hbm,
+    tok_hbm,
+    out1_hbm,
+    out2_hbm,
+    out3_hbm,
+    dwi_hbm,
+    dwb_hbm,
+    gm_hbm,
+    gq_hbm,
+    dwq_hbm,
+    dwp_hbm,
+    dg_ref,
+    share_hbm,
+    near_hbm,
+    far_hbm,
+    wide,
+    mid,
+    cot,
+    ctx,
+    gctx,
+    qkv,
+    half_a,
+    half_b,
+    own_rows,
+    came_y,
+    came_z,
+    acc,
+    dwp,
+    local_sems,
+    send_sems,
+    recv_sems,
+    z_send,
+    z_recv,
+):
+    batch, ffn = lax.axis_index("batch"), lax.axis_index("ffn")
+    z, y = batch // 2, batch % 2
+    near, far, across = (batch, ffn ^ 1), (batch, ffn ^ 2), (batch ^ 1, ffn)
+    along = {k: (batch ^ (2 * k), ffn) for k in (1, 2, 3)}
+    greet([near, far] + ([across] + list(along.values()) if small else []))
+    wire, mover = Wire(send_sems, recv_sems), Mover(local_sems)
+
+    parts_near = wire.send(gx1_hbm, wide.at[:, D : 2 * D], near)
+    near_sent = wire.send(out3_hbm, half_b, near)
+    half_in = mover.go(out2_hbm, half_a)
+    over_y = {}
+    own_in = {}
+    if small:
+        for turn in TURNS:
+            there = pl.ds(pl.multiple_of(((z ^ turn) * 2 + 1 - y) * CHUNK, 16), CHUNK)
+            over_y[turn] = [
+                wire.send(grad.at[:, there, :], came_y.at[turn, i], across)
+                for i, grad in enumerate((dwi_hbm, dwb_hbm))
+            ]
+    parts_in = [
+        mover.go(part, wide.at[:, i * D : i * D + D])
+        for i, part in ((0, gx0_hbm), (2, gx2_hbm))
+    ]
+    rows_in = [mover.go(mid_hbm, mid), mover.go(cot_hbm, cot), mover.go(ctx_hbm, ctx)]
+    qkv_in = mover.go(qkv_hbm, qkv)
+    if small:
+        for turn in TURNS:
+            here = pl.ds(pl.multiple_of(((z ^ turn) * 2 + y) * CHUNK, 16), CHUNK)
+            own_in[turn] = [
+                mover.go(grad.at[:, here, :], own_rows.at[turn, i])
+                for i, grad in enumerate((dwi_hbm, dwb_hbm))
+            ]
+    sent = [wire.send(out1_hbm, near_hbm, near)]
+    stored = []
+
+    def z_copy(turn, i):
+        return pltpu.make_async_remote_copy(
+            src_ref=came_y.at[turn, i],
+            dst_ref=came_z.at[turn - 1, i],
+            send_sem=z_send.at[turn - 1, i],
+            recv_sem=z_recv.at[turn - 1, i],
+            device_id=along[turn],
+            device_id_type=MESH,
+        )
+
+    def take_turn(turn, i):
+        if not small:
+            return
+        over_y[turn][i].wait()
+        own_in[turn][i].wait()
+        for e in range(EXPERTS):
+            came_y[turn, i, e] = (
+                came_y[turn, i, e].astype(F32) + own_rows[turn, i, e].astype(F32)
+            ).astype(BF16)
+        if turn:
+            z_copy(turn, i).start()
+
+    wait_all(parts_in + rows_in + [parts_near])
+    top = 0
+    for size in SORT_TILES:
+        rows = slice(top, top + size)
+        wide[rows, 0:D] = (
+            wide[rows, 0:D].astype(F32)
+            + wide[rows, D : 2 * D].astype(F32)
+            + wide[rows, 2 * D : 3 * D].astype(F32)
+        ).astype(BF16)
+        top += size
+    half_in.wait()
+    near_sent.wait()
+    half_a[...] = (half_a[...].astype(F32) + half_b[...].astype(F32)).astype(BF16)
+    sent.append(wire.send(half_a, far_hbm, far))
+
+    gctx[1552:ROWS, :] = jnp.zeros((ROWS - 1552, D), BF16)
+    grad_gain = jnp.zeros((1, D), F32)
+    for i, rows in enumerate(token_tiles()):
+        grad_normed = unsort(pos_ref[rows, :], wide[:, 0:D])
+        normal, inverse = norm_parts(mid[rows, :])
+        grad_gain = grad_gain + jnp.sum(grad_normed * normal, axis=0, keepdims=True)
+        part = norm_pull(grad_normed, gain_two_ref[...], normal, inverse)
+        grad_middle = cot[rows, :].astype(F32) + part
+        mid[rows, :] = grad_middle
+        low = grad_middle.astype(BF16)
+        product = dot(ctx[rows, :], low, CONTRACT_ROWS)
+        if i == 0:
+            acc[...] = product
+        elif i == 1:
+            acc[...] += product
+        else:
+            dwp[...] = (acc[...] + product).astype(BF16)
+        gctx[rows, :] = dot(low, w_ref[...], CONTRACT_LANES).astype(BF16)
+        if i < 2:
+            take_turn(2, i)
+    dg_ref[...] = grad_gain
+    stored.append(mover.go(mid, gm_hbm))
+    stored.append(mover.go(dwp, dwp_hbm))
+    tok_in = mover.go(tok_hbm, cot)
+    wide[1552:SORTED, :] = jnp.zeros((SORTED - 1552, 3 * D), BF16)
+    qkv_in.wait()
+    take_turn(3, 0)
+
+    @pl.loop(0, SEQ_DEV)
+    def _(pair):
+        attend_back_pair(pair, len_ref[pair], qkv, gctx, lse_ref, wide)
+        for when, turn, i in ((1, 3, 1), (3, 1, 0), (4, 1, 1)):
+
+            @pl.when(pair == when)
+            def _(turn=turn, i=i):
+                take_turn(turn, i)
+
+    stored.append(mover.go(wide.at[0:ROWS, :], gq_hbm))
+    tok_in.wait()
+    for rows in token_tiles():
+        normal, _ = norm_parts(cot[rows, :].astype(F32))
+        gctx[rows, :] = (normal * gain_one_ref[...]).astype(BF16)
+    for i in range(3):
+        cols = slice(i * D, i * D + D)
+        qkv[0:D, cols] = dot(gctx[...], wide[0:ROWS, cols], CONTRACT_ROWS).astype(BF16)
+    stored.append(mover.go(qkv.at[0:D, :], dwq_hbm))
+    if small:
+        take_turn(0, 0)
+        take_turn(0, 1)
+        wait_all([z_copy(turn, i) for turn in TURNS[:3] for i in range(2)])
+        for i in range(2):
+            for e in range(EXPERTS):
+                total = came_y[0, i, e].astype(F32)
+                for k in range(3):
+                    total = total + came_z[k, i, e].astype(F32)
+                came_y[0, i, e] = total.astype(BF16)
+        stored.append(mover.go(came_y.at[0], share_hbm))
+    wait_all(sent + stored)
+
+
+def rear(small, lengths, pos_col, gain_one, gain_two, w_proj, lse, *arrays):
+    vmem = pl.BlockSpec(memory_space=pltpu.VMEM)
+    any_space = pl.BlockSpec(memory_space=pl.ANY)
+    dma = pltpu.SemaphoreType.DMA
+    copies = 12
     return pl.pallas_call(
-        attend_back_kernel,
-        grid=(SEQ_DEV,),
-        out_shape=jax.ShapeDtypeStruct((ROWS, 3 * D), BF16),
-        in_specs=[
-            pl.BlockSpec(memory_space=pltpu.SMEM),
-            once((ROWS, 3 * D)),
-            once((ROWS, D)),
-            pl.BlockSpec((1, 16, 384), lambda s: (s, 0, 0)),
-        ],
-        out_specs=full((ROWS, 3 * D)),
-        compiler_params=params(),
-        cost_estimate=cost(72 * 10 * WIN * 384 * 128, 2 * ROWS * D * 7),
-        name="attend_back",
-    )(lengths, qkv, gctx, lse)
-
-
-def first_back_kernel(tok_ref, gain_ref, gq_ref, w_ref, gm_ref, ig_ref, dw_ref, dg_ref, acc):
-    step = pl.program_id(0)
-
-    @pl.when(step == 0)
-    def _():
-        acc[...] = jnp.zeros_like(acc)
-        dg_ref[...] = jnp.zeros_like(dg_ref)
-
-    keep = row_mask(step * TILE, TILE, TOK_DEV)
-    tokens = jnp.where(keep, tok_ref[...].astype(F32), 0.0)
-    normal, inverse = norm_parts(tokens)
-    normed = (normal * gain_ref[...]).astype(BF16)
-    grad_qkv = gq_ref[...]
-    acc[...] += dot(normed, grad_qkv, CONTRACT_ROWS)
-
-    @pl.when(step == ROWS // TILE - 1)
-    def _():
-        dw_ref[...] = acc[...].astype(BF16)
-
-    grad_normed = dot(grad_qkv, w_ref[...], CONTRACT_LANES)
-    dg_ref[...] += jnp.sum(grad_normed * normal, axis=0, keepdims=True)
-    ig_ref[...] = gm_ref[...] + norm_pull(grad_normed, gain_ref[...], normal, inverse)
-
-
-def first_back(tokens, gain, grad_qkv, w_qkv, grad_middle):
-    tile = pl.BlockSpec((TILE, D), lambda i: (i, 0))
-    return pl.pallas_call(
-        first_back_kernel,
-        grid=(ROWS // TILE,),
+        functools.partial(rear_kernel, small),
         out_shape=(
             jax.ShapeDtypeStruct((TOK_DEV, D), F32),
+            jax.ShapeDtypeStruct((ROWS, 3 * D), BF16),
             jax.ShapeDtypeStruct((D, 3 * D), BF16),
+            jax.ShapeDtypeStruct((D, D), BF16),
             jax.ShapeDtypeStruct((1, D), F32),
+            jax.ShapeDtypeStruct((2, EXPERTS, CHUNK, D), BF16),
+            jax.ShapeDtypeStruct((SORTED, D), BF16),
+            jax.ShapeDtypeStruct((SORTED, D), BF16),
         ),
-        in_specs=[
-            tile,
-            full((1, D)),
-            pl.BlockSpec((TILE, 3 * D), lambda i: (i, 0)),
-            once((D, 3 * D)),
-            tile,
+        in_specs=[pl.BlockSpec(memory_space=pltpu.SMEM)] + [vmem] * 5 + [any_space] * len(arrays),
+        out_specs=(any_space,) * 4 + (vmem,) + (any_space,) * 3,
+        scratch_shapes=[
+            pltpu.VMEM((SORTED, 3 * D), BF16),
+            pltpu.VMEM((TOK_DEV, D), F32),
+            pltpu.VMEM((TOK_DEV, D), BF16),
+            pltpu.VMEM((ROWS, D), BF16),
+            pltpu.VMEM((ROWS, D), BF16),
+            pltpu.VMEM((ROWS, 3 * D), BF16),
+            pltpu.VMEM((SORTED, D), BF16),
+            pltpu.VMEM((SORTED, D), BF16),
+            pltpu.VMEM((4, 2, EXPERTS, CHUNK, D), BF16),
+            pltpu.VMEM((4, 2, EXPERTS, CHUNK, D), BF16),
+            pltpu.VMEM((3, 2, EXPERTS, CHUNK, D), BF16),
+            pltpu.VMEM((D, D), F32),
+            pltpu.VMEM((D, D), BF16),
+            dma((24,)),
+            dma((copies,)),
+            dma((copies,)),
+            dma((3, 2)),
+            dma((3, 2)),
         ],
-        out_specs=(tile, full((D, 3 * D)), full((1, D))),
-        scratch_shapes=[pltpu.VMEM((D, 3 * D), F32)],
-        compiler_params=params(),
-        cost_estimate=cost(4 * ROWS * D * 3 * D, 16 * ROWS * D),
-        name="first_back",
-    )(tokens, gain, grad_qkv, w_qkv, grad_middle)
-
-
-def swap(rows, bit):
-    pairs = [(f, f ^ bit) for f in range(4)]
-    return lax.ppermute(rows, "ffn", pairs)
-
-
-def spread(rows):
-    near = swap(rows, 1)
-    far = swap(rows, 2)
-    return [rows, near, far, swap(far, 1)]
-
-
-def cross(rows, bits):
-    return lax.ppermute(rows, "batch", [(b, b ^ bits) for b in range(8)])
-
-
-def tie(value, *others):
-    return lax.optimization_barrier((value, *others))[0]
-
-
-CHUNK = D // 8
-
-
-Z_GROUPS = [[0, 2, 4, 6], [1, 3, 5, 7]]
-
-
-def deliver_kernel(gm_ref, in_ref, back_ref, out_ref):
-    for b in range(8):
-        e = gm_ref[b]
-        out_ref[b, 0] = in_ref[e]
-        total = sum(back_ref[e, z].astype(F32) for z in range(4))
-        out_ref[b, 1] = total.astype(BF16)
-
-
-def deliver(grad_in, grad_back, group_map):
-    vmem = pl.BlockSpec(memory_space=pltpu.VMEM)
-    return pl.pallas_call(
-        deliver_kernel,
-        out_shape=jax.ShapeDtypeStruct((8, 2, CHUNK, D), BF16),
-        in_specs=[pl.BlockSpec(memory_space=pltpu.SMEM), vmem, vmem],
-        out_specs=vmem,
-        compiler_params=params(),
-        cost_estimate=cost(0, 6 << 20),
-        name="deliver",
-    )(group_map, grad_in, grad_back)
-
-
-def cross_y(dwb, own):
-    y = own % 2
-    cut = dwb.reshape(EXPERTS, 4, 2, CHUNK, D)
-    there = cross(lax.dynamic_index_in_dim(cut, 1 - y, 2, keepdims=False), 1)
-    mine = lax.dynamic_index_in_dim(cut, y, 2, keepdims=False)
-    return (mine.astype(F32) + there.astype(F32)).astype(BF16)
-
-
-def cross_z(rows):
-    return lax.all_to_all(
-        rows, "batch", split_axis=1, concat_axis=1, axis_index_groups=Z_GROUPS, tiled=True
-    )
-
-
-AXES = ("x", "y", "z")
-ORDERS = (("x", "y", "z"), ("y", "z", "x"), ("z", "x", "y"))
+        compiler_params=params(collective_id=2, has_side_effects=True),
+        name="rear",
+    )(lengths, pos_col, gain_one, gain_two, w_proj, lse, *arrays)
+
+
+ORDERS = (("x", "y", "z"), ("y", "x", "z"))
 WIDE = 4 * D
-COLOUR = WIDE // 3
+COLOUR = WIDE // 2
 QUARTER = COLOUR // 4
 GAIN_ROWS = 8
 
 
-def total_kernel(
-    qkv_ref, proj_ref, gain_ref, out_ref, gain_out_ref, near, held, came, gain_in, send_sems, recv_sems
+def last_kernel(
+    small,
+    group_ref,
+    pos_ref,
+    gain_ref,
+    w_ref,
+    dg_two_ref,
+    tok_hbm,
+    gq_hbm,
+    gm_hbm,
+    mid_hbm,
+    out0_hbm,
+    out1_hbm,
+    out2_hbm,
+    dwq_hbm,
+    dwp_hbm,
+    share_hbm,
+    ig_hbm,
+    bo_hbm,
+    sum_ref,
+    gains_ref,
+    pieces_ref,
+    tok,
+    gq,
+    gm,
+    mid,
+    outs,
+    share,
+    stage,
+    near_rows,
+    held,
+    came_z,
+    came_xy,
+    gain_in,
+    local_sems,
+    send_sems,
+    recv_sems,
 ):
     batch, ffn = lax.axis_index("batch"), lax.axis_index("ffn")
     z, y, x, c = batch // 2, batch % 2, ffn // 2, ffn % 2
     place = {"x": x, "y": y, "z": z}
+    mover = Mover(local_sems)
 
     def peer(axis, k=1):
         if axis == "c":
@@ -917,122 +1010,103 @@
             return (batch ^ 1, ffn)
         return (batch ^ (2 * k), ffn)
 
-    peers = [peer("c"), peer("x"), peer("y")] + [peer("z", k) for k in (1, 2, 3)]
-    barrier = pltpu.get_barrier_semaphore()
-    for device in peers:
-        pl.semaphore_signal(barrier, inc=1, device_id=device, device_id_type=pl.DeviceIdType.MESH)
-    pl.semaphore_wait(barrier, len(peers))
-
-    used = [0]
-
-    def send(src, dst, device):
-        number = used[0]
-        used[0] += 1
-        copy = pltpu.make_async_remote_copy(
-            src_ref=src,
-            dst_ref=dst,
-            send_sem=send_sems.at[number],
-            recv_sem=recv_sems.at[number],
-            device_id=device,
-            device_id_type=pl.DeviceIdType.MESH,
-        )
-        copy.start()
-        return copy
-
-    give = pl.ds(pl.multiple_of((1 - c) * 384, 16), 384)
-    keep = pl.ds(pl.multiple_of(c * 384, 16), 384)
-    first = [
-        send(qkv_ref.at[give, :], near.at[:, 0 : 3 * D], peer("c")),
-        send(proj_ref.at[give, :], near.at[:, 3 * D : WIDE], peer("c")),
-        send(gain_ref, gain_in.at[0], peer("c")),
+    flying = []
+    top = [0, 0]
+    left = [COLOUR * i for i in range(2)]
+    rows, cols = [384] * 2, [COLOUR] * 2
+    base = pl.multiple_of(c * 384, 16)
+    if small:
+        greet([peer("c"), peer("x")] + [(batch ^ j, ffn) for j in range(1, 8)])
+        wire = Wire(send_sems, recv_sems)
+        share_in = mover.go(share_hbm, share)
+        give = pl.ds(pl.multiple_of((1 - c) * 384, 16), 384)
+        keep = pl.ds(base, 384)
+        to_core = [
+            wire.send(dwq_hbm.at[give, :], near_rows.at[:, 0 : 3 * D], peer("c")),
+            wire.send(dwp_hbm.at[give, :], near_rows.at[:, 3 * D : WIDE], peer("c")),
+        ]
+        kept = [
+            mover.go(dwq_hbm.at[keep, :], held.at[:, 0 : 3 * D]),
+            mover.go(dwp_hbm.at[keep, :], held.at[:, 3 * D : WIDE]),
+        ]
+    loads = [mover.go(tok_hbm, tok), mover.go(gq_hbm, gq), mover.go(gm_hbm, gm)]
+    later = [mover.go(mid_hbm, mid)] + [
+        mover.go(part, outs.at[i]) for i, part in enumerate((out0_hbm, out1_hbm, out2_hbm))
     ]
-    for copy in first:
-        copy.wait()
-    held[:, 0 : 3 * D] = (
-        qkv_ref[keep, :].astype(F32) + near[:, 0 : 3 * D].astype(F32)
-    ).astype(BF16)
-    held[:, 3 * D : WIDE] = (
-        proj_ref[keep, :].astype(F32) + near[:, 3 * D : WIDE].astype(F32)
-    ).astype(BF16)
-    gain_out_ref[...] = gain_ref[...] + gain_in[0]
-
-    top = [0, 0, 0]
-    left = [COLOUR * i for i in range(3)]
-    rows, cols = [384] * 3, [COLOUR] * 3
-    gain_slot = 1
-    for step in range(3):
-        flying = []
-        for i in range(3):
+    handed = []
+    if small:
+        share_in.wait()
+        for j in range(8):
+            expert = group_ref[batch ^ j]
+            for i in range(2):
+                stage[j, i] = share[i, expert]
+            if j:
+                handed.append(wire.send(stage.at[j], pieces_ref.at[batch], (batch ^ j, ffn)))
+        pieces_ref[batch] = stage[0]
+
+    def core_done():
+        wait_all(to_core + kept)
+        for i in range(4):
+            lanes = slice(i * D, i * D + D)
+            held[:, lanes] = (
+                held[:, lanes].astype(F32) + near_rows[:, lanes].astype(F32)
+            ).astype(BF16)
+
+    def sum_go(step):
+        for i in range(2):
             axis = ORDERS[i][step]
             if axis == "z":
+                live = pl.ds(top[i], rows[i])
                 for k in (1, 2, 3):
                     there = pl.ds(pl.multiple_of(left[i] + (z ^ k) * QUARTER, 128), QUARTER)
-                    live = pl.ds(top[i], rows[i])
                     flying.append(
-                        send(
-                            held.at[live, there],
-                            came.at[i, k - 1, 0 : rows[i], 0:QUARTER],
-                            peer("z", k),
+                        wire.send(
+                            held.at[live, there], came_z.at[i, k - 1, 0 : rows[i]], peer("z", k)
                         )
                     )
             else:
                 half = rows[i] // 2
                 there = pl.ds(pl.multiple_of(top[i] + (1 - place[axis]) * half, 16), half)
                 flying.append(
-                    send(
+                    wire.send(
                         held.at[there, pl.ds(left[i], cols[i])],
-                        came.at[i, 3 if axis == "x" else 4, 0:half, 0 : cols[i]],
+                        came_xy.at[i, 0 if axis == "x" else 1, 0:half, 0 : cols[i]],
                         peer(axis),
                     )
                 )
-        gain_axis = AXES[step]
-        if gain_axis == "z":
-            flying += [send(gain_out_ref, gain_in.at[gain_slot + k - 1], peer("z", k)) for k in (1, 2, 3)]
-        else:
-            flying.append(send(gain_out_ref, gain_in.at[gain_slot], peer(gain_axis)))
-        for copy in flying:
-            copy.wait()
-        for i in range(3):
+
+    def sum_done(step):
+        wait_all(flying)
+        flying.clear()
+        for i in range(2):
             axis = ORDERS[i][step]
             if axis == "z":
                 left[i] = pl.multiple_of(left[i] + z * QUARTER, 128)
                 cols[i] = QUARTER
-                spots = (0, 1, 2)
+                terms = [came_z[i, k, 0 : rows[i]] for k in range(3)]
             else:
                 rows[i] = rows[i] // 2
                 top[i] = pl.multiple_of(top[i] + place[axis] * rows[i], 16)
-                spots = (3,) if axis == "x" else (4,)
+                terms = [came_xy[i, 0 if axis == "x" else 1, 0 : rows[i], 0 : cols[i]]]
             spot = (pl.ds(top[i], rows[i]), pl.ds(left[i], cols[i]))
             total = held[spot].astype(F32)
-            for number in spots:
-                total = total + came[i, number, 0 : rows[i], 0 : cols[i]].astype(F32)
+            for term in terms:
+                total = total + term.astype(F32)
             held[spot] = total.astype(BF16)
-        if gain_axis == "z":
-            gain_out_ref[...] = (
-                (gain_out_ref[...] + gain_in[gain_slot])
-                + gain_in[gain_slot + 1]
-                + gain_in[gain_slot + 2]
-            )
-        else:
-            gain_out_ref[...] = gain_out_ref[...] + gain_in[gain_slot]
-            gain_slot += 1
-
-    base = c * 384
-    for i in range(3):
-        spot = (pl.ds(top[i], rows[i]), pl.ds(left[i], cols[i]))
-        out_ref[pl.ds(pl.multiple_of(base + top[i], 16), rows[i]), spot[1]] = held[spot]
-    for step in (2, 1, 0):
-        flying = []
-        for i in range(3):
+
+    def spread_go(step):
+        for i in range(2):
             axis = ORDERS[i][step]
-            mine = out_ref.at[
+            mine = sum_ref.at[
                 pl.ds(pl.multiple_of(base + top[i], 16), rows[i]), pl.ds(left[i], cols[i])
             ]
             for k in (1, 2, 3) if axis == "z" else (1,):
-                flying.append(send(mine, mine, peer(axis, k)))
-        for copy in flying:
-            copy.wait()
-        for i in range(3):
+                flying.append(wire.send(mine, mine, peer(axis, k)))
+
+    def spread_done(step):
+        wait_all(flying)
+        flying.clear()
+        for i in range(2):
             axis = ORDERS[i][step]
             if axis == "z":
                 left[i] = COLOUR * i
@@ -1040,36 +1114,124 @@
             else:
                 top[i] = top[i] - place[axis] * rows[i]
                 rows[i] = rows[i] * 2
-                if rows[i] == 384:
-                    top[i] = 0
-    mine = out_ref.at[pl.ds(pl.multiple_of(base, 16), 384), :]
-    send(mine, mine, peer("c")).wait()
-
-
-COPIES = 3 + 2 * (2 + 3 + 2 + 3 + 2 + 3) // 2 + 5 + 15 + 1
-
-
-def total_over_all(dw_qkv, dw_proj, gains):
+
+    def gains_go(axis, slot):
+        for k in (1, 2, 3) if axis == "z" else (1,):
+            flying.append(wire.send(gains_ref, gain_in.at[slot + k - 1], peer(axis, k)))
+
+    def gains_done(axis, slot):
+        total = gains_ref[...]
+        for k in (0, 1, 2) if axis == "z" else (0,):
+            total = total + gain_in[slot + k]
+        gains_ref[...] = total
+
+    tiles = list(token_tiles())
+    grad_gain = jnp.zeros((1, D), F32)
+    stored = []
+
+    def first_back(part):
+        normal, inverse = norm_parts(tok[part, :].astype(F32))
+        grad_normed = dot(gq[part, :], w_ref[...], CONTRACT_LANES)
+        gain_part = jnp.sum(grad_normed * normal, axis=0, keepdims=True)
+        pulled = norm_pull(grad_normed, gain_ref[...], normal, inverse)
+        gm[part, :] = gm[part, :] + pulled
+        stored.append(mover.go(gm.at[part], ig_hbm.at[part]))
+        return gain_part
+
+    def finish(part):
+        mid[part, :] = mid[part, :] + unsort(pos_ref[part, :], outs[0])
+        stored.append(mover.go(mid.at[part], bo_hbm.at[part]))
+
+    wait_all(loads)
+    grad_gain = grad_gain + first_back(tiles[0])
+    if small:
+        core_done()
+        sum_go(0)
+    grad_gain = grad_gain + first_back(tiles[1])
+    grad_gain = grad_gain + first_back(tiles[2])
+    gains_ref[0:1, :] = grad_gain
+    gains_ref[1:2, :] = dg_two_ref[...]
+    gains_ref[2:GAIN_ROWS, :] = jnp.zeros((GAIN_ROWS - 2, D), F32)
+    if small:
+        gains_go("c", 0)
+        sum_done(0)
+        gains_done("c", 0)
+        gains_go("x", 1)
+        sum_go(1)
+    wait_all(later)
+    at = 0
+    for size in SORT_TILES:
+        part = slice(at, at + size)
+        outs[0, part] = (
+            outs[0, part].astype(F32) + outs[1, part].astype(F32) + outs[2, part].astype(F32)
+        ).astype(BF16)
+        at += size
+    finish(tiles[0])
+    if small:
+        sum_done(1)
+        gains_done("x", 1)
+        gains_go("y", 2)
+        sum_go(2)
+    finish(tiles[1])
+    if small:
+        sum_done(2)
+        gains_done("y", 2)
+        for i in range(2):
+            spot = (pl.ds(top[i], rows[i]), pl.ds(left[i], cols[i]))
+            sum_ref[pl.ds(pl.multiple_of(base + top[i], 16), rows[i]), spot[1]] = held[spot]
+        gains_go("z", 3)
+        spread_go(2)
+    finish(tiles[2])
+    if small:
+        spread_done(2)
+        gains_done("z", 3)
+        spread_go(1)
+        spread_done(1)
+        spread_go(0)
+        spread_done(0)
+        mine = sum_ref.at[pl.ds(base, 384), :]
+        wire.send(mine, mine, peer("c")).wait()
+        wait_all(handed)
+    wait_all(stored)
+
+
+def last(small, group_map, pos_col, gain_one, w_qkv, dg_two, *arrays):
     vmem = pl.BlockSpec(memory_space=pltpu.VMEM)
+    any_space = pl.BlockSpec(memory_space=pl.ANY)
+    dma = pltpu.SemaphoreType.DMA
+    copies = 2 + 7 + 10 + 10 + 6 + 1
+    extra = dict(collective_id=3, has_side_effects=True) if small else {}
     return pl.pallas_call(
-        total_kernel,
+        functools.partial(last_kernel, small),
         out_shape=(
+            jax.ShapeDtypeStruct((TOK_DEV, D), F32),
+            jax.ShapeDtypeStruct((TOK_DEV, D), F32),
             jax.ShapeDtypeStruct((D, WIDE), BF16),
             jax.ShapeDtypeStruct((GAIN_ROWS, D), F32),
+            jax.ShapeDtypeStruct((8, 2, CHUNK, D), BF16),
         ),
-        in_specs=[vmem] * 3,
-        out_specs=(vmem, vmem),
+        in_specs=[pl.BlockSpec(memory_space=pltpu.SMEM)] + [vmem] * 4 + [any_space] * len(arrays),
+        out_specs=(any_space,) * 2 + (vmem,) * 3,
         scratch_shapes=[
+            pltpu.VMEM((TOK_DEV, D), BF16),
+            pltpu.VMEM((ROWS, 3 * D), BF16),
+            pltpu.VMEM((TOK_DEV, D), F32),
+            pltpu.VMEM((TOK_DEV, D), F32),
+            pltpu.VMEM((3, SORTED, D), BF16),
+            pltpu.VMEM((2, EXPERTS, CHUNK, D), BF16),
+            pltpu.VMEM((8, 2, CHUNK, D), BF16),
             pltpu.VMEM((384, WIDE), BF16),
             pltpu.VMEM((384, WIDE), BF16),
-            pltpu.VMEM((3, 5, 384, COLOUR), BF16),
+            pltpu.VMEM((2, 3, 96, QUARTER), BF16),
+            pltpu.VMEM((2, 2, 192, COLOUR), BF16),
             pltpu.VMEM((6, GAIN_ROWS, D), F32),
-            pltpu.SemaphoreType.DMA((COPIES,)),
-            pltpu.SemaphoreType.DMA((COPIES,)),
+            dma((16,)),
+            dma((copies,)),
+            dma((copies,)),
         ],
-        compiler_params=params(collective_id=0, has_side_effects=True),
-        name="total",
-    )(dw_qkv, dw_proj, gains)
+        compiler_params=params(**extra),
+        name="last",
+    )(group_map, pos_col, gain_one, w_qkv, dg_two, *arrays)
 
 
 def body(
@@ -1134,36 +1296,49 @@
     gx_half = add(gx2, swap(gx3, 1))
     gx_far = swap(gx_half, 2)
     out0, out1, gx0, gx1, dwi, dwb = run((0, 1), tie(x, gx_half), (dwi, dwb))
-    gx_near = swap(gx1, 1)
-    out_near = swap(out1, 1)
-    out_far = swap(tie(add(out2, swap(out3, 1)), gx_far), 2)
-    if small:
-        share_in = lax.psum_scatter(dwi, "batch", scatter_dimension=1, tiled=True)
-        share_back = cross_y(dwb, own)
-
-    grad_middle, gctx, dw_proj, dg_two = back_rows(
-        gx0, gx_near, gx_far, pos_col, middle, cotangent, gain_two, context, w_proj
+    grad_middle, grad_qkv, dw_qkv, dw_proj, dg_two, share, out_near, out_far = rear(
+        small,
+        text_lengths,
+        pos_col,
+        gain_one,
+        gain_two,
+        w_proj,
+        lse,
+        gx0,
+        gx1,
+        gx_far,
+        middle,
+        cotangent,
+        context,
+        qkv,
+        tokens,
+        out1,
+        out2,
+        out3,
+        dwi,
+        dwb,
     )
-    if small:
-        gctx = tie(gctx, share_back)
-        share_back = cross_z(share_back)
-    grad_qkv = attend_back(qkv, gctx, lse, text_lengths)
-    input_grad, dw_qkv, dg_one = first_back(tokens, gain_one, grad_qkv, w_qkv, grad_middle)
-    block_out = finish_rows(out0, out_near, out_far, pos_col, middle)
-
-    if small:
-        share_in = tie(share_in, grad_qkv)
-        pieces = lax.all_to_all(
-            deliver(share_in, share_back, group_map),
-            "batch",
-            split_axis=0,
-            concat_axis=0,
-            tiled=True,
-        )
+    input_grad, block_out, summed, gains, pieces = last(
+        small,
+        group_map,
+        pos_col,
+        gain_one,
+        w_qkv,
+        dg_two,
+        tokens,
+        grad_qkv,
+        grad_middle,
+        middle,
+        out0,
+        out_near,
+        out_far,
+        dw_qkv,
+        dw_proj,
+        share,
+    )
+    if small:
         grad_w_in = pieces[:, 0].reshape(1, D, D).astype(F32)
         grad_w_back = pieces[:, 1].reshape(1, D, D).astype(F32)
-        gains = jnp.concatenate([dg_one, dg_two, jnp.zeros((GAIN_ROWS - 2, D), F32)], axis=0)
-        summed, gains = total_over_all(dw_qkv, dw_proj, gains)
         summed_qkv, summed_proj = summed[:, 0 : 3 * D], summed[:, 3 * D : WIDE]
     else:
 
@@ -1175,7 +1350,7 @@
         grad_w_in = settle_any(dwi)
         grad_w_back = settle_any(dwb)
         summed_qkv, summed_proj = lax.psum((dw_qkv, dw_proj), ("batch", "ffn"))
-        gains = lax.psum(jnp.concatenate([dg_one, dg_two], axis=0), ("batch", "ffn"))
+        gains = lax.psum(gains, ("batch", "ffn"))
     return (
         block_out,
         input_grad,

time: 550 us -> 494 us (0.90)
  the two profiles are of different devices: /device:TPU:9 before, /device:TPU:0 now
where the time goes in v4:
time: 494 us; the launch traced here: 485 us
  Pallas kernels  433 us (88%)
  other arithmetic  20.4 us (4%)
  local copies, waits for them, and re-layouts  17.8 us (4%)
  starting transfers between devices  7.6 us (2%)
  waiting for transfers between devices  5.36 us (1%)
    pallas_call x1, Pallas kernels, front(): pl.pallas_call(functools.partial(front_kernel, small), out_shape=(jax.Sha...  117 us
    pallas_call x1, Pallas kernels, last(): pl.pallas_call(functools.partial(last_kernel, small), out_shape=(jax.Shap...  113 us
    pallas_call x1, Pallas kernels, rear(): pl.pallas_call(functools.partial(rear_kernel, small), out_shape=(jax.Shap...  107 us
    pallas_call x2, Pallas kernels, experts(): pl.pallas_call(functools.partial(expert_kernel, carried), grid_spec=pltpu...  94.1 us
  transfers between devices with their start and end apart: 5, of which 3 were waited for; matrix products, arithmetic and copies ran while one was open for 3% of the time, Pallas kernels for 35%

profile of v4, /device:TPU:0, one launch (start us, length us, event | category | flops | bytes accessed | tf_op | source)
XLA Modules:
  0.0 485.2 jit_solution(5672369386067881325)
XLA Ops:
  0.6 1.4 pad.4.routes_ref
  2.0 1.8 route.1
  3.9 2.9 collective-permute-start.1
  6.8 0.8 select_reduce_fusion.1
  7.6 1.2 dynamic_slice.13
  8.8 1.9 fusion.1
  11.4 0.9 dynamic-slice_bitcast_fusion.wb_hbm
  12.3 1.9 dynamic-slice_bitcast_fusion.1.wi_hbm
  14.2 1.3 reshape.63.gain_one_ref.gain_ref
  15.5 0.8 select_reduce_fusion
  16.4 1.3 reshape.64.gain_two_ref
  17.7 0.6 reshape.65.hosts_ref
  18.4 116.9 %front.1 = (bf16[1584,2304]{1,0:T(8,128)(2,1)}, bf16[1584,768]{1,0:T(8,128)(2,1)}, f32[6,16,384]{2,1,0:T(8,128)}, f32[1566,768]{1,0:T(8,128)}, bf16[4,1616,768]{...) custom-call(s32[6]{0:T(128)} %len_ref.3, ...), custom_call_target="tpu_custom_call" | custom-call | tf_op jit(solution)/shard_map/front/pallas_call | solution.py:420
  135.7 0.8 collective-permute-done.2
  136.5 0.6 pad_add_fusion.2.offs_ref
  137.1 41.3 %experts.2 = (bf16[1616,768]{1,0:T(8,128)(2,1)}, bf16[1616,768]{1,0:T(8,128)(2,1)}, bf16[1616,768]{1,0:T(8,128)(2,1)}, bf16[1616,768]{1,0:T(8,128)(2,1)}, bf16[3...) custom-call(s32[8]{0:T(128)} %pad_add_fusion.2.offs_ref, s32[6]{0:T(128)} %reshape.65.hosts_ref, ...), custom_call_target="tpu_custom_call" | custom-call | flops 22875734016 | bytes 19857408 | tf_op jit(solution)/shard_map/experts/pallas_call | solution.py:596
  179.1 4.4 collective-permute-done.3
  183.5 3.9 add_convert_fusion
  187.3 3.7 collective-permute-start.4
  191.0 1.2 copy.25.pos_ref
  192.2 0.6 pad_add_fusion.1.offs_ref
  192.8 52.7 %experts.3 = (bf16[1616,768]{1,0:T(8,128)(2,1)}, bf16[1616,768]{1,0:T(8,128)(2,1)}, bf16[1616,768]{1,0:T(8,128)(2,1)}, bf16[1616,768]{1,0:T(8,128)(2,1)}, bf16[3...) custom-call(s32[8]{0:T(128)} %pad_add_fusion.1.offs_ref, s32[6]{0:T(128)} %reshape.65.hosts_ref, ...), custom_call_target="tpu_custom_call" | custom-call | flops 22875734016 | bytes 19857408 | tf_op jit(solution)/shard_map/experts/pallas_call | solution.py:596
  245.7 106.8 %rear.1 = (f32[1566,768]{1,0:T(8,128)}, bf16[1584,2304]{1,0:T(8,128)(2,1)}, bf16[768,2304]{1,0:T(8,128)(2,1)}, bf16[768,768]{1,0:T(8,128)(2,1)}, f32[1,768]{1,0:...) custom-call(s32[6]{0:T(128)} %len_ref.3, ...), custom_call_target="tpu_custom_call" | custom-call | tf_op jit(solution)/shard_map/rear/pallas_call | solution.py:915
  352.5 112.9 %last.1 = (f32[1566,768]{1,0:T(8,128)}, f32[1566,768]{1,0:T(8,128)}, bf16[768,3072]{1,0:T(8,128)(2,1)}, f32[8,768]{1,0:T(8,128)}, bf16[8,2,96,768]{3,2,1,0:T(8,128)(2,1)}) custom-call(s32[8]{0:T(128)} %group_ref.1, s32[1584,1]{1,0:T(8,128)} %copy.25.pos_ref, f32[1,768]{1,0:T(1,128)} %reshape.63.gain_one_ref.gain_ref, bf16[768,2304]{1,0:T(8,128)(2,1)} %w_ref.3, ...), custom_call_target="tpu_custom_call" | custom-call | tf_op jit(solution)/shard_map/last/pallas_call | solution.py:1204
  465.4 5.6 %slice_convert_fusion = f32[768,2304]{1,0:T(8,128)} fusion(bf16[768,3072]{1,0:T(8,128)(2,1)} %get-tuple-element.78), kind=kLoop, calls=%fused_computation.1 | loop fusion | flops 1769472 | bytes 10616832 | tf_op jit(solution)/shard_map/convert_element_type | solution.py:1358
  471.0 3.0 slice_convert_fusion.1
  474.2 1.6 convert.2
  475.8 1.6 convert.3
  477.3 1.4 slice_reduce_fusion
  478.8 2.5 copy.28
  481.2 1.4 slice-done
  482.8 2.2 copy.29
  (33 shorter events, 1.6 us)
Async XLA Ops:
  0.6 10.8 %copy-start = (bf16[1,768,768]{2,1,0:T(8,128)(2,1)S(1)}, bf16[1,768,768]{2,1,0:T(8,128)(2,1)}, u32[]{:S(2)}) copy-start(bf16[1,768,768]{2,1,0:T(8,128)(2,1)} %param.20) | copy-start | bytes 3538948
  3.9 131.4 %collective-permute-start.1 = (s32[1,128]{1,0:T(1,128)}, s32[1,128]{1,0:T(1,128)S(1)}, u32[]{:S(2)}, u32[]{:S(2)}) collective-permute-start(s32[1,128]{1,0:T(1,128)} %get-tuple-element.46), channel_id=1, source_target_pairs={{0,2},{1,3},{2,0},{3,1},{4,6},{5,7},{6,4},{7,5},{8,10},{9,11},{10,... | collective-permute-start | bytes 1544 | tf_op jit(solution)/shard_map/ppermute | solution.py:622
  135.3 1.3 collective-permute-start.2
  137.1 41.7 %copy-start.4 = (s32[1,128]{1,0:T(1,128)S(1)}, s32[1,128]{1,0:T(1,128)}, u32[]{:S(2)}) copy-start(s32[1,128]{1,0:T(1,128)} %get-tuple-element.46) | copy-start | bytes 1540
  137.1 41.9 %copy-start.3 = (s32[1,1664]{1,0:T(1,128)S(1)}, s32[1,1664]{1,0:T(1,128)}, u32[]{:S(2)}) copy-start(s32[1,1664]{1,0:T(1,128)} %get-tuple-element.44.pos_ref) | copy-start | bytes 19972
  178.5 5.0 %collective-permute-start.3 = (bf16[1616,768]{1,0:T(8,128)(2,1)}, bf16[1616,768]{1,0:T(8,128)(2,1)S(1)}, u32[]{:S(2)}, u32[]{:S(2)}) collective-permute-start(bf16[1616,768]{1,0:T(8,128)(2,1)} %get-tuple-element.52), channel_id=1, source_target_pairs={{0,1},{1,0},{2,3},{3,2},{4,5},{5,4},{6,7},{7,6},{8,9},{9,8},{10,11... | collective-permute-start | bytes 7446536 | tf_op jit(solution)/shard_map/ppermute | solution.py:622
  178.8 13.3 %collective-permute-start = (s32[1,128]{1,0:T(1,128)S(1)}, s32[1,128]{1,0:T(1,128)S(1)}, u32[]{:S(2)}, u32[]{:S(2)}) collective-permute-start(s32[1,128]{1,0:T(1,128)S(1)} %copy-done.4), channel_id=1, source_target_pairs={{0,1},{1,0},{2,3},{3,2},{4,5},{5,4},{6,7},{7,6},{8,9},{9,8},{10,11... | collective-permute-start | bytes 1544 | tf_op jit(solution)/shard_map/ppermute | solution.py:622
  187.3 58.3 %collective-permute-start.4 = (bf16[1616,768]{1,0:T(8,128)(2,1)}, bf16[1616,768]{1,0:T(8,128)(2,1)}, u32[]{:S(2)}, u32[]{:S(2)}) collective-permute-start(bf16[1616,768]{1,0:T(8,128)(2,1)} %add_convert_fusion), channel_id=1, source_target_pairs={{0,2},{1,3},{2,0},{3,1},{4,6},{5,7},{6,4},{7,5},{8,10},{9,11},{10,... | collective-permute-start | bytes 7446536 | tf_op jit(solution)/shard_map/ppermute | solution.py:622
  465.4 8.6 %copy-start.2 = (bf16[8,2,96,768]{3,2,1,0:T(8,128)(2,1)S(1)}, bf16[8,2,96,768]{3,2,1,0:T(8,128)(2,1)}, u32[]{:S(2)}) copy-start(bf16[8,2,96,768]{3,2,1,0:T(8,128)(2,1)} %get-tuple-element.79) | copy-start | bytes 7077892
  471.0 7.7 %slice-start.2 = ((s8[4816896]{0:T(1024)(128)(4,1)}), s8[4194304]{0:T(1024)(128)(4,1)S(1)}, s32[]{:S(2)}) async-start(s8[4816896]{0:T(1024)(128)(4,1)} %bitcast.24), calls=%async_computation.2 | async-start | bytes 8388608
  474.0 4.7 slice-start.3
  478.8 3.9 slice-start
  478.8 4.1 slice-start.1
  478.8 6.3 %copy-start.1 = (bf16[1,768,768]{2,1,0:T(8,128)(2,1)S(1)}, bf16[1,768,768]{2,1,0:T(8,128)(2,1)}, u32[]{:S(2)}) copy-start(bf16[1,768,768]{2,1,0:T(8,128)(2,1)} %param.20) | copy-start | bytes 3538948
